TPU v7x, 256 devices: a whole 4x4x8 slice. The times are simulated.
256 devices in a mesh: frame: 16 (over z_hi, y), space: 16 (over z_lo, x, core).
Axes of the slice: x: 4, y: 4, z: 8 (z_hi: 4, z_lo: 2; z = z_hi * 2 + z_lo), core: 2. Of those that a mesh axis runs over, the one named last changes fastest.
Arguments:
- hidden_in: bfloat16 [2, 16, 32, 64, 1152], P(None, 'frame', 'space'), may hold values from -6 to 6
- attn_cotangent: bfloat16 [2, 16, 32, 64, 1152], P(None, 'frame', 'space'), may hold values from -6 to 6
- w_qkv: bfloat16 [1152, 3456], P('space'), may hold values from -0.1875 to 0.1875
- modulation_table: bfloat16 [1000, 2, 1152], replicated, may hold values from -3 to 3
- snr_table: float32 [1000], replicated, may hold values from 0.1 to 1
- timestep: int32 [2], replicated, may hold values from 0 to 999
- weight_index: int32 [2], replicated, may hold values from 0 to 999
Outputs:
- grad_input: bfloat16 [2, 16, 32, 64, 1152], P(None, 'frame', 'space')
- grad_w_qkv: float32 [1152, 3456], P('space')
- grad_modulation: float32 [2, 2, 1152], replicated
All inputs are finite; a program needn't handle non-finite values.
Results may differ from a plain program's by a relative error of at most 0.029.
Values may be sent and summed in bfloat16 or wider, within the bound.
A program may use at most 128 MiB of HBM per device.

v0:
```python
import jax
import jax.numpy as jnp
from jax import lax
from jax.sharding import PartitionSpec as P

HEADS = 16
HEAD_DIM = 72


def attend_back(queries, keys, values, upstream):
    factor = queries.shape[-1] ** (-0.5)
    queries = queries.astype(jnp.float32)
    keys = keys.astype(jnp.float32)
    values = values.astype(jnp.float32)
    upstream = upstream.astype(jnp.float32)
    highest = lax.Precision.HIGHEST
    scores = jnp.einsum("bfxhe,bgxhe->bxhfg", queries, keys, precision=highest) * factor
    expd = jnp.exp(scores)
    probs = expd / jnp.sum(expd, axis=-1, keepdims=True)
    grad_probs = jnp.einsum("bfxhe,bgxhe->bxhfg", upstream, values, precision=highest)
    grad_values = jnp.einsum("bxhfg,bfxhe->bgxhe", probs, upstream, precision=highest)
    grad_scores = probs * (grad_probs - jnp.sum(probs * grad_probs, axis=-1, keepdims=True))
    grad_queries = jnp.einsum("bxhfg,bgxhe->bfxhe", grad_scores, keys, precision=highest) * factor
    grad_keys = jnp.einsum("bxhfg,bfxhe->bgxhe", grad_scores, queries, precision=highest) * factor
    return (
        grad_queries.astype(jnp.bfloat16),
        grad_keys.astype(jnp.bfloat16),
        grad_values.astype(jnp.bfloat16),
    )


def per_device(
    hidden_in, attn_cotangent, w_qkv, modulation_table, snr_table, timestep, weight_index
):
    clip_count, frame_dev, row_dev, col_count, model_width = hidden_in.shape
    positions = row_dev * col_count
    values_in = hidden_in.astype(jnp.float32)
    average = jnp.mean(values_in, axis=-1, keepdims=True)
    centered = values_in - average
    variance = jnp.mean(centered * centered, axis=-1, keepdims=True)
    inverse_std = lax.rsqrt(variance + 1e-06)
    normed = centered * inverse_std
    modulation = modulation_table[timestep].astype(jnp.float32)
    shift = modulation[:, 0][:, None, None, None, :]
    scale = modulation[:, 1][:, None, None, None, :]
    modulated = (normed * (1.0 + scale) + shift).astype(jnp.bfloat16)
    mod_rows = modulated.reshape(-1, model_width)
    w_full = lax.all_gather(w_qkv, "space", axis=0, tiled=True)
    projected = jnp.dot(mod_rows, w_full, preferred_element_type=jnp.float32).astype(jnp.bfloat16)
    projected = projected.reshape(clip_count, frame_dev, positions, 3, model_width)
    loss_weight = snr_table[weight_index]
    upstream = (loss_weight[:, None, None, None, None] * attn_cotangent.astype(jnp.float32)).astype(
        jnp.bfloat16
    )
    upstream = upstream.reshape(clip_count, frame_dev, positions, 1, model_width)
    packed = jnp.concatenate([projected, upstream], axis=3)
    received = lax.all_to_all(packed, "frame", split_axis=2, concat_axis=1, tiled=True)
    item_count = received.shape[0]
    frames = received.shape[1]
    across = received.shape[2]
    pieces = received.reshape(item_count, frames, across, 4, HEADS, HEAD_DIM)
    head_grads = attend_back(
        pieces[:, :, :, 0], pieces[:, :, :, 1], pieces[:, :, :, 2], pieces[:, :, :, 3]
    )
    stacked = jnp.stack(head_grads, axis=3).reshape(item_count, frames, across, 3, model_width)
    grad_projected = lax.all_to_all(stacked, "frame", split_axis=1, concat_axis=2, tiled=True)
    grad_rows = grad_projected.reshape(-1, 3 * model_width)
    device_count = lax.axis_size("frame") * lax.axis_size("space")
    grad_scale_factor = float(mod_rows.shape[0] * device_count) ** (-0.5)
    row_share = lax.psum_scatter(
        lax.dot_general(
            mod_rows, grad_rows, (((0,), (0,)), ((), ())), preferred_element_type=jnp.float32
        ).astype(jnp.bfloat16),
        "space",
        scatter_dimension=0,
        tiled=True,
    )
    grad_weight = lax.psum(row_share, "frame").astype(jnp.float32) * grad_scale_factor
    grad_hidden = lax.dot_general(
        grad_rows, w_full, (((1,), (1,)), ((), ())), preferred_element_type=jnp.float32
    )
    grad_hidden = grad_hidden.reshape(values_in.shape)
    local_sums = jnp.stack(
        [jnp.sum(grad_hidden, axis=(1, 2, 3)), jnp.sum(grad_hidden * normed, axis=(1, 2, 3))],
        axis=1,
    )
    grad_modulation = lax.psum(local_sums, ("frame", "space")) * grad_scale_factor
    grad_normed = grad_hidden * (1.0 + scale)
    grad_input = (
        grad_normed
        - jnp.mean(grad_normed, axis=-1, keepdims=True)
        - normed * jnp.mean(grad_normed * normed, axis=-1, keepdims=True)
    ) * inverse_std
    return (grad_input.astype(jnp.bfloat16), grad_weight, grad_modulation)


def solution(mesh):
    in_specs = (
        P(None, "frame", "space", None, None),
        P(None, "frame", "space", None, None),
        P("space", None),
        P(),
        P(),
        P(),
        P(),
    )
    out_specs = (P(None, "frame", "space", None, None), P("space", None), P())
    return jax.shard_map(
        per_device, mesh=mesh, in_specs=in_specs, out_specs=out_specs, check_vma=False
    )
```

profile of v0, /device:TPU:6, one launch (start us, length us, event | category | flops | bytes accessed | tf_op | source)
XLA Modules:
  0.0 491.3 jit_solution(7075564899825200032)
XLA Ops:
  8.6 2.9 gather_fusion
  15.6 49.9 %all-gather.2.cloned.1.call-done = bf16[1152,3456]{1,0:T(8,128)(2,1)} async-done(((bf16[72,3456]{1,0:T(8,128)(2,1)}), bf16[1152,3456]{1,0:T(8,128)(2,1)}) %all-gather.2.cloned.1.call-update) | async-done | bytes 7962640 | tf_op jit(solution)/shard_map/all_gather | solution.py:48
  65.5 7.1 %convolution_convert_fusion.1 = bf16[256,3456]{1,0:T(8,128)(2,1)} fusion(bf16[256,1152]{1,0:T(8,128)(2,1)S(1)} %bitcast.76, bf16[1152,3456]{1,0:T(8,128)(2,1)} %all-gather.2.cloned.1.call-done), kind=kOutput, calls=%fused_computation.3 | convolution fusion | flops 2039316480 | bytes 10321920 | tf_op jit(solution)/shard_map/dot_general | solution.py:49
  72.6 2.6 copy.63
  75.2 2.0 reshape.124
  77.2 4.6 pad_maximum_fusion
  81.8 4.9 copy.66
  86.7 61.9 %all_to_all.8 = bf16[2,1,128,4,1152]{4,3,1,0,2:T(4,128)(2,1)S(1)} all-to-all(bf16[2,1,128,4,1152]{4,3,1,0,2:T(4,128)(2,1)} %copy.66), channel_id=1, replica_groups=mesh['frame'=16,'space'=16] {'frame'}, dimensions={2} | all-to-all | bytes 4718592 | tf_op jit(solution)/shard_map/all_to_all | solution.py:57
  148.6 8.8 %reshape.148 = bf16[2,16,8,4,16,72]{5,4,3,0,2,1:T(8,128)(2,1)} reshape(bf16[2,1,128,4,1152]{4,3,1,0,2:T(4,128)(2,1)S(1)} %all_to_all.8) | data formatting | bytes 4718592 | tf_op jit(solution)/shard_map/reshape | solution.py:61
  157.4 3.6 fusion.25
  161.0 1.7 fusion.1
  162.7 1.8 multiply_reduce_fusion
  164.4 2.4 fusion.9
  166.9 2.2 fusion.10
  169.1 3.0 fusion.8
  172.4 1.5 stack.21
  175.6 1.5 copy.75
  178.8 40.4 %all_to_all.9 = bf16[2,16,8,3,1152]{4,2,0,3,1:T(8,128)(2,1)S(1)} all-to-all(bf16[2,16,8,3,1152]{4,2,0,3,1:T(8,128)(2,1)S(1)} %copy.76), channel_id=1, replica_groups=mesh['frame'=16,'space'=16] {'frame'}, dimensions={1} | all-to-all | bytes 3538944 | tf_op jit(solution)/shard_map/all_to_all | solution.py:66
  221.1 5.5 %convolution_convert_fusion = bf16[1152,3456]{1,0:T(8,128)(2,1)} fusion(bf16[256,1152]{1,0:T(8,128)(2,1)S(1)} %bitcast.77, bf16[256,3456]{1,0:T(8,128)(2,1)S(1)} %bitcast.73), kind=kOutput, calls=%fused_computation.2 | convolution fusion | flops 2042413056 | bytes 10321920 | tf_op jit(solution)/shard_map/dot_general | solution.py:71
  226.7 6.5 %fusion.19 = (f32[256]{0:T(256)}, f32[256,1152]{1,0:T(8,128)S(1)}) fusion(f32[2,1152]{1,0:T(2,128)S(1)} %bitcast.80, bf16[256,3456]{1,0:T(8,128)(2,1)S(1)} %bitcast.74, bf16[1152,3456]{1,0:T(8,128)(2,1)} %all-gather.2.cloned.1.call-done), kind=kOutput, calls=%fused_computation.34 | convolution fusion | flops 2039021312 | bytes 10921984 | tf_op jit(solution)/shard_map/dot_general | solution.py:79
  234.6 83.7 %psum.15 = f32[2,2,1152]{2,0,1:T(2,128)S(1)} all-reduce(f32[2,2,1152]{2,0,1:T(2,128)S(1)} %pad_maximum_fusion.2), channel_id=1, replica_groups=mesh['frame'=16,'space'=16] {'frame','space'}, use_global_device_ids=true, to_apply=%region_10.0 | all-reduce | flops 4608 | bytes 36864 | tf_op jit(solution)/shard_map/psum | solution.py:87
  319.0 1.9 fusion.16
  320.9 161.8 %all-reduce.3.cloned.1.call-done = bf16[72,3456]{1,0:T(8,128)(2,1)} async-done(((bf16[72,3456]{1,0:T(8,128)(2,1)}), bf16[72,3456]{1,0:T(8,128)(2,1)}) %all-reduce.3.cloned.1.call-update) | async-done | bytes 497680 | tf_op jit(solution)/shard_map/psum | solution.py:78
  482.7 2.0 convert_multiply_fusion
  (58 shorter events, 13.1 us)
Async XLA Ops:
  7.2 5.1 %copy-start = (f32[1000]{0:T(1024)S(1)}, f32[1000]{0:T(1024)}, u32[]{:S(2)}) copy-start(f32[1000]{0:T(1024)} %param.11) | copy-start | bytes 12004
  7.2 7.6 %copy-start.2 = (bf16[2,1,2,64,1152]{4,3,2,1,0:T(8,128)(2,1)S(1)}, bf16[2,1,2,64,1152]{4,3,2,1,0:T(8,128)(2,1)}, u32[]{:S(2)}) copy-start(bf16[2,1,2,64,1152]{4,3,2,1,0:T(8,128)(2,1)} %param.7) | copy-start | bytes 1769476
  7.2 58.3 %all-gather.2.cloned.1.call-start = ((), (), s32[]{:S(2)}) async-start(), calls=%async_computation.3 | async-start | bytes 8460288 | tf_op jit(solution)/shard_map/all_gather | solution.py:48
  7.9 311.1 %reduce-scatter.5.cloned.1.call-start = ((), (), s32[]{:S(2)}) async-start(), calls=%async_computation.5 | async-start | bytes 8460288
  15.0 218.4 %copy-start.5 = (f32[2,2,64]{2,1,0:T(2,128)}, f32[2,2,64]{2,1,0:T(2,128)S(1)}, u32[]{:S(2)}) copy-start(f32[2,2,64]{2,1,0:T(2,128)S(1)} %broadcast_multiply_fusion.2) | copy-start | bytes 3076
  15.3 50.2 %copy-start.6 = (f32[2,2,64]{2,1,0:T(2,128)}, f32[2,2,64]{2,1,0:T(2,128)S(1)}, u32[]{:S(2)}) copy-start(f32[2,2,64]{2,1,0:T(2,128)S(1)} %add_rsqrt_fusion) | copy-start | bytes 3076
  15.6 49.9 %copy-start.3 = (bf16[2,1,2,64,1152]{4,3,2,1,0:T(8,128)(2,1)}, bf16[2,1,2,64,1152]{4,3,2,1,0:T(8,128)(2,1)S(1)}, u32[]{:S(2)}) copy-start(bf16[2,1,2,64,1152]{4,3,2,1,0:T(8,128)(2,1)S(1)} %fusion.12) | copy-start | bytes 1769476
  220.1 1.1 copy-start.4
  226.7 256.0 %all-reduce.3.cloned.1.call-start = ((), (), s32[]{:S(2)}) async-start(), calls=%async_computation.4 | async-start | bytes 995328 | tf_op jit(solution)/shard_map/psum | solution.py:78
  233.2 85.7 %copy-start.8 = (f32[256]{0:T(256)S(1)}, f32[256]{0:T(256)}, u32[]{:S(2)}) copy-start(f32[256]{0:T(256)} %get-tuple-element.25) | copy-start | bytes 3076
  233.3 85.7 %copy-start.7 = (f32[2,2,64]{2,1,0:T(2,128)S(1)}, f32[2,2,64]{2,1,0:T(2,128)}, u32[]{:S(2)}) copy-start(f32[2,2,64]{2,1,0:T(2,128)} %copy-done.6) | copy-start | bytes 3076
  319.0 165.7 %copy-start.1 = (f32[1000]{0:T(1024)S(1)}, f32[1000]{0:T(1024)}, u32[]{:S(2)}) copy-start(f32[1000]{0:T(1024)} %param.11) | copy-start | bytes 12004
Sparse Core Ops, SparseCore 0:
  9.9 55.5 all-gather.1
  226.8 80.7 reduce-scatter.4
  319.2 163.5 all-reduce.2
where the time goes:
time: 492 us; the launch traced here: 491 us
  waiting for transfers between devices  212 us (43%)
  blocking collectives  186 us (38%)
  local copies, waits for them, and re-layouts  35.1 us (7%)
  matrix products  30.3 us (6%)
  between operations  14 us (3%)
  other arithmetic  13.4 us (3%)
    psum x1, waiting for transfers between devices, per_device(): lax.psum(row_share, 'frame').astype(jnp.float32) * grad_scale_factor  162 us
    psum x1, blocking collectives, per_device(): lax.psum(local_sums, ('frame', 'space')) * grad_scale_factor  83.7 us
    all_to_all x1, blocking collectives, per_device(): lax.all_to_all(packed, 'frame', split_axis=2, concat_axis=1, tiled=True)  61.9 us
    all_gather x1, waiting for transfers between devices, per_device(): w_full = lax.all_gather(w_qkv, 'space', axis=0, tiled=True)  49.9 us
    all_to_all x1, blocking collectives, per_device(): lax.all_to_all(stacked, 'frame', split_axis=1, concat_axis=2, tiled=True)  40.4 us
  transfers between devices with their start and end apart: 3, of which 2 were waited for; matrix products, arithmetic and copies ran while one was open for 4% of the time, Pallas kernels for 0%

commit v1 on v0

v1 whole, which is shorter than its diff:
```python
import jax
import jax.numpy as jnp
from jax import lax
from jax.sharding import PartitionSpec as P

HEADS = 16
HEAD_DIM = 72


def attend_back(queries, keys, values, upstream):
    factor = queries.shape[-1] ** (-0.5)
    queries = queries.astype(jnp.float32)
    keys = keys.astype(jnp.float32)
    values = values.astype(jnp.float32)
    upstream = upstream.astype(jnp.float32)
    highest = lax.Precision.HIGHEST
    scores = jnp.einsum("bfxhe,bgxhe->bxhfg", queries, keys, precision=highest) * factor
    expd = jnp.exp(scores)
    probs = expd / jnp.sum(expd, axis=-1, keepdims=True)
    grad_probs = jnp.einsum("bfxhe,bgxhe->bxhfg", upstream, values, precision=highest)
    grad_values = jnp.einsum("bxhfg,bfxhe->bgxhe", probs, upstream, precision=highest)
    grad_scores = probs * (grad_probs - jnp.sum(probs * grad_probs, axis=-1, keepdims=True))
    grad_queries = jnp.einsum("bxhfg,bgxhe->bfxhe", grad_scores, keys, precision=highest) * factor
    grad_keys = jnp.einsum("bxhfg,bfxhe->bgxhe", grad_scores, queries, precision=highest) * factor
    return (
        grad_queries.astype(jnp.bfloat16),
        grad_keys.astype(jnp.bfloat16),
        grad_values.astype(jnp.bfloat16),
    )


def per_device(
    hidden_in, attn_cotangent, w_qkv, modulation_table, snr_table, timestep, weight_index
):
    clip_count, frame_dev, row_dev, col_count, model_width = hidden_in.shape
    frame_n = lax.axis_size("frame")
    space_n = lax.axis_size("space")
    positions = row_dev * col_count
    w_full = lax.all_gather(w_qkv, "space", axis=0, tiled=True)
    both = jnp.stack(
        [
            hidden_in.reshape(clip_count, frame_dev, positions, model_width),
            attn_cotangent.reshape(clip_count, frame_dev, positions, model_width),
        ],
        axis=3,
    )
    both = lax.all_to_all(both, "frame", split_axis=2, concat_axis=1, tiled=True)
    frames = both.shape[1]
    across = both.shape[2]
    values_in = both[:, :, :, 0].astype(jnp.float32)
    average = jnp.mean(values_in, axis=-1, keepdims=True)
    centered = values_in - average
    variance = jnp.mean(centered * centered, axis=-1, keepdims=True)
    inverse_std = lax.rsqrt(variance + 1e-06)
    normed = centered * inverse_std
    modulation = modulation_table[timestep].astype(jnp.float32)
    shift = modulation[:, 0][:, None, None, :]
    scale = modulation[:, 1][:, None, None, :]
    modulated = (normed * (1.0 + scale) + shift).astype(jnp.bfloat16)
    mod_rows = modulated.reshape(-1, model_width)
    projected = jnp.dot(mod_rows, w_full, preferred_element_type=jnp.float32).astype(jnp.bfloat16)
    pieces = projected.reshape(clip_count, frames, across, 3, HEADS, HEAD_DIM)
    loss_weight = snr_table[weight_index]
    upstream = (
        loss_weight[:, None, None, None] * both[:, :, :, 1].astype(jnp.float32)
    ).astype(jnp.bfloat16)
    upstream = upstream.reshape(clip_count, frames, across, HEADS, HEAD_DIM)
    head_grads = attend_back(pieces[:, :, :, 0], pieces[:, :, :, 1], pieces[:, :, :, 2], upstream)
    grad_rows = jnp.stack(head_grads, axis=3).reshape(-1, 3 * model_width)
    grad_scale_factor = float(mod_rows.shape[0] * frame_n * space_n) ** (-0.5)
    term = lax.dot_general(
        mod_rows, grad_rows, (((0,), (0,)), ((), ())), preferred_element_type=jnp.float32
    ).astype(jnp.bfloat16)
    col_blk = 3 * model_width // frame_n
    share = lax.psum_scatter(term, "space", scatter_dimension=0, tiled=True)
    share = share.reshape(share.shape[0], frame_n, col_blk)
    share = lax.psum_scatter(share, "frame", scatter_dimension=1, tiled=True)
    grad_weight = lax.all_gather(share, "frame", axis=1, tiled=True)
    grad_weight = grad_weight.reshape(share.shape[0], 3 * model_width)
    grad_weight = grad_weight.astype(jnp.float32) * grad_scale_factor
    grad_hidden = lax.dot_general(
        grad_rows, w_full, (((1,), (1,)), ((), ())), preferred_element_type=jnp.float32
    )
    grad_hidden = grad_hidden.reshape(values_in.shape)
    local_sums = jnp.stack(
        [jnp.sum(grad_hidden, axis=(1, 2)), jnp.sum(grad_hidden * normed, axis=(1, 2))],
        axis=1,
    )
    grad_modulation = lax.psum(local_sums, ("frame", "space")) * grad_scale_factor
    grad_normed = grad_hidden * (1.0 + scale)
    grad_input = (
        grad_normed
        - jnp.mean(grad_normed, axis=-1, keepdims=True)
        - normed * jnp.mean(grad_normed * normed, axis=-1, keepdims=True)
    ) * inverse_std
    grad_input = grad_input.astype(jnp.bfloat16)
    grad_input = lax.all_to_all(grad_input, "frame", split_axis=1, concat_axis=2, tiled=True)
    grad_input = grad_input.reshape(clip_count, frame_dev, row_dev, col_count, model_width)
    return (grad_input, grad_weight, grad_modulation)


def solution(mesh):
    in_specs = (
        P(None, "frame", "space", None, None),
        P(None, "frame", "space", None, None),
        P("space", None),
        P(),
        P(),
        P(),
        P(),
    )
    out_specs = (P(None, "frame", "space", None, None), P("space", None), P())
    return jax.shard_map(
        per_device, mesh=mesh, in_specs=in_specs, out_specs=out_specs, check_vma=False
    )
```

time: 492 us -> 376 us (0.76)
  waiting for transfers between devices: 212 us -> 141 us
  blocking collectives: 186 us -> 127 us
  starting transfers between devices: 0.12 us -> 20 us
  other arithmetic: 13.4 us -> 4.83 us
    psum x1 -> x0, waiting for transfers between devices: 162 us -> none  [per_device(): lax.psum(row_share, 'frame').astype(jnp.float32) * grad_scale_factor]
    all_to_all x2 -> x0, blocking collectives: 102 us -> none  [the longest x1 61.9 us: per_device(): lax.all_to_all(packed, 'frame', split_axis=2, concat_axis=1, tiled=True)]
    unnamed x4, waiting for transfers between devices: 0.72 us -> 75.7 us
    all_gather x0 -> x1, blocking collectives: none -> 46.2 us  [per_device(): grad_weight = lax.all_gather(share, 'frame', axis=1, tiled=True)]
    all_to_all x0 -> x2, waiting for transfers between devices: none -> 41.8 us  [the longest x1 41.8 us: per_device(): lax.all_to_all(both, 'frame', split_axis=2, concat_axis=1, tiled=True)]
    all_gather x1, waiting for transfers between devices: 49.9 us -> 15.8 us  [per_device(): w_full = lax.all_gather(w_qkv, 'space', axis=0, tiled=True)]
    all_to_all x0 -> x2, starting transfers between devices: none -> 19.9 us  [the longest x1 11.2 us: per_device(): lax.all_to_all(both, 'frame', split_axis=2, concat_axis=1, tiled=True)]
    reduce_scatter x0 -> x1, waiting for transfers between devices: none -> 8.11 us  [per_device(): share = lax.psum_scatter(share, 'frame', scatter_dimension=1, tiled=True)]
  transfers between devices with their start and end apart: 3 -> 5, of which waited for: 2 -> 4; matrix products, arithmetic and copies ran while one was open for 4% -> 5% of each run, Pallas kernels for 0% -> 0%
where the time goes in v1:
time: 376 us
  waiting for transfers between devices  141 us (38%)
  blocking collectives  127 us (34%)
  local copies, waits for them, and re-layouts  37.7 us (10%)
  matrix products  30.6 us (8%)
  starting transfers between devices  20 us (5%)
  between operations  14.1 us (4%)
  other arithmetic  4.83 us (1%)
    psum x1, blocking collectives, per_device(): lax.psum(local_sums, ('frame', 'space')) * grad_scale_factor  80.8 us
    unnamed x4, waiting for transfers between devices  75.7 us
    all_gather x1, blocking collectives, per_device(): grad_weight = lax.all_gather(share, 'frame', axis=1, tiled=True)  46.2 us
    all_to_all x1, waiting for transfers between devices, per_device(): lax.all_to_all(both, 'frame', split_axis=2, concat_axis=1, tiled=True)  41.8 us
    all_gather x1, waiting for transfers between devices, per_device(): w_full = lax.all_gather(w_qkv, 'space', axis=0, tiled=True)  15.8 us
    all_to_all x1, starting transfers between devices, per_device(): lax.all_to_all(both, 'frame', split_axis=2, concat_axis=1, tiled=True)  11.2 us
    all_to_all x1, starting transfers between devices, per_device(): lax.all_to_all(grad_input, 'frame', split_axis=1, concat_axis=2, tiled=True)  8.66 us
    reduce_scatter x1, waiting for transfers between devices, per_device(): share = lax.psum_scatter(share, 'frame', scatter_dimension=1, tiled=True)  8.11 us
  transfers between devices with their start and end apart: 5, of which 4 were waited for; matrix products, arithmetic and copies ran while one was open for 5% of the time, Pallas kernels for 0%

profile of v1, /device:TPU:6, one launch (start us, length us, event | category | flops | bytes accessed | tf_op | source)
XLA Modules:
  0.0 375.6 jit_solution(3701805909269728193)
XLA Ops:
  9.6 1.7 copy.39
  11.3 2.7 pad_maximum_fusion.1
  13.9 11.2 %all-to-all-start = ((bf16[2,1,128,2,1152]{4,0,3,1,2:T(2,128)(2,1)}), bf16[2,1,128,2,1152]{4,0,3,1,2:T(2,128)(2,1)S(1)}, u32[]{:S(2)}, u32[]{:S(2)}) async-start(bf16[2,1,128,2,1152]{4,0,3,1,2:T(2,128)(2,1)} %pad_maximum_fusion.1), calls=%async_computation | async-start | bytes 2359296 | tf_op jit(solution)/shard_map/all_to_all | solution.py:47
  25.2 2.9 gather_fusion
  28.9 41.8 %all-to-all-done = bf16[2,1,128,2,1152]{4,0,3,1,2:T(2,128)(2,1)S(1)} async-done(((bf16[2,1,128,2,1152]{4,0,3,1,2:T(2,128)(2,1)}), bf16[2,1,128,2,1152]{4,0,3,1,2:T(2,128)(2,1)S(1)}, u32[]{:S(2)}, u32[]{:S(2)}) %all-to-all-start) | async-done | bytes 1179680 | tf_op jit(solution)/shard_map/all_to_all | solution.py:47
  71.5 3.1 reshape.157
  75.0 15.8 %all-gather.2.cloned.1.call-done = bf16[1152,3456]{1,0:T(8,128)(2,1)} async-done(((bf16[72,3456]{1,0:T(8,128)(2,1)}), bf16[1152,3456]{1,0:T(8,128)(2,1)}) %all-gather.2.cloned.1.call-update) | async-done | bytes 7962640 | tf_op jit(solution)/shard_map/all_gather | solution.py:39
  90.8 7.0 %convolution_convert_fusion.1 = bf16[256,3456]{1,0:T(8,128)(2,1)} fusion(bf16[256,1152]{1,0:T(8,128)(2,1)S(1)} %fusion.8, bf16[1152,3456]{1,0:T(8,128)(2,1)} %all-gather.2.cloned.1.call-done), kind=kOutput, calls=%fused_computation.5 | convolution fusion | flops 2039316480 | bytes 10321920 | tf_op jit(solution)/shard_map/dot_general | solution.py:61
  97.8 7.1 %reshape.152 = bf16[2,16,8,3,16,72]{5,4,3,2,1,0:T(8,128)(2,1)S(1)} reshape(bf16[256,3456]{1,0:T(8,128)(2,1)} %convolution_convert_fusion.1) | data formatting | bytes 3538944 | tf_op jit(solution)/shard_map/reshape | solution.py:62
  105.9 1.7 fusion.4
  107.6 2.3 multiply_reduce_fusion
  109.9 2.4 fusion.6
  112.3 2.2 fusion.7
  114.5 2.8 fusion.5
  118.9 4.6 %dot_general.32 = bf16[2,16,8,3456]{3,2,1,0:T(8,128)(2,1)} reshape(bf16[2,16,8,3,16,72]{5,4,3,2,1,0:T(8,128)(2,1)S(1)} %copy.46) | data formatting | bytes 3538944 | tf_op jit(solution)/shard_map/dot_general | solution.py:81
  123.5 4.6 %reshape.154 = bf16[256,3456]{1,0:T(8,128)(2,1)} reshape(bf16[2,16,8,3,16,72]{5,4,3,2,1,0:T(8,128)(2,1)S(1)} %copy.46) | data formatting | bytes 3538944 | tf_op jit(solution)/shard_map/reshape | solution.py:69
  128.1 6.7 %multiply_reduce_fusion.1 = (f32[2,1152]{1,0:T(2,128)S(1)}, f32[2,16,8]{2,1,0:T(8,128)S(1)}, f32[2,16,8]{2,1,0:T(8,128)S(1)}, f32[2,1152]{1,0:T(2,128)S(1)}, bf1...) fusion(f32[2,16,8]{2,1,0:T(8,128)S(1)} %add_rsqrt_fusion, ...), kind=kOutput, calls=%fused_computation.28 | convolution fusion | flops 2042260480 | bytes 12132352 | tf_op jit(solution)/shard_map/dot_general | solution.py:81
  134.8 5.4 %convolution_convert_fusion = bf16[1152,3456]{1,0:T(8,128)(2,1)} fusion(bf16[256,1152]{1,0:T(8,128)(2,1)S(1)} %bitcast.101, bf16[256,3456]{1,0:T(8,128)(2,1)S(1)} %copy-done.3), kind=kOutput, calls=%fused_computation.2 | convolution fusion | flops 2042413056 | bytes 10321920 | tf_op jit(solution)/shard_map/dot_general | solution.py:71
  142.8 8.7 %all-to-all-start.1 = ((bf16[2,16,8,1152]{3,2,0,1:T(8,128)(2,1)}), bf16[2,16,8,1152]{3,2,0,1:T(8,128)(2,1)S(1)}, u32[]{:S(2)}, u32[]{:S(2)}) async-start(bf16[2,16,8,1152]{3,2,0,1:T(8,128)(2,1)} %copy.47), calls=%async_computation.1 | async-start | bytes 1179648 | tf_op jit(solution)/shard_map/all_to_all | solution.py:97
  151.6 74.9 %reduce-scatter.8.cloned.1.call-done = bf16[72,3456]{1,0:T(8,128)(2,1)} async-done(((bf16[1152,3456]{1,0:T(8,128)(2,1)}), bf16[72,3456]{1,0:T(8,128)(2,1)}) %reduce-scatter.8.cloned.1.call-update) | async-done | bytes 497680
  226.5 2.8 reshape.155
  230.3 80.8 %psum.7 = f32[2,2,1152]{2,0,1:T(2,128)S(1)} all-reduce(f32[2,2,1152]{2,0,1:T(2,128)S(1)} %pad_maximum_fusion.2), channel_id=1, replica_groups=mesh['frame'=16,'space'=16] {'frame','space'}, use_global_device_ids=true, to_apply=%region_10.0 | all-reduce | flops 4608 | bytes 36864 | tf_op jit(solution)/shard_map/psum | solution.py:89
  312.6 8.1 %reduce-scatter.6.cloned.1.call-done = bf16[72,1,216]{2,0,1:T(8,128)(2,1)} async-done(((bf16[72,16,216]{2,0,1:T(8,128)(2,1)}), bf16[72,1,216]{2,0,1:T(8,128)(2,1)}) %reduce-scatter.6.cloned.1.call-update) | async-done | bytes 31120 | tf_op jit(solution)/shard_map/reduce_scatter | solution.py:77
  320.7 46.2 %all_gather.7 = bf16[72,16,216]{2,0,1:T(8,128)(2,1)S(1)} all-gather(bf16[72,1,216]{2,0,1:T(8,128)(2,1)} %reduce-scatter.6.cloned.1.call-done), channel_id=1, replica_groups=mesh['frame'=16,'space'=16] {'frame'}, dimensions={1}, use_global_device_ids=true | all-gather | bytes 528768 | tf_op jit(solution)/shard_map/all_gather | solution.py:78
  (55 shorter events, 14.0 us)
Async XLA Ops:
  7.2 21.0 %copy-start = (f32[1000]{0:T(1024)S(1)}, f32[1000]{0:T(1024)}, u32[]{:S(2)}) copy-start(f32[1000]{0:T(1024)} %param.11) | copy-start | bytes 12004
  7.2 83.6 %all-gather.2.cloned.1.call-start = ((), (), s32[]{:S(2)}) async-start(), calls=%async_computation.4 | async-start | bytes 8460288 | tf_op jit(solution)/shard_map/all_gather | solution.py:39
  11.3 13.9 %copy-start.5 = (s32[2]{0:T(128)S(1)}, s32[2]{0:T(128)}, u32[]{:S(2)}) copy-start(s32[2]{0:T(128)} %param.12) | copy-start | bytes 28
  11.3 16.9 %copy-start.6 = (s32[2]{0:T(128)S(1)}, s32[2]{0:T(128)}, u32[]{:S(2)}) copy-start(s32[2]{0:T(128)} %param.13) | copy-start | bytes 28
  13.9 56.7 %all-to-all-start = ((bf16[2,1,128,2,1152]{4,0,3,1,2:T(2,128)(2,1)}), bf16[2,1,128,2,1152]{4,0,3,1,2:T(2,128)(2,1)S(1)}, u32[]{:S(2)}, u32[]{:S(2)}) async-start(bf16[2,1,128,2,1152]{4,0,3,1,2:T(2,128)(2,1)} %pad_maximum_fusion.1), calls=%async_computation | async-start | bytes 2359296 | tf_op jit(solution)/shard_map/all_to_all | solution.py:47
  25.2 201.3 %reduce-scatter.8.cloned.1.call-start = ((), (), s32[]{:S(2)}) async-start(), calls=%async_computation.6 | async-start | bytes 8460288
  70.8 3.9 %copy-start.1 = (bf16[2,1,128,2,1152]{4,2,0,3,1:T(8,128)(2,1)}, bf16[2,1,128,2,1152]{4,2,0,3,1:T(8,128)(2,1)S(1)}, u32[]{:S(2)}) copy-start(bf16[2,1,128,2,1152]{4,2,0,3,1:T(8,128)(2,1)S(1)} %copy.85) | copy-start | bytes 3538948
  105.9 1.7 copy-start.4
  128.1 6.7 %copy-start.3 = (bf16[256,3456]{1,0:T(8,128)(2,1)S(1)}, bf16[256,3456]{1,0:T(8,128)(2,1)}, u32[]{:S(2)}) copy-start(bf16[256,3456]{1,0:T(8,128)(2,1)} %reshape.154) | copy-start | bytes 5308420
  140.3 1.3 copy-start.2
  142.8 168.9 %all-to-all-start.1 = ((bf16[2,16,8,1152]{3,2,0,1:T(8,128)(2,1)}), bf16[2,16,8,1152]{3,2,0,1:T(8,128)(2,1)S(1)}, u32[]{:S(2)}, u32[]{:S(2)}) async-start(bf16[2,16,8,1152]{3,2,0,1:T(8,128)(2,1)} %copy.47), calls=%async_computation.1 | async-start | bytes 1179648 | tf_op jit(solution)/shard_map/all_to_all | solution.py:97
  151.5 169.2 %reduce-scatter.6.cloned.1.call-start = ((), (), s32[]{:S(2)}) async-start(), calls=%async_computation.5 | async-start | bytes 626688 | tf_op jit(solution)/shard_map/reduce_scatter | solution.py:77
Sparse Core Ops, SparseCore 0:
  9.9 80.8 all-gather.1
  140.4 86.0 reduce-scatter.7
  230.6 90.0 reduce-scatter.5

commit v2 on v1

--- a/solution.py
+++ b/solution.py
@@ -1,7 +1,13 @@
+import functools
+
 import jax
 import jax.numpy as jnp
 from jax import lax
+from jax.experimental import pallas as pl
+from jax.experimental.pallas import tpu as pltpu
 from jax.sharding import PartitionSpec as P
+
+MESH = pl.DeviceIdType.MESH
 
 HEADS = 16
 HEAD_DIM = 72
@@ -27,6 +33,123 @@
         grad_keys.astype(jnp.bfloat16),
         grad_values.astype(jnp.bfloat16),
     )
+
+
+def reduce_kernel(
+    nf, ns, chunks_ref, sums_ref, gw_ref, gm_ref,
+    recv1, msum1, redbuf, mbuf, recv2, msum2, s1c, r1c, s1m, r1m, s2c, r2c, s2m, r2m,
+):
+    me_f = lax.axis_index("frame")
+    me_s = lax.axis_index("space")
+    barrier = pltpu.get_barrier_semaphore()
+    for k in range(1, nf):
+        pl.semaphore_signal(
+            barrier, inc=1, device_id=(lax.rem(me_f + k, nf), me_s), device_id_type=MESH
+        )
+    for k in range(1, ns):
+        pl.semaphore_signal(
+            barrier, inc=1, device_id=(me_f, lax.rem(me_s + k, ns)), device_id_type=MESH
+        )
+    pl.semaphore_wait(barrier, (nf - 1) + (ns - 1))
+
+    sends = []
+    for k in range(1, nf):
+        t = lax.rem(me_f + k, nf)
+        c = pltpu.make_async_remote_copy(
+            src_ref=chunks_ref.at[t], dst_ref=recv1.at[me_f], send_sem=s1c.at[k],
+            recv_sem=r1c.at[me_f], device_id=(t, me_s), device_id_type=MESH,
+        )
+        c.start()
+        m = pltpu.make_async_remote_copy(
+            src_ref=sums_ref, dst_ref=msum1.at[me_f], send_sem=s1m.at[k],
+            recv_sem=r1m.at[me_f], device_id=(t, me_s), device_id_type=MESH,
+        )
+        m.start()
+        sends += [c, m]
+    recv1[me_f] = chunks_ref[me_f]
+    msum1[me_f] = sums_ref[...]
+    for k in range(1, nf):
+        src = lax.rem(me_f + nf - k, nf)
+        pltpu.make_async_remote_copy(
+            src_ref=chunks_ref.at[0], dst_ref=recv1.at[src], send_sem=s1c.at[k],
+            recv_sem=r1c.at[src], device_id=(src, me_s), device_id_type=MESH,
+        ).wait_recv()
+        pltpu.make_async_remote_copy(
+            src_ref=sums_ref, dst_ref=msum1.at[src], send_sem=s1m.at[k],
+            recv_sem=r1m.at[src], device_id=(src, me_s), device_id_type=MESH,
+        ).wait_recv()
+    for c in sends:
+        c.wait_send()
+    acc = recv1[0].astype(jnp.float32)
+    macc = msum1[0]
+    for j in range(1, nf):
+        acc = acc + recv1[j].astype(jnp.float32)
+        macc = macc + msum1[j]
+    redbuf[...] = acc
+    mbuf[...] = macc
+    recv2[me_f] = acc
+    msum2[me_s] = macc
+
+    sends = []
+    for k in range(1, nf):
+        t = lax.rem(me_f + k, nf)
+        c = pltpu.make_async_remote_copy(
+            src_ref=redbuf, dst_ref=recv2.at[me_f], send_sem=s2c.at[k],
+            recv_sem=r2c.at[me_f], device_id=(t, me_s), device_id_type=MESH,
+        )
+        c.start()
+        sends.append(c)
+    for k in range(1, ns):
+        t = lax.rem(me_s + k, ns)
+        m = pltpu.make_async_remote_copy(
+            src_ref=mbuf, dst_ref=msum2.at[me_s], send_sem=s2m.at[k],
+            recv_sem=r2m.at[me_s], device_id=(me_f, t), device_id_type=MESH,
+        )
+        m.start()
+        sends.append(m)
+    for k in range(1, nf):
+        src = lax.rem(me_f + nf - k, nf)
+        pltpu.make_async_remote_copy(
+            src_ref=redbuf, dst_ref=recv2.at[src], send_sem=s2c.at[k],
+            recv_sem=r2c.at[src], device_id=(src, me_s), device_id_type=MESH,
+        ).wait_recv()
+    for k in range(1, ns):
+        src = lax.rem(me_s + ns - k, ns)
+        pltpu.make_async_remote_copy(
+            src_ref=mbuf, dst_ref=msum2.at[src], send_sem=s2m.at[k],
+            recv_sem=r2m.at[src], device_id=(me_f, src), device_id_type=MESH,
+        ).wait_recv()
+    for c in sends:
+        c.wait_send()
+    gw_ref[...] = recv2[...]
+    total = msum2[0]
+    for j in range(1, ns):
+        total = total + msum2[j]
+    gm_ref[...] = total
+
+
+def reduce_frame(chunks, sums, nf, ns):
+    count, rows, cols = chunks.shape
+    vmem = pl.BlockSpec(memory_space=pltpu.VMEM)
+    return pl.pallas_call(
+        functools.partial(reduce_kernel, nf, ns),
+        out_shape=(
+            jax.ShapeDtypeStruct((count, rows, cols), jnp.float32),
+            jax.ShapeDtypeStruct(sums.shape, jnp.float32),
+        ),
+        in_specs=[vmem, vmem],
+        out_specs=(vmem, vmem),
+        scratch_shapes=[
+            pltpu.VMEM((nf, rows, cols), chunks.dtype),
+            pltpu.VMEM((nf,) + sums.shape, jnp.float32),
+            pltpu.VMEM((rows, cols), jnp.float32),
+            pltpu.VMEM(sums.shape, jnp.float32),
+            pltpu.VMEM((nf, rows, cols), jnp.float32),
+            pltpu.VMEM((ns,) + sums.shape, jnp.float32),
+        ]
+        + [pltpu.SemaphoreType.DMA((max(nf, ns),))] * 8,
+        compiler_params=pltpu.CompilerParams(collective_id=0, has_side_effects=True),
+    )(chunks, sums)
 
 
 def per_device(
@@ -73,11 +196,8 @@
     ).astype(jnp.bfloat16)
     col_blk = 3 * model_width // frame_n
     share = lax.psum_scatter(term, "space", scatter_dimension=0, tiled=True)
-    share = share.reshape(share.shape[0], frame_n, col_blk)
-    share = lax.psum_scatter(share, "frame", scatter_dimension=1, tiled=True)
-    grad_weight = lax.all_gather(share, "frame", axis=1, tiled=True)
-    grad_weight = grad_weight.reshape(share.shape[0], 3 * model_width)
-    grad_weight = grad_weight.astype(jnp.float32) * grad_scale_factor
+    row_blk = share.shape[0]
+    share = share.reshape(row_blk, frame_n, col_blk).transpose(1, 0, 2)
     grad_hidden = lax.dot_general(
         grad_rows, w_full, (((1,), (1,)), ((), ())), preferred_element_type=jnp.float32
     )
@@ -86,7 +206,10 @@
         [jnp.sum(grad_hidden, axis=(1, 2)), jnp.sum(grad_hidden * normed, axis=(1, 2))],
         axis=1,
     )
-    grad_modulation = lax.psum(local_sums, ("frame", "space")) * grad_scale_factor
+    local_sums = local_sums.reshape(-1, model_width)
+    gw, gm = reduce_frame(share, local_sums, frame_n, space_n)
+    grad_weight = gw.transpose(1, 0, 2).reshape(row_blk, 3 * model_width) * grad_scale_factor
+    grad_modulation = gm.reshape(clip_count, 2, model_width) * grad_scale_factor
     grad_normed = grad_hidden * (1.0 + scale)
     grad_input = (
         grad_normed

time: 376 us -> 308 us (0.82); the launches traced: 376 us -> 303 us
  blocking collectives: 127 us -> 0 us
  Pallas kernels: 0 us -> 61.9 us
  waiting for transfers between devices: 141 us -> 132 us
    psum x1 -> x0, blocking collectives: 80.8 us -> none  [per_device(): lax.psum(local_sums, ('frame', 'space')) * grad_scale_factor]
    pallas_call x0 -> x1, Pallas kernels: none -> 61.9 us  [reduce_frame(): pl.pallas_call(functools.partial(reduce_kernel, nf, ns), out_shape=(jax.S...]
    all_gather x1 -> x0, blocking collectives: 46.2 us -> none  [per_device(): grad_weight = lax.all_gather(share, 'frame', axis=1, tiled=True)]
    unnamed x4 -> x3, waiting for transfers between devices: 75.7 us -> 51.7 us
    all_to_all x1, waiting for transfers between devices: 0.01 us -> 22.5 us  [per_device(): lax.all_to_all(grad_input, 'frame', split_axis=1, concat_axis=2, tiled=True)]
    reduce_scatter x1 -> x0, waiting for transfers between devices: 8.11 us -> none  [per_device(): share = lax.psum_scatter(share, 'frame', scatter_dimension=1, tiled=True)]
  transfers between devices with their start and end apart: 5 -> 4, of which waited for: 4 -> 4; matrix products, arithmetic and copies ran while one was open for 5% -> 6% of each run, Pallas kernels for 0% -> 0%
where the time goes in v2:
time: 308 us; the launch traced here: 303 us
  waiting for transfers between devices  132 us (43%)
  Pallas kernels  61.9 us (20%)
  local copies, waits for them, and re-layouts  38.4 us (12%)
  matrix products  30.6 us (10%)
  starting transfers between devices  20 us (6%)
  between operations  14.4 us (5%)
  other arithmetic  6.11 us (2%)
    pallas_call x1, Pallas kernels, reduce_frame(): pl.pallas_call(functools.partial(reduce_kernel, nf, ns), out_shape=(jax.S...  61.9 us
    unnamed x3, waiting for transfers between devices  51.7 us
    all_to_all x1, waiting for transfers between devices, per_device(): lax.all_to_all(both, 'frame', split_axis=2, concat_axis=1, tiled=True)  41.8 us
    all_to_all x1, waiting for transfers between devices, per_device(): lax.all_to_all(grad_input, 'frame', split_axis=1, concat_axis=2, tiled=True)  22.5 us
    all_gather x1, waiting for transfers between devices, per_device(): w_full = lax.all_gather(w_qkv, 'space', axis=0, tiled=True)  15.8 us
    all_to_all x1, starting transfers between devices, per_device(): lax.all_to_all(both, 'frame', split_axis=2, concat_axis=1, tiled=True)  11.2 us
    all_to_all x1, starting transfers between devices, per_device(): lax.all_to_all(grad_input, 'frame', split_axis=1, concat_axis=2, tiled=True)  8.67 us
    reshape x1, local copies, waits for them, and re-layouts, per_device(): pieces = projected.reshape(clip_count, frames, across, 3, HEADS, HEAD_DIM)  7.1 us
  transfers between devices with their start and end apart: 4, of which 4 were waited for; matrix products, arithmetic and copies ran while one was open for 6% of the time, Pallas kernels for 0%

profile of v2, /device:TPU:6, one launch (start us, length us, event | category | flops | bytes accessed | tf_op | source)
XLA Modules:
  0.0 303.1 jit_solution(7861790101254611122)
XLA Ops:
  7.9 1.7 copy.39
  9.6 1.7 copy.40
  11.3 2.7 pad_maximum_fusion.1
  13.9 11.2 %all-to-all-start = ((bf16[2,1,128,2,1152]{4,0,3,1,2:T(2,128)(2,1)}), bf16[2,1,128,2,1152]{4,0,3,1,2:T(2,128)(2,1)S(1)}, u32[]{:S(2)}, u32[]{:S(2)}) async-start(bf16[2,1,128,2,1152]{4,0,3,1,2:T(2,128)(2,1)} %pad_maximum_fusion.1), calls=%async_computation | async-start | bytes 2359296 | tf_op jit(solution)/shard_map/all_to_all | solution.py:170
  25.2 2.9 gather_fusion
  28.9 41.8 %all-to-all-done = bf16[2,1,128,2,1152]{4,0,3,1,2:T(2,128)(2,1)S(1)} async-done(((bf16[2,1,128,2,1152]{4,0,3,1,2:T(2,128)(2,1)}), bf16[2,1,128,2,1152]{4,0,3,1,2:T(2,128)(2,1)S(1)}, u32[]{:S(2)}, u32[]{:S(2)}) %all-to-all-start) | async-done | bytes 1179680 | tf_op jit(solution)/shard_map/all_to_all | solution.py:170
  71.5 3.1 %reshape.163 = f32[2,16,8,16,72]{4,3,2,1,0:T(8,128)} reshape(f32[2,16,8,1,1152]{4,2,1,0,3:T(8,128)S(1)} %slice_convert_fusion) | data formatting | bytes 2359296 | tf_op jit(solution)/shard_map/convert_element_type | solution.py:188
  75.0 15.8 %all-gather.2.cloned.1.call-done = bf16[1152,3456]{1,0:T(8,128)(2,1)} async-done(((bf16[72,3456]{1,0:T(8,128)(2,1)}), bf16[1152,3456]{1,0:T(8,128)(2,1)}) %all-gather.2.cloned.1.call-update) | async-done | bytes 7962640 | tf_op jit(solution)/shard_map/all_gather | solution.py:162
  90.8 7.0 %convolution_convert_fusion.1 = bf16[256,3456]{1,0:T(8,128)(2,1)} fusion(bf16[256,1152]{1,0:T(8,128)(2,1)S(1)} %fusion.8, bf16[1152,3456]{1,0:T(8,128)(2,1)} %all-gather.2.cloned.1.call-done), kind=kOutput, calls=%fused_computation.5 | convolution fusion | flops 2039316480 | bytes 10321920 | tf_op jit(solution)/shard_map/dot_general | solution.py:184
  97.8 7.1 %reshape.157 = bf16[2,16,8,3,16,72]{5,4,3,2,1,0:T(8,128)(2,1)S(1)} reshape(bf16[256,3456]{1,0:T(8,128)(2,1)} %convolution_convert_fusion.1) | data formatting | bytes 3538944 | tf_op jit(solution)/shard_map/reshape | solution.py:185
  105.9 1.7 fusion.4
  107.6 2.3 multiply_reduce_fusion
  109.9 2.4 fusion.6
  112.3 2.2 fusion.7
  114.5 2.8 fusion.5
  118.9 4.6 %dot_general.32 = bf16[2,16,8,3456]{3,2,1,0:T(8,128)(2,1)} reshape(bf16[2,16,8,3,16,72]{5,4,3,2,1,0:T(8,128)(2,1)S(1)} %copy.47) | data formatting | bytes 3538944 | tf_op jit(solution)/shard_map/dot_general | solution.py:201
  123.5 4.6 %reshape.159 = bf16[256,3456]{1,0:T(8,128)(2,1)} reshape(bf16[2,16,8,3,16,72]{5,4,3,2,1,0:T(8,128)(2,1)S(1)} %copy.47) | data formatting | bytes 3538944 | tf_op jit(solution)/shard_map/reshape | solution.py:192
  128.1 6.7 %multiply_reduce_fusion.1 = (f32[2,1152]{1,0:T(2,128)S(1)}, f32[2,16,8]{2,1,0:T(8,128)S(1)}, f32[2,16,8]{2,1,0:T(8,128)S(1)}, f32[2,1152]{1,0:T(2,128)S(1)}, bf1...) fusion(f32[2,16,8]{2,1,0:T(8,128)S(1)} %add_rsqrt_fusion, ...), kind=kOutput, calls=%fused_computation.29 | convolution fusion | flops 2042260480 | bytes 12132352 | tf_op jit(solution)/shard_map/dot_general | solution.py:201
  134.8 5.4 %convolution_convert_fusion = bf16[1152,3456]{1,0:T(8,128)(2,1)} fusion(bf16[256,1152]{1,0:T(8,128)(2,1)S(1)} %bitcast.105, bf16[256,3456]{1,0:T(8,128)(2,1)S(1)} %copy-done.3), kind=kOutput, calls=%fused_computation.2 | convolution fusion | flops 2042413056 | bytes 10321920 | tf_op jit(solution)/shard_map/dot_general | solution.py:194
  142.8 8.7 %all-to-all-start.1 = ((bf16[2,16,8,1152]{3,2,0,1:T(8,128)(2,1)}), bf16[2,16,8,1152]{3,2,0,1:T(8,128)(2,1)S(1)}, u32[]{:S(2)}, u32[]{:S(2)}) async-start(bf16[2,16,8,1152]{3,2,0,1:T(8,128)(2,1)} %copy.48), calls=%async_computation.1 | async-start | bytes 1179648 | tf_op jit(solution)/shard_map/all_to_all | solution.py:220
  152.2 22.5 %all-to-all-done.1 = bf16[2,16,8,1152]{3,2,0,1:T(8,128)(2,1)S(1)} async-done(((bf16[2,16,8,1152]{3,2,0,1:T(8,128)(2,1)}), bf16[2,16,8,1152]{3,2,0,1:T(8,128)(2,1)S(1)}, u32[]{:S(2)}, u32[]{:S(2)}) %all-to-all-start.1) | async-done | bytes 589856 | tf_op jit(solution)/shard_map/all_to_all | solution.py:220
  175.6 51.0 %reduce-scatter.5.cloned.1.call-done = bf16[72,3456]{1,0:T(8,128)(2,1)} async-done(((bf16[1152,3456]{1,0:T(8,128)(2,1)}), bf16[72,3456]{1,0:T(8,128)(2,1)}) %reduce-scatter.5.cloned.1.call-update) | async-done | bytes 497680
  226.6 2.8 reshape.160
  230.3 61.9 %shard_map.94 = (f32[16,72,216]{2,1,0:T(8,128)}, f32[4,1152]{1,0:T(4,128)}) custom-call(bf16[16,72,216]{2,1,0:T(8,128)(2,1)} %bitcast.102, f32[4,1152]{1,0:T(4,128)} %reshape.161.sums_ref), custom_call_target="tpu_custom_call" | custom-call | tf_op jit(solution)/shard_map/pallas_call | solution.py:134
  (56 shorter events, 14.2 us)
Async XLA Ops:
  7.2 21.0 %copy-start = (f32[1000]{0:T(1024)S(1)}, f32[1000]{0:T(1024)}, u32[]{:S(2)}) copy-start(f32[1000]{0:T(1024)} %param.11) | copy-start | bytes 12004
  7.2 83.6 %all-gather.2.cloned.1.call-start = ((), (), s32[]{:S(2)}) async-start(), calls=%async_computation.3 | async-start | bytes 8460288 | tf_op jit(solution)/shard_map/all_gather | solution.py:162
  11.3 13.9 %copy-start.6 = (s32[2]{0:T(128)S(1)}, s32[2]{0:T(128)}, u32[]{:S(2)}) copy-start(s32[2]{0:T(128)} %param.12) | copy-start | bytes 28
  11.3 16.9 %copy-start.7 = (s32[2]{0:T(128)S(1)}, s32[2]{0:T(128)}, u32[]{:S(2)}) copy-start(s32[2]{0:T(128)} %param.13) | copy-start | bytes 28
  13.9 56.7 %all-to-all-start = ((bf16[2,1,128,2,1152]{4,0,3,1,2:T(2,128)(2,1)}), bf16[2,1,128,2,1152]{4,0,3,1,2:T(2,128)(2,1)S(1)}, u32[]{:S(2)}, u32[]{:S(2)}) async-start(bf16[2,1,128,2,1152]{4,0,3,1,2:T(2,128)(2,1)} %pad_maximum_fusion.1), calls=%async_computation | async-start | bytes 2359296 | tf_op jit(solution)/shard_map/all_to_all | solution.py:170
  25.2 201.4 %reduce-scatter.5.cloned.1.call-start = ((), (), s32[]{:S(2)}) async-start(), calls=%async_computation.4 | async-start | bytes 8460288
  70.8 3.9 %copy-start.1 = (bf16[2,1,128,2,1152]{4,2,0,3,1:T(8,128)(2,1)}, bf16[2,1,128,2,1152]{4,2,0,3,1:T(8,128)(2,1)S(1)}, u32[]{:S(2)}) copy-start(bf16[2,1,128,2,1152]{4,2,0,3,1:T(8,128)(2,1)S(1)} %copy.86) | copy-start | bytes 3538948
  105.9 1.7 copy-start.4
  128.1 6.7 %copy-start.3 = (bf16[256,3456]{1,0:T(8,128)(2,1)S(1)}, bf16[256,3456]{1,0:T(8,128)(2,1)}, u32[]{:S(2)}) copy-start(bf16[256,3456]{1,0:T(8,128)(2,1)} %reshape.159) | copy-start | bytes 5308420
  140.3 1.3 copy-start.2
  142.8 31.9 %all-to-all-start.1 = ((bf16[2,16,8,1152]{3,2,0,1:T(8,128)(2,1)}), bf16[2,16,8,1152]{3,2,0,1:T(8,128)(2,1)S(1)}, u32[]{:S(2)}, u32[]{:S(2)}) async-start(bf16[2,16,8,1152]{3,2,0,1:T(8,128)(2,1)} %copy.48), calls=%async_computation.1 | async-start | bytes 1179648 | tf_op jit(solution)/shard_map/all_to_all | solution.py:220
  293.6 2.0 copy-start.5
Sparse Core Ops, SparseCore 0:
  9.9 80.8 all-gather.1
  140.4 86.0 reduce-scatter.4

commit v3 on v2

--- a/solution.py
+++ b/solution.py
@@ -36,19 +36,24 @@
 
 
 def reduce_kernel(
-    nf, ns, chunks_ref, sums_ref, gw_ref, gm_ref,
+    nf, sub, chunks_ref, sums_ref, gw_ref, gm_ref,
     recv1, msum1, redbuf, mbuf, recv2, msum2, s1c, r1c, s1m, r1m, s2c, r2c, s2m, r2m,
 ):
+    nz, nx, nc = sub
+    ns = nz * nx * nc
     me_f = lax.axis_index("frame")
-    me_s = lax.axis_index("space")
+    me_s = (lax.axis_index("sz") * nx + lax.axis_index("sx")) * nc + lax.axis_index("sc")
+
+    def dev(f, s):
+        return (f, s // (nx * nc), lax.rem(s // nc, nx), lax.rem(s, nc))
     barrier = pltpu.get_barrier_semaphore()
     for k in range(1, nf):
         pl.semaphore_signal(
-            barrier, inc=1, device_id=(lax.rem(me_f + k, nf), me_s), device_id_type=MESH
+            barrier, inc=1, device_id=dev(lax.rem(me_f + k, nf), me_s), device_id_type=MESH
         )
     for k in range(1, ns):
         pl.semaphore_signal(
-            barrier, inc=1, device_id=(me_f, lax.rem(me_s + k, ns)), device_id_type=MESH
+            barrier, inc=1, device_id=dev(me_f, lax.rem(me_s + k, ns)), device_id_type=MESH
         )
     pl.semaphore_wait(barrier, (nf - 1) + (ns - 1))
 
@@ -57,12 +62,12 @@
         t = lax.rem(me_f + k, nf)
         c = pltpu.make_async_remote_copy(
             src_ref=chunks_ref.at[t], dst_ref=recv1.at[me_f], send_sem=s1c.at[k],
-            recv_sem=r1c.at[me_f], device_id=(t, me_s), device_id_type=MESH,
+            recv_sem=r1c.at[me_f], device_id=dev(t, me_s), device_id_type=MESH,
         )
         c.start()
         m = pltpu.make_async_remote_copy(
             src_ref=sums_ref, dst_ref=msum1.at[me_f], send_sem=s1m.at[k],
-            recv_sem=r1m.at[me_f], device_id=(t, me_s), device_id_type=MESH,
+            recv_sem=r1m.at[me_f], device_id=dev(t, me_s), device_id_type=MESH,
         )
         m.start()
         sends += [c, m]
@@ -72,11 +77,11 @@
         src = lax.rem(me_f + nf - k, nf)
         pltpu.make_async_remote_copy(
             src_ref=chunks_ref.at[0], dst_ref=recv1.at[src], send_sem=s1c.at[k],
-            recv_sem=r1c.at[src], device_id=(src, me_s), device_id_type=MESH,
+            recv_sem=r1c.at[src], device_id=dev(src, me_s), device_id_type=MESH,
         ).wait_recv()
         pltpu.make_async_remote_copy(
             src_ref=sums_ref, dst_ref=msum1.at[src], send_sem=s1m.at[k],
-            recv_sem=r1m.at[src], device_id=(src, me_s), device_id_type=MESH,
+            recv_sem=r1m.at[src], device_id=dev(src, me_s), device_id_type=MESH,
         ).wait_recv()
     for c in sends:
         c.wait_send()
@@ -95,7 +100,7 @@
         t = lax.rem(me_f + k, nf)
         c = pltpu.make_async_remote_copy(
             src_ref=redbuf, dst_ref=recv2.at[me_f], send_sem=s2c.at[k],
-            recv_sem=r2c.at[me_f], device_id=(t, me_s), device_id_type=MESH,
+            recv_sem=r2c.at[me_f], device_id=dev(t, me_s), device_id_type=MESH,
         )
         c.start()
         sends.append(c)
@@ -103,7 +108,7 @@
         t = lax.rem(me_s + k, ns)
         m = pltpu.make_async_remote_copy(
             src_ref=mbuf, dst_ref=msum2.at[me_s], send_sem=s2m.at[k],
-            recv_sem=r2m.at[me_s], device_id=(me_f, t), device_id_type=MESH,
+            recv_sem=r2m.at[me_s], device_id=dev(me_f, t), device_id_type=MESH,
         )
         m.start()
         sends.append(m)
@@ -111,13 +116,13 @@
         src = lax.rem(me_f + nf - k, nf)
         pltpu.make_async_remote_copy(
             src_ref=redbuf, dst_ref=recv2.at[src], send_sem=s2c.at[k],
-            recv_sem=r2c.at[src], device_id=(src, me_s), device_id_type=MESH,
+            recv_sem=r2c.at[src], device_id=dev(src, me_s), device_id_type=MESH,
         ).wait_recv()
     for k in range(1, ns):
         src = lax.rem(me_s + ns - k, ns)
         pltpu.make_async_remote_copy(
             src_ref=mbuf, dst_ref=msum2.at[src], send_sem=s2m.at[k],
-            recv_sem=r2m.at[src], device_id=(me_f, src), device_id_type=MESH,
+            recv_sem=r2m.at[src], device_id=dev(me_f, src), device_id_type=MESH,
         ).wait_recv()
     for c in sends:
         c.wait_send()
@@ -128,11 +133,11 @@
     gm_ref[...] = total
 
 
-def reduce_frame(chunks, sums, nf, ns):
+def reduce_frame(chunks, sums, nf, sub):
     count, rows, cols = chunks.shape
     vmem = pl.BlockSpec(memory_space=pltpu.VMEM)
     return pl.pallas_call(
-        functools.partial(reduce_kernel, nf, ns),
+        functools.partial(reduce_kernel, nf, sub),
         out_shape=(
             jax.ShapeDtypeStruct((count, rows, cols), jnp.float32),
             jax.ShapeDtypeStruct(sums.shape, jnp.float32),
@@ -145,9 +150,9 @@
             pltpu.VMEM((rows, cols), jnp.float32),
             pltpu.VMEM(sums.shape, jnp.float32),
             pltpu.VMEM((nf, rows, cols), jnp.float32),
-            pltpu.VMEM((ns,) + sums.shape, jnp.float32),
+            pltpu.VMEM((sub[0] * sub[1] * sub[2],) + sums.shape, jnp.float32),
         ]
-        + [pltpu.SemaphoreType.DMA((max(nf, ns),))] * 8,
+        + [pltpu.SemaphoreType.DMA((max(nf, sub[0] * sub[1] * sub[2]),))] * 8,
         compiler_params=pltpu.CompilerParams(collective_id=0, has_side_effects=True),
     )(chunks, sums)
 
@@ -157,9 +162,13 @@
 ):
     clip_count, frame_dev, row_dev, col_count, model_width = hidden_in.shape
     frame_n = lax.axis_size("frame")
-    space_n = lax.axis_size("space")
+    sub = (lax.axis_size("sz"), lax.axis_size("sx"), lax.axis_size("sc"))
+    space_n = sub[0] * sub[1] * sub[2]
     positions = row_dev * col_count
-    w_full = lax.all_gather(w_qkv, "space", axis=0, tiled=True)
+    w_full = lax.all_gather(w_qkv, "sz", axis=0)
+    w_full = lax.all_gather(w_full, "sx", axis=0)
+    w_full = lax.all_gather(w_full, "sc", axis=0)
+    w_full = w_full.reshape(-1, w_qkv.shape[1])
     both = jnp.stack(
         [
             hidden_in.reshape(clip_count, frame_dev, positions, model_width),
@@ -180,7 +189,9 @@
     shift = modulation[:, 0][:, None, None, :]
     scale = modulation[:, 1][:, None, None, :]
     modulated = (normed * (1.0 + scale) + shift).astype(jnp.bfloat16)
-    mod_rows = modulated.reshape(-1, model_width)
+    row_blk = model_width // space_n
+    mod_rows = modulated.reshape((-1,) + sub + (row_blk,)).transpose(0, 3, 2, 1, 4)
+    mod_rows = mod_rows.reshape(-1, model_width)
     projected = jnp.dot(mod_rows, w_full, preferred_element_type=jnp.float32).astype(jnp.bfloat16)
     pieces = projected.reshape(clip_count, frames, across, 3, HEADS, HEAD_DIM)
     loss_weight = snr_table[weight_index]
@@ -195,19 +206,24 @@
         mod_rows, grad_rows, (((0,), (0,)), ((), ())), preferred_element_type=jnp.float32
     ).astype(jnp.bfloat16)
     col_blk = 3 * model_width // frame_n
-    share = lax.psum_scatter(term, "space", scatter_dimension=0, tiled=True)
-    row_blk = share.shape[0]
+    share = term.reshape(sub[2], -1, 3 * model_width)
+    share = lax.psum_scatter(share, "sc", scatter_dimension=0, tiled=True)
+    share = share.reshape(sub[1], -1, 3 * model_width)
+    share = lax.psum_scatter(share, "sx", scatter_dimension=0, tiled=True)
+    share = share.reshape(sub[0], -1, 3 * model_width)
+    share = lax.psum_scatter(share, "sz", scatter_dimension=0, tiled=True)
     share = share.reshape(row_blk, frame_n, col_blk).transpose(1, 0, 2)
     grad_hidden = lax.dot_general(
         grad_rows, w_full, (((1,), (1,)), ((), ())), preferred_element_type=jnp.float32
     )
+    grad_hidden = grad_hidden.reshape((-1,) + sub[::-1] + (row_blk,)).transpose(0, 3, 2, 1, 4)
     grad_hidden = grad_hidden.reshape(values_in.shape)
     local_sums = jnp.stack(
         [jnp.sum(grad_hidden, axis=(1, 2)), jnp.sum(grad_hidden * normed, axis=(1, 2))],
         axis=1,
     )
     local_sums = local_sums.reshape(-1, model_width)
-    gw, gm = reduce_frame(share, local_sums, frame_n, space_n)
+    gw, gm = reduce_frame(share, local_sums, frame_n, sub)
     grad_weight = gw.transpose(1, 0, 2).reshape(row_blk, 3 * model_width) * grad_scale_factor
     grad_modulation = gm.reshape(clip_count, 2, model_width) * grad_scale_factor
     grad_normed = grad_hidden * (1.0 + scale)
@@ -223,16 +239,20 @@
 
 
 def solution(mesh):
+    space_sub = (2, 4, 2)
+    devices = mesh.devices.reshape((mesh.shape["frame"],) + space_sub)
+    fine = jax.sharding.Mesh(devices, ("frame", "sz", "sx", "sc"))
+    space = ("sz", "sx", "sc")
     in_specs = (
-        P(None, "frame", "space", None, None),
-        P(None, "frame", "space", None, None),
-        P("space", None),
-        P(),
-        P(),
-        P(),
-        P(),
-    )
-    out_specs = (P(None, "frame", "space", None, None), P("space", None), P())
+        P(None, "frame", space, None, None),
+        P(None, "frame", space, None, None),
+        P(space, None),
+        P(),
+        P(),
+        P(),
+        P(),
+    )
+    out_specs = (P(None, "frame", space, None, None), P(space, None), P())
     return jax.shard_map(
-        per_device, mesh=mesh, in_specs=in_specs, out_specs=out_specs, check_vma=False
-    )
+        per_device, mesh=fine, in_specs=in_specs, out_specs=out_specs, check_vma=False
+    )

time: 308 us -> 369 us (1.20)
  local copies, waits for them, and re-layouts: 38.4 us -> 67.7 us
  blocking collectives: 0 us -> 16 us
  waiting for transfers between devices: 132 us -> 146 us
  Pallas kernels: 61.9 us -> 56.9 us
  other arithmetic: 6.11 us -> 10.3 us
    reduce_scatter x0 -> x2, waiting for transfers between devices: none -> 64 us  [the longest x1 45.1 us: per_device(): share = lax.psum_scatter(share, 'sx', scatter_dimension=0, tiled=True)]
    unnamed x3 -> x6, waiting for transfers between devices: 51.7 us -> 0.08 us
    all_gather x1 -> x2, waiting for transfers between devices: 15.8 us -> 49.3 us  [the longest x1 49.3 us: per_device(): w_full = lax.all_gather(w_full, 'sx', axis=0)]
    all_to_all x1, waiting for transfers between devices: 41.8 us -> 13.1 us  [per_device(): lax.all_to_all(both, 'frame', split_axis=2, concat_axis=1, tiled=True)]
    all_gather x0 -> x1, blocking collectives: none -> 16 us  [per_device(): w_full = lax.all_gather(w_qkv, 'sz', axis=0)]
    add x0 -> x3, local copies, waits for them, and re-layouts: none -> 8.98 us  [per_device(): modulated = (normed * (1.0 + scale) + shift).astype(jnp.bfloat16)]
    convert_element_type x0 -> x2, local copies, waits for them, and re-layouts: none -> 7.77 us  [per_device(): values_in = both[:, :, :, 0].astype(jnp.float32)]
    mul x0 -> x3, local copies, waits for them, and re-layouts: none -> 6.21 us  [per_device(): modulated = (normed * (1.0 + scale) + shift).astype(jnp.bfloat16)]
  transfers between devices with their start and end apart: 4 -> 7, of which waited for: 4 -> 5; matrix products, arithmetic and copies ran while one was open for 6% -> 17% of each run, Pallas kernels for 0% -> 0%
where the time goes in v3:
time: 369 us; the launch traced here: 362 us
  waiting for transfers between devices  146 us (40%)
  local copies, waits for them, and re-layouts  67.7 us (18%)
  Pallas kernels  56.9 us (15%)
  matrix products  30.3 us (8%)
  starting transfers between devices  19.9 us (5%)
  blocking collectives  16 us (4%)
  between operations  14.5 us (4%)
  other arithmetic  10.3 us (3%)
    pallas_call x1, Pallas kernels, reduce_frame(): pl.pallas_call(functools.partial(reduce_kernel, nf, sub), out_shape=(jax....  56.9 us
    all_gather x1, waiting for transfers between devices, per_device(): w_full = lax.all_gather(w_full, 'sx', axis=0)  49.3 us
    reduce_scatter x1, waiting for transfers between devices, per_device(): share = lax.psum_scatter(share, 'sx', scatter_dimension=0, tiled=True)  45.1 us
    all_to_all x1, waiting for transfers between devices, per_device(): lax.all_to_all(grad_input, 'frame', split_axis=1, concat_axis=2, tiled=True)  19.9 us
    reduce_scatter x1, waiting for transfers between devices, per_device(): share = lax.psum_scatter(share, 'sc', scatter_dimension=0, tiled=True)  18.8 us
    all_gather x1, blocking collectives, per_device(): w_full = lax.all_gather(w_qkv, 'sz', axis=0)  16 us
    all_to_all x1, waiting for transfers between devices, per_device(): lax.all_to_all(both, 'frame', split_axis=2, concat_axis=1, tiled=True)  13.1 us
    all_to_all x1, starting transfers between devices, per_device(): lax.all_to_all(both, 'frame', split_axis=2, concat_axis=1, tiled=True)  9.85 us
  transfers between devices with their start and end apart: 7, of which 5 were waited for; matrix products, arithmetic and copies ran while one was open for 17% of the time, Pallas kernels for 0%

profile of v3, /device:TPU:6, one launch (start us, length us, event | category | flops | bytes accessed | tf_op | source)
XLA Modules:
  0.0 361.9 jit_solution(17629933219138197301)
XLA Ops:
  7.2 16.0 %all-gather = bf16[144,3456]{1,0:T(8,128)(2,1)} all-gather(bf16[72,3456]{1,0:T(8,128)(2,1)} %param.9), channel_id=2, replica_groups=mesh['frame'=16,'sz'=2,'sx'=4,'sc'=2] {'sz'}, dimensions={0}, use_global_device_ids=true | all-gather | bytes 1492992 | tf_op jit(solution)/shard_map/all_gather | solution.py:168
  23.3 49.3 %all-gather.6.cloned.1.call-done = bf16[8,72,3456]{2,1,0:T(8,128)(2,1)} async-done(((bf16[2,72,3456]{2,1,0:T(8,128)(2,1)}), bf16[8,72,3456]{2,1,0:T(8,128)(2,1)}) %all-gather.6.cloned.1.call-update) | async-done | bytes 3981328 | tf_op jit(solution)/shard_map/all_gather | solution.py:169
  76.9 9.8 %all-to-all-start = ((bf16[2,1,128,2,1152]{4,0,3,1,2:T(2,128)(2,1)}), bf16[2,1,128,2,1152]{4,0,3,1,2:T(2,128)(2,1)}, u32[]{:S(2)}, u32[]{:S(2)}) async-start(bf16[2,1,128,2,1152]{4,0,3,1,2:T(2,128)(2,1)} %pad_maximum_fusion.1), calls=%async_computation | async-start | bytes 2359296 | tf_op jit(solution)/shard_map/all_to_all | solution.py:179
  86.8 3.6 gather_fusion
  90.6 4.1 %mul.113 = f32[256,2,4,2,72]{4,3,2,1,0:T(2,128)S(1)} reshape(f32[2,16,8,1152]{3,2,1,0:T(8,128)S(1)} %mul.112) | data formatting | bytes 2359296 | tf_op jit(solution)/shard_map/mul | solution.py:191
  98.0 5.2 %add.57 = f32[256,2,4,2,72]{4,3,2,1,0:T(2,128)S(1)} reshape(f32[2,16,8,1152]{3,2,1,0:T(8,128)} %add.56) | data formatting | bytes 2359296 | tf_op jit(solution)/shard_map/add | solution.py:191
  103.2 2.6 copy.52
  106.4 13.1 %all-to-all-done = bf16[2,1,128,2,1152]{4,0,3,1,2:T(2,128)(2,1)} async-done(((bf16[2,1,128,2,1152]{4,0,3,1,2:T(2,128)(2,1)}), bf16[2,1,128,2,1152]{4,0,3,1,2:T(2,128)(2,1)}, u32[]{:S(2)}, u32[]{:S(2)}) %all-to-all-start) | async-done | bytes 1179680 | tf_op jit(solution)/shard_map/all_to_all | solution.py:179
  123.1 5.2 %reshape.139 = f32[256,2,4,2,72]{4,3,2,1,0:T(2,128)S(1)} reshape(f32[2,16,8,1,1152]{4,2,1,0,3:T(8,128)} %get-tuple-element.21) | data formatting | bytes 2359296 | tf_op jit(solution)/shard_map/convert_element_type | solution.py:182
  128.3 2.6 copy.50
  130.9 2.9 reshape.140
  136.9 7.1 %fusion = bf16[256,3456]{1,0:T(8,128)(2,1)} fusion(bf16[2,4,2,72,3456]{4,3,2,1,0:T(8,128)(2,1)} %bitcast.122, bf16[256,2,4,2,72]{0,4,1,2,3:T(8,128)(2,1)S(1)} %add_convert_fusion), kind=kOutput, calls=%fused_computation.4 | convolution fusion | flops 2039316480 | bytes 10321920 | tf_op jit(solution)/shard_map/dot_general | solution.py:195
  144.1 7.1 %reshape.129 = bf16[2,16,8,3,16,72]{5,4,3,2,1,0:T(8,128)(2,1)S(1)} reshape(bf16[256,3456]{1,0:T(8,128)(2,1)} %fusion) | data formatting | bytes 3538944 | tf_op jit(solution)/shard_map/reshape | solution.py:196
  163.8 4.6 %reshape.130 = bf16[256,3456]{1,0:T(8,128)(2,1)} reshape(bf16[2,16,8,3,16,72]{5,4,3,2,1,0:T(8,128)(2,1)S(1)} %copy.59) | data formatting | bytes 3538944 | tf_op jit(solution)/shard_map/reshape | solution.py:203
  168.4 7.2 %convolution_convert_fusion = bf16[1152,3456]{1,0:T(8,128)(2,1)} fusion(bf16[256,1152]{0,1:T(8,128)(2,1)} %bitcast.113, bf16[256,3456]{1,0:T(8,128)(2,1)} %reshape.130), kind=kOutput, calls=%fused_computation.2 | convolution fusion | flops 2042413056 | bytes 10321920 | tf_op jit(solution)/shard_map/dot_general | solution.py:205
  175.6 18.8 %reduce-scatter.7.cloned.1.call-done = bf16[1,576,3456]{2,1,0:T(8,128)(2,1)} async-done(((bf16[2,576,3456]{2,1,0:T(8,128)(2,1)}), bf16[1,576,3456]{2,1,0:T(8,128)(2,1)}) %reduce-scatter.7.cloned.1.call-update) | async-done | bytes 3981328 | tf_op jit(solution)/shard_map/reduce_scatter | solution.py:210
  194.5 4.6 %reshape.163 = bf16[256,3456,1,1,1]{1,0,2,3,4:T(8,128)(2,1)} reshape(bf16[2,16,8,3,16,72]{5,4,3,2,1,0:T(8,128)(2,1)S(1)} %copy.59) | data formatting | bytes 3538944 | tf_op jit(solution)/shard_map/reshape | solution.py:203
  199.1 45.1 %reduce-scatter.9.cloned.1.call-done = bf16[1,144,3456]{2,1,0:T(8,128)(2,1)} async-done(((bf16[4,144,3456]{2,1,0:T(8,128)(2,1)}), bf16[1,144,3456]{2,1,0:T(8,128)(2,1)}) %reduce-scatter.9.cloned.1.call-update) | async-done | bytes 995344 | tf_op jit(solution)/shard_map/reduce_scatter | solution.py:212
  244.2 5.9 %multiply_reduce_fusion.4 = (f32[256]{0:T(256)S(1)}, f32[256]{0:T(256)S(1)}, f32[256,2,4,2,72]{0,4,1,2,3:T(8,128)S(1)}) fusion(f32[256,2,4,2,72]{0,4,1,2,3:T(8,128)} %copy-done.4, f32[256]{0:T(256)S(1)} %rsqrt.13, f32[256,2,4,2,72]{0,4,1,2,3:T(8,128)} %copy.50, f32[256]{0:T(256)S(1)} %div.27, bf16[2,4,2,72,3456]{4,3,2,1,0:T(8,128)(2,1)} %bitcast.123, ...), kind=kOutput, calls=%fused_computation.43 | convolution fusion | flops 2040200704 | bytes 13275136 | tf_op jit(solution)/shard_map/dot_general | solution.py:216
  251.9 4.4 %reshape.131 = f32[2,16,8,1152]{3,2,1,0:T(8,128)} reshape(f32[256,2,4,2,72]{4,3,2,1,0:T(2,128)S(1)} %copy.60) | data formatting | bytes 2359296 | tf_op jit(solution)/shard_map/reshape | solution.py:220
  259.1 9.8 %all-to-all-start.1 = ((bf16[2,16,8,1152]{3,2,0,1:T(8,128)(2,1)}), bf16[2,16,8,1152]{3,2,0,1:T(8,128)(2,1)S(1)}, u32[]{:S(2)}, u32[]{:S(2)}) async-start(bf16[2,16,8,1152]{3,2,0,1:T(8,128)(2,1)} %copy.62), calls=%async_computation.1 | async-start | bytes 1179648 | tf_op jit(solution)/shard_map/all_to_all | solution.py:236
  269.6 19.9 %all-to-all-done.1 = bf16[2,16,8,1152]{3,2,0,1:T(8,128)(2,1)S(1)} async-done(((bf16[2,16,8,1152]{3,2,0,1:T(8,128)(2,1)}), bf16[2,16,8,1152]{3,2,0,1:T(8,128)(2,1)S(1)}, u32[]{:S(2)}, u32[]{:S(2)}) %all-to-all-start.1) | async-done | bytes 589856 | tf_op jit(solution)/shard_map/all_to_all | solution.py:236
  290.3 2.8 reshape.137
  294.1 56.9 %shard_map.94 = (f32[16,72,216]{2,1,0:T(8,128)}, f32[4,1152]{1,0:T(4,128)}) custom-call(bf16[16,72,216]{2,1,0:T(8,128)(2,1)} %bitcast.114, f32[4,1152]{1,0:T(4,128)} %reshape.138.sums_ref), custom_call_target="tpu_custom_call" | custom-call | tf_op jit(solution)/shard_map/pallas_call | solution.py:139
  (91 shorter events, 38.8 us)
Async XLA Ops:
  7.2 98.6 %copy-start = (f32[1000]{0:T(1024)S(1)}, f32[1000]{0:T(1024)}, u32[]{:S(2)}) copy-start(f32[1000]{0:T(1024)} %param.11) | copy-start | bytes 12004
  7.2 65.5 %all-gather.6.cloned.1.call-start = ((), (), s32[]{:S(2)}) async-start(), calls=%async_computation.7 | async-start | bytes 4976640 | tf_op jit(solution)/shard_map/all_gather | solution.py:169
  23.3 49.4 %copy-start.9 = (bf16[2,1,2,64,1152]{4,3,2,1,0:T(8,128)(2,1)S(1)}, bf16[2,1,2,64,1152]{4,3,2,1,0:T(8,128)(2,1)}, u32[]{:S(2)}) copy-start(bf16[2,1,2,64,1152]{4,3,2,1,0:T(8,128)(2,1)} %param.7) | copy-start | bytes 1769476
  23.3 112.9 %all-gather.8.cloned.1.call-start = ((), (), s32[]{:S(2)}) async-start(), calls=%async_computation.8 | async-start | bytes 11943936 | tf_op jit(solution)/shard_map/all_gather | solution.py:170
  72.6 1.1 copy-start.10
  74.3 12.5 %copy-start.12 = (s32[2]{0:T(128)S(1)}, s32[2]{0:T(128)}, u32[]{:S(2)}) copy-start(s32[2]{0:T(128)} %param.12) | copy-start | bytes 28
  76.9 42.6 %all-to-all-start = ((bf16[2,1,128,2,1152]{4,0,3,1,2:T(2,128)(2,1)}), bf16[2,1,128,2,1152]{4,0,3,1,2:T(2,128)(2,1)}, u32[]{:S(2)}, u32[]{:S(2)}) async-start(bf16[2,1,128,2,1152]{4,0,3,1,2:T(2,128)(2,1)} %pad_maximum_fusion.1), calls=%async_computation | async-start | bytes 2359296 | tf_op jit(solution)/shard_map/all_to_all | solution.py:179
  86.7 107.7 %reduce-scatter.7.cloned.1.call-start = ((), (), s32[]{:S(2)}) async-start(), calls=%async_computation.5 | async-start | bytes 11943936 | tf_op jit(solution)/shard_map/reduce_scatter | solution.py:210
  96.7 38.4 %copy-start.4 = (f32[256,2,4,2,72]{0,4,1,2,3:T(8,128)}, f32[256,2,4,2,72]{0,4,1,2,3:T(8,128)S(1)}, u32[]{:S(2)}) copy-start(f32[256,2,4,2,72]{0,4,1,2,3:T(8,128)S(1)} %copy.51) | copy-start | bytes 3538948
  103.2 2.6 copy-start.13
  120.9 2.2 copy-start.2
  133.8 1.3 copy-start.5
  133.8 2.0 copy-start.6
  136.1 0.8 copy-start.7
  151.8 1.7 copy-start.8
  175.5 68.7 %reduce-scatter.9.cloned.1.call-start = ((), (), s32[]{:S(2)}) async-start(), calls=%async_computation.6 | async-start | bytes 4976640 | tf_op jit(solution)/shard_map/reduce_scatter | solution.py:212
  194.5 95.9 %reduce-scatter.11.cloned.1.call-start = ((), (), s32[]{:S(2)}) async-start(), calls=%async_computation.9 | async-start | bytes 1492992
  251.9 4.4 %copy-start.3 = (bf16[2,1,128,2,1152]{4,2,0,3,1:T(8,128)(2,1)S(1)}, bf16[2,1,128,2,1152]{4,2,0,3,1:T(8,128)(2,1)}, u32[]{:S(2)}) copy-start(bf16[2,1,128,2,1152]{4,2,0,3,1:T(8,128)(2,1)} %copy-done.2) | copy-start | bytes 3538948
  259.1 30.4 %all-to-all-start.1 = ((bf16[2,16,8,1152]{3,2,0,1:T(8,128)(2,1)}), bf16[2,16,8,1152]{3,2,0,1:T(8,128)(2,1)S(1)}, u32[]{:S(2)}, u32[]{:S(2)}) async-start(bf16[2,16,8,1152]{3,2,0,1:T(8,128)(2,1)} %copy.62), calls=%async_computation.1 | async-start | bytes 1179648 | tf_op jit(solution)/shard_map/all_to_all | solution.py:236
  351.0 4.1 %copy-start.1 = (f32[1000]{0:T(1024)S(1)}, f32[1000]{0:T(1024)}, u32[]{:S(2)}) copy-start(f32[1000]{0:T(1024)} %param.11) | copy-start | bytes 12004
  352.4 2.0 copy-start.11
Sparse Core Ops, SparseCore 0:
  23.4 49.2 all-gather.5
  74.4 26.7 all-gather.7
  175.7 18.7 reduce-scatter.6
  197.0 47.1 reduce-scatter.8
  246.6 32.7 reduce-scatter.10

commit v4 on v1

--- a/solution.py
+++ b/solution.py
@@ -1,7 +1,13 @@
+import functools
+
 import jax
 import jax.numpy as jnp
 from jax import lax
+from jax.experimental import pallas as pl
+from jax.experimental.pallas import tpu as pltpu
 from jax.sharding import PartitionSpec as P
+
+MESH = pl.DeviceIdType.MESH
 
 HEADS = 16
 HEAD_DIM = 72
@@ -27,6 +33,121 @@
         grad_keys.astype(jnp.bfloat16),
         grad_values.astype(jnp.bfloat16),
     )
+
+
+def barrier_with(peers):
+    barrier = pltpu.get_barrier_semaphore()
+    for p in peers:
+        pl.semaphore_signal(barrier, inc=1, device_id=p, device_id_type=MESH)
+    pl.semaphore_wait(barrier, len(peers))
+
+
+def exchange(src_ref, dst, peer_of, index_of, count, send_sem, recv_sem):
+    sends = []
+    for k in range(1, count):
+        t = lax.rem(index_of + k, count)
+        c = pltpu.make_async_remote_copy(
+            src_ref=src_ref(t), dst_ref=dst.at[index_of], send_sem=send_sem.at[k],
+            recv_sem=recv_sem.at[index_of], device_id=peer_of(t), device_id_type=MESH,
+        )
+        c.start()
+        sends.append(c)
+    return sends
+
+
+def wait_all(src_ref, dst, peer_of, index_of, count, send_sem, recv_sem, sends):
+    for k in range(1, count):
+        src = lax.rem(index_of + count - k, count)
+        pltpu.make_async_remote_copy(
+            src_ref=src_ref(0), dst_ref=dst.at[src], send_sem=send_sem.at[k],
+            recv_sem=recv_sem.at[src], device_id=peer_of(src), device_id_type=MESH,
+        ).wait_recv()
+    for c in sends:
+        c.wait_send()
+
+
+def weight_kernel(nf, chunks_ref, gw_ref, recv1, redbuf, recv2, s1, r1, s2, r2):
+    me_f = lax.axis_index("frame")
+    me_s = lax.axis_index("space")
+    peer = lambda t: (t, me_s)
+    barrier_with([peer(lax.rem(me_f + k, nf)) for k in range(1, nf)])
+    first = lambda t: chunks_ref.at[t]
+    sends = exchange(first, recv1, peer, me_f, nf, s1, r1)
+    recv1[me_f] = chunks_ref[me_f]
+    wait_all(first, recv1, peer, me_f, nf, s1, r1, sends)
+    acc = recv1[0].astype(jnp.float32)
+    for j in range(1, nf):
+        acc = acc + recv1[j].astype(jnp.float32)
+    acc = acc.astype(redbuf.dtype)
+    redbuf[...] = acc
+    recv2[me_f] = acc
+    second = lambda t: redbuf
+    sends = exchange(second, recv2, peer, me_f, nf, s2, r2)
+    wait_all(second, recv2, peer, me_f, nf, s2, r2, sends)
+    gw_ref[...] = recv2[...]
+
+
+def sums_kernel(nf, ns, sums_ref, gm_ref, msum1, mbuf, msum2, s1, r1, s2, r2):
+    me_f = lax.axis_index("frame")
+    me_s = lax.axis_index("space")
+    fpeer = lambda t: (t, me_s)
+    speer = lambda t: (me_f, t)
+    barrier_with(
+        [fpeer(lax.rem(me_f + k, nf)) for k in range(1, nf)]
+        + [speer(lax.rem(me_s + k, ns)) for k in range(1, ns)]
+    )
+    first = lambda t: sums_ref
+    sends = exchange(first, msum1, fpeer, me_f, nf, s1, r1)
+    msum1[me_f] = sums_ref[...]
+    wait_all(first, msum1, fpeer, me_f, nf, s1, r1, sends)
+    macc = msum1[0]
+    for j in range(1, nf):
+        macc = macc + msum1[j]
+    mbuf[...] = macc
+    msum2[me_s] = macc
+    second = lambda t: mbuf
+    sends = exchange(second, msum2, speer, me_s, ns, s2, r2)
+    wait_all(second, msum2, speer, me_s, ns, s2, r2, sends)
+    total = msum2[0]
+    for j in range(1, ns):
+        total = total + msum2[j]
+    gm_ref[...] = total
+
+
+def reduce_weight(chunks, nf):
+    count, rows, cols = chunks.shape
+    vmem = pl.BlockSpec(memory_space=pltpu.VMEM)
+    return pl.pallas_call(
+        functools.partial(weight_kernel, nf),
+        out_shape=jax.ShapeDtypeStruct((count, rows, cols), chunks.dtype),
+        in_specs=[vmem],
+        out_specs=vmem,
+        scratch_shapes=[
+            pltpu.VMEM((nf, rows, cols), chunks.dtype),
+            pltpu.VMEM((rows, cols), chunks.dtype),
+            pltpu.VMEM((nf, rows, cols), chunks.dtype),
+        ]
+        + [pltpu.SemaphoreType.DMA((nf,))] * 4,
+        compiler_params=pltpu.CompilerParams(collective_id=0, has_side_effects=True),
+    )(chunks)
+
+
+def reduce_sums(sums, nf, ns):
+    vmem = pl.BlockSpec(memory_space=pltpu.VMEM)
+    return pl.pallas_call(
+        functools.partial(sums_kernel, nf, ns),
+        out_shape=jax.ShapeDtypeStruct(sums.shape, jnp.float32),
+        in_specs=[vmem],
+        out_specs=vmem,
+        scratch_shapes=[
+            pltpu.VMEM((nf,) + sums.shape, jnp.float32),
+            pltpu.VMEM(sums.shape, jnp.float32),
+            pltpu.VMEM((ns,) + sums.shape, jnp.float32),
+        ]
+        + [pltpu.SemaphoreType.DMA((nf,)), pltpu.SemaphoreType.DMA((nf,))]
+        + [pltpu.SemaphoreType.DMA((ns,)), pltpu.SemaphoreType.DMA((ns,))],
+        compiler_params=pltpu.CompilerParams(collective_id=1, has_side_effects=True),
+    )(sums)
 
 
 def per_device(
@@ -73,11 +194,8 @@
     ).astype(jnp.bfloat16)
     col_blk = 3 * model_width // frame_n
     share = lax.psum_scatter(term, "space", scatter_dimension=0, tiled=True)
-    share = share.reshape(share.shape[0], frame_n, col_blk)
-    share = lax.psum_scatter(share, "frame", scatter_dimension=1, tiled=True)
-    grad_weight = lax.all_gather(share, "frame", axis=1, tiled=True)
-    grad_weight = grad_weight.reshape(share.shape[0], 3 * model_width)
-    grad_weight = grad_weight.astype(jnp.float32) * grad_scale_factor
+    row_blk = share.shape[0]
+    share = share.reshape(row_blk, frame_n, col_blk).transpose(1, 0, 2)
     grad_hidden = lax.dot_general(
         grad_rows, w_full, (((1,), (1,)), ((), ())), preferred_element_type=jnp.float32
     )
@@ -86,7 +204,11 @@
         [jnp.sum(grad_hidden, axis=(1, 2)), jnp.sum(grad_hidden * normed, axis=(1, 2))],
         axis=1,
     )
-    grad_modulation = lax.psum(local_sums, ("frame", "space")) * grad_scale_factor
+    local_sums = local_sums.reshape(-1, model_width)
+    gm = reduce_sums(local_sums, frame_n, space_n)
+    gw = reduce_weight(share, frame_n).astype(jnp.float32)
+    grad_weight = gw.transpose(1, 0, 2).reshape(row_blk, 3 * model_width) * grad_scale_factor
+    grad_modulation = gm.reshape(clip_count, 2, model_width) * grad_scale_factor
     grad_normed = grad_hidden * (1.0 + scale)
     grad_input = (
         grad_normed

time: 376 us -> 295 us (0.78)
  blocking collectives: 127 us -> 0 us
  Pallas kernels: 0 us -> 81.2 us
  waiting for transfers between devices: 141 us -> 102 us
    pallas_call x0 -> x2, Pallas kernels: none -> 81.2 us  [the longest x1 46 us: reduce_weight(): pl.pallas_call(functools.partial(weight_kernel, nf), out_shape=jax.ShapeD...]
    psum x1 -> x0, blocking collectives: 80.8 us -> none  [per_device(): lax.psum(local_sums, ('frame', 'space')) * grad_scale_factor]
    all_gather x1 -> x0, blocking collectives: 46.2 us -> none  [per_device(): grad_weight = lax.all_gather(share, 'frame', axis=1, tiled=True)]
    unnamed x4 -> x3, waiting for transfers between devices: 75.7 us -> 44 us
    reduce_scatter x1 -> x0, waiting for transfers between devices: 8.11 us -> none  [per_device(): share = lax.psum_scatter(share, 'frame', scatter_dimension=1, tiled=True)]
  transfers between devices with their start and end apart: 5 -> 4, of which waited for: 4 -> 3; matrix products, arithmetic and copies ran while one was open for 5% -> 6% of each run, Pallas kernels for 0% -> 12%
where the time goes in v4:
time: 295 us; the launch traced here: 293 us
  waiting for transfers between devices  102 us (35%)
  Pallas kernels  81.2 us (28%)
  local copies, waits for them, and re-layouts  38.4 us (13%)
  matrix products  30.6 us (10%)
  starting transfers between devices  20 us (7%)
  between operations  14.4 us (5%)
  other arithmetic  6.62 us (2%)
    pallas_call x1, Pallas kernels, reduce_weight(): pl.pallas_call(functools.partial(weight_kernel, nf), out_shape=jax.ShapeD...  46 us
    unnamed x3, waiting for transfers between devices  44 us
    all_to_all x1, waiting for transfers between devices, per_device(): lax.all_to_all(both, 'frame', split_axis=2, concat_axis=1, tiled=True)  41.8 us
    pallas_call x1, Pallas kernels, reduce_sums(): pl.pallas_call(functools.partial(sums_kernel, nf, ns), out_shape=jax.Shap...  35.2 us
    all_gather x1, waiting for transfers between devices, per_device(): w_full = lax.all_gather(w_qkv, 'space', axis=0, tiled=True)  15.8 us
    all_to_all x1, starting transfers between devices, per_device(): lax.all_to_all(both, 'frame', split_axis=2, concat_axis=1, tiled=True)  11.2 us
    all_to_all x1, starting transfers between devices, per_device(): lax.all_to_all(grad_input, 'frame', split_axis=1, concat_axis=2, tiled=True)  8.67 us
    reshape x1, local copies, waits for them, and re-layouts, per_device(): pieces = projected.reshape(clip_count, frames, across, 3, HEADS, HEAD_DIM)  7.1 us
  transfers between devices with their start and end apart: 4, of which 3 were waited for; matrix products, arithmetic and copies ran while one was open for 6% of the time, Pallas kernels for 12%

profile of v4, /device:TPU:6, one launch (start us, length us, event | category | flops | bytes accessed | tf_op | source)
XLA Modules:
  0.0 292.7 jit_solution(8289335157304519728)
XLA Ops:
  7.9 1.7 copy.39
  9.6 1.7 copy.40
  11.3 2.7 pad_maximum_fusion.1
  13.9 11.2 %all-to-all-start = ((bf16[2,1,128,2,1152]{4,0,3,1,2:T(2,128)(2,1)}), bf16[2,1,128,2,1152]{4,0,3,1,2:T(2,128)(2,1)S(1)}, u32[]{:S(2)}, u32[]{:S(2)}) async-start(bf16[2,1,128,2,1152]{4,0,3,1,2:T(2,128)(2,1)} %pad_maximum_fusion.1), calls=%async_computation | async-start | bytes 2359296 | tf_op jit(solution)/shard_map/all_to_all | solution.py:168
  25.2 2.9 gather_fusion
  28.9 41.8 %all-to-all-done = bf16[2,1,128,2,1152]{4,0,3,1,2:T(2,128)(2,1)S(1)} async-done(((bf16[2,1,128,2,1152]{4,0,3,1,2:T(2,128)(2,1)}), bf16[2,1,128,2,1152]{4,0,3,1,2:T(2,128)(2,1)S(1)}, u32[]{:S(2)}, u32[]{:S(2)}) %all-to-all-start) | async-done | bytes 1179680 | tf_op jit(solution)/shard_map/all_to_all | solution.py:168
  71.5 3.1 %reshape.163 = f32[2,16,8,16,72]{4,3,2,1,0:T(8,128)} reshape(f32[2,16,8,1,1152]{4,2,1,0,3:T(8,128)S(1)} %slice_convert_fusion) | data formatting | bytes 2359296 | tf_op jit(solution)/shard_map/convert_element_type | solution.py:186
  75.0 15.8 %all-gather.2.cloned.1.call-done = bf16[1152,3456]{1,0:T(8,128)(2,1)} async-done(((bf16[72,3456]{1,0:T(8,128)(2,1)}), bf16[1152,3456]{1,0:T(8,128)(2,1)}) %all-gather.2.cloned.1.call-update) | async-done | bytes 7962640 | tf_op jit(solution)/shard_map/all_gather | solution.py:160
  90.8 7.0 %convolution_convert_fusion.1 = bf16[256,3456]{1,0:T(8,128)(2,1)} fusion(bf16[256,1152]{1,0:T(8,128)(2,1)S(1)} %fusion.8, bf16[1152,3456]{1,0:T(8,128)(2,1)} %all-gather.2.cloned.1.call-done), kind=kOutput, calls=%fused_computation.5 | convolution fusion | flops 2039316480 | bytes 10321920 | tf_op jit(solution)/shard_map/dot_general | solution.py:182
  97.8 7.1 %reshape.157 = bf16[2,16,8,3,16,72]{5,4,3,2,1,0:T(8,128)(2,1)S(1)} reshape(bf16[256,3456]{1,0:T(8,128)(2,1)} %convolution_convert_fusion.1) | data formatting | bytes 3538944 | tf_op jit(solution)/shard_map/reshape | solution.py:183
  105.9 1.7 fusion.4
  107.6 2.3 multiply_reduce_fusion
  109.9 2.4 fusion.6
  112.3 2.2 fusion.7
  114.5 2.8 fusion.5
  118.9 4.6 %dot_general.32 = bf16[2,16,8,3456]{3,2,1,0:T(8,128)(2,1)} reshape(bf16[2,16,8,3,16,72]{5,4,3,2,1,0:T(8,128)(2,1)S(1)} %copy.47) | data formatting | bytes 3538944 | tf_op jit(solution)/shard_map/dot_general | solution.py:199
  123.5 4.6 %reshape.159 = bf16[256,3456]{1,0:T(8,128)(2,1)} reshape(bf16[2,16,8,3,16,72]{5,4,3,2,1,0:T(8,128)(2,1)S(1)} %copy.47) | data formatting | bytes 3538944 | tf_op jit(solution)/shard_map/reshape | solution.py:190
  128.1 6.7 %multiply_reduce_fusion.1 = (f32[2,1152]{1,0:T(2,128)S(1)}, f32[2,16,8]{2,1,0:T(8,128)S(1)}, f32[2,16,8]{2,1,0:T(8,128)S(1)}, f32[2,1152]{1,0:T(2,128)S(1)}, bf1...) fusion(f32[2,16,8]{2,1,0:T(8,128)S(1)} %add_rsqrt_fusion, ...), kind=kOutput, calls=%fused_computation.28 | convolution fusion | flops 2042260480 | bytes 12132352 | tf_op jit(solution)/shard_map/dot_general | solution.py:199
  134.8 5.4 %convolution_convert_fusion = bf16[1152,3456]{1,0:T(8,128)(2,1)} fusion(bf16[256,1152]{1,0:T(8,128)(2,1)S(1)} %bitcast.105, bf16[256,3456]{1,0:T(8,128)(2,1)S(1)} %copy-done.3), kind=kOutput, calls=%fused_computation.2 | convolution fusion | flops 2042413056 | bytes 10321920 | tf_op jit(solution)/shard_map/dot_general | solution.py:192
  142.8 8.7 %all-to-all-start.1 = ((bf16[2,16,8,1152]{3,2,0,1:T(8,128)(2,1)}), bf16[2,16,8,1152]{3,2,0,1:T(8,128)(2,1)S(1)}, u32[]{:S(2)}, u32[]{:S(2)}) async-start(bf16[2,16,8,1152]{3,2,0,1:T(8,128)(2,1)} %copy.48), calls=%async_computation.1 | async-start | bytes 1179648 | tf_op jit(solution)/shard_map/all_to_all | solution.py:219
  152.2 35.2 %shard_map.95 = f32[4,1152]{1,0:T(4,128)} custom-call(f32[4,1152]{1,0:T(4,128)} %reshape.161.sums_ref), custom_call_target="tpu_custom_call" | custom-call | tf_op jit(solution)/shard_map/pallas_call | solution.py:137
  189.6 43.3 %reduce-scatter.5.cloned.1.call-done = bf16[72,3456]{1,0:T(8,128)(2,1)} async-done(((bf16[1152,3456]{1,0:T(8,128)(2,1)}), bf16[72,3456]{1,0:T(8,128)(2,1)}) %reduce-scatter.5.cloned.1.call-update) | async-done | bytes 497680
  232.9 2.8 reshape.160
  236.7 46.0 %shard_map.94 = bf16[16,72,216]{2,1,0:T(8,128)(2,1)} custom-call(bf16[16,72,216]{2,1,0:T(8,128)(2,1)} %bitcast.102), custom_call_target="tpu_custom_call" | custom-call | tf_op jit(solution)/shard_map/pallas_call | solution.py:120
  (55 shorter events, 14.7 us)
Async XLA Ops:
  7.2 21.0 %copy-start = (f32[1000]{0:T(1024)S(1)}, f32[1000]{0:T(1024)}, u32[]{:S(2)}) copy-start(f32[1000]{0:T(1024)} %param.11) | copy-start | bytes 12004
  7.2 83.6 %all-gather.2.cloned.1.call-start = ((), (), s32[]{:S(2)}) async-start(), calls=%async_computation.3 | async-start | bytes 8460288 | tf_op jit(solution)/shard_map/all_gather | solution.py:160
  11.3 13.9 %copy-start.5 = (s32[2]{0:T(128)S(1)}, s32[2]{0:T(128)}, u32[]{:S(2)}) copy-start(s32[2]{0:T(128)} %param.12) | copy-start | bytes 28
  11.3 16.9 %copy-start.6 = (s32[2]{0:T(128)S(1)}, s32[2]{0:T(128)}, u32[]{:S(2)}) copy-start(s32[2]{0:T(128)} %param.13) | copy-start | bytes 28
  13.9 56.7 %all-to-all-start = ((bf16[2,1,128,2,1152]{4,0,3,1,2:T(2,128)(2,1)}), bf16[2,1,128,2,1152]{4,0,3,1,2:T(2,128)(2,1)S(1)}, u32[]{:S(2)}, u32[]{:S(2)}) async-start(bf16[2,1,128,2,1152]{4,0,3,1,2:T(2,128)(2,1)} %pad_maximum_fusion.1), calls=%async_computation | async-start | bytes 2359296 | tf_op jit(solution)/shard_map/all_to_all | solution.py:168
  25.2 207.8 %reduce-scatter.5.cloned.1.call-start = ((), (), s32[]{:S(2)}) async-start(), calls=%async_computation.4 | async-start | bytes 8460288
  70.8 3.9 %copy-start.1 = (bf16[2,1,128,2,1152]{4,2,0,3,1:T(8,128)(2,1)}, bf16[2,1,128,2,1152]{4,2,0,3,1:T(8,128)(2,1)S(1)}, u32[]{:S(2)}) copy-start(bf16[2,1,128,2,1152]{4,2,0,3,1:T(8,128)(2,1)S(1)} %copy.86) | copy-start | bytes 3538948
  105.9 1.7 copy-start.4
  128.1 6.7 %copy-start.3 = (bf16[256,3456]{1,0:T(8,128)(2,1)S(1)}, bf16[256,3456]{1,0:T(8,128)(2,1)}, u32[]{:S(2)}) copy-start(bf16[256,3456]{1,0:T(8,128)(2,1)} %reshape.159) | copy-start | bytes 5308420
  140.3 1.3 copy-start.2
  142.8 45.9 %all-to-all-start.1 = ((bf16[2,16,8,1152]{3,2,0,1:T(8,128)(2,1)}), bf16[2,16,8,1152]{3,2,0,1:T(8,128)(2,1)S(1)}, u32[]{:S(2)}, u32[]{:S(2)}) async-start(bf16[2,16,8,1152]{3,2,0,1:T(8,128)(2,1)} %copy.48), calls=%async_computation.1 | async-start | bytes 1179648 | tf_op jit(solution)/shard_map/all_to_all | solution.py:219
Sparse Core Ops, SparseCore 0:
  9.9 80.8 all-gather.1
  140.4 92.4 reduce-scatter.4

commit v5 on v4

--- a/solution.py
+++ b/solution.py
@@ -8,6 +8,7 @@
 from jax.sharding import PartitionSpec as P
 
 MESH = pl.DeviceIdType.MESH
+FRAME_SUB = (4, 4)
 
 HEADS = 16
 HEAD_DIM = 72
@@ -66,25 +67,44 @@
         c.wait_send()
 
 
-def weight_kernel(nf, chunks_ref, gw_ref, recv1, redbuf, recv2, s1, r1, s2, r2):
+def weight_kernel(
+    nzh, ny, chunks_ref, out_ref, a_recv, partbuf, b_recv, redbuf, c_recv, sems
+):
     me_f = lax.axis_index("frame")
     me_s = lax.axis_index("space")
-    peer = lambda t: (t, me_s)
-    barrier_with([peer(lax.rem(me_f + k, nf)) for k in range(1, nf)])
+    my_y = lax.rem(me_f, ny)
+    my_z = me_f // ny
+    ypeer = lambda t: (my_z * ny + t, me_s)
+    zpeer = lambda t: (t * ny + my_y, me_s)
+    barrier_with(
+        [ypeer(lax.rem(my_y + k, ny)) for k in range(1, ny)]
+        + [zpeer(lax.rem(my_z + k, nzh)) for k in range(1, nzh)]
+    )
+    s = [sems.at[i] for i in range(8)]
     first = lambda t: chunks_ref.at[t]
-    sends = exchange(first, recv1, peer, me_f, nf, s1, r1)
-    recv1[me_f] = chunks_ref[me_f]
-    wait_all(first, recv1, peer, me_f, nf, s1, r1, sends)
-    acc = recv1[0].astype(jnp.float32)
-    for j in range(1, nf):
-        acc = acc + recv1[j].astype(jnp.float32)
-    acc = acc.astype(redbuf.dtype)
-    redbuf[...] = acc
-    recv2[me_f] = acc
-    second = lambda t: redbuf
-    sends = exchange(second, recv2, peer, me_f, nf, s2, r2)
-    wait_all(second, recv2, peer, me_f, nf, s2, r2, sends)
-    gw_ref[...] = recv2[...]
+    sends = exchange(first, a_recv, ypeer, my_y, ny, s[0], s[1])
+    a_recv[my_y] = chunks_ref[my_y]
+    wait_all(first, a_recv, ypeer, my_y, ny, s[0], s[1], sends)
+    part = a_recv[0].astype(jnp.float32)
+    for j in range(1, ny):
+        part = part + a_recv[j].astype(jnp.float32)
+    partbuf[...] = part
+    second = lambda t: partbuf.at[t]
+    sends = exchange(second, b_recv, zpeer, my_z, nzh, s[2], s[3])
+    b_recv[my_z] = partbuf[my_z]
+    wait_all(second, b_recv, zpeer, my_z, nzh, s[2], s[3], sends)
+    red = b_recv[0]
+    for j in range(1, nzh):
+        red = red + b_recv[j]
+    redbuf[...] = red
+    third = lambda t: redbuf
+    sends = exchange(third, c_recv, zpeer, my_z, nzh, s[4], s[5])
+    c_recv[my_z] = red
+    wait_all(third, c_recv, zpeer, my_z, nzh, s[4], s[5], sends)
+    fourth = lambda t: c_recv
+    sends = exchange(fourth, out_ref, ypeer, my_y, ny, s[6], s[7])
+    out_ref[my_y] = c_recv[...]
+    wait_all(fourth, out_ref, ypeer, my_y, ny, s[6], s[7], sends)
 
 
 def sums_kernel(nf, ns, sums_ref, gm_ref, msum1, mbuf, msum2, s1, r1, s2, r2):
@@ -114,20 +134,22 @@
     gm_ref[...] = total
 
 
-def reduce_weight(chunks, nf):
-    count, rows, cols = chunks.shape
+def reduce_weight(chunks, nzh, ny):
+    rows, cols = chunks.shape[2:]
     vmem = pl.BlockSpec(memory_space=pltpu.VMEM)
     return pl.pallas_call(
-        functools.partial(weight_kernel, nf),
-        out_shape=jax.ShapeDtypeStruct((count, rows, cols), chunks.dtype),
+        functools.partial(weight_kernel, nzh, ny),
+        out_shape=jax.ShapeDtypeStruct((ny, nzh, rows, cols), jnp.float32),
         in_specs=[vmem],
         out_specs=vmem,
         scratch_shapes=[
-            pltpu.VMEM((nf, rows, cols), chunks.dtype),
-            pltpu.VMEM((rows, cols), chunks.dtype),
-            pltpu.VMEM((nf, rows, cols), chunks.dtype),
-        ]
-        + [pltpu.SemaphoreType.DMA((nf,))] * 4,
+            pltpu.VMEM((ny, nzh, rows, cols), chunks.dtype),
+            pltpu.VMEM((nzh, rows, cols), jnp.float32),
+            pltpu.VMEM((nzh, rows, cols), jnp.float32),
+            pltpu.VMEM((rows, cols), jnp.float32),
+            pltpu.VMEM((nzh, rows, cols), jnp.float32),
+            pltpu.SemaphoreType.DMA((8, max(nzh, ny))),
+        ],
         compiler_params=pltpu.CompilerParams(collective_id=0, has_side_effects=True),
     )(chunks)
 
@@ -195,7 +217,8 @@
     col_blk = 3 * model_width // frame_n
     share = lax.psum_scatter(term, "space", scatter_dimension=0, tiled=True)
     row_blk = share.shape[0]
-    share = share.reshape(row_blk, frame_n, col_blk).transpose(1, 0, 2)
+    nzh, ny = FRAME_SUB
+    share = share.reshape(row_blk, nzh, ny, col_blk).transpose(2, 1, 0, 3)
     grad_hidden = lax.dot_general(
         grad_rows, w_full, (((1,), (1,)), ((), ())), preferred_element_type=jnp.float32
     )
@@ -206,8 +229,8 @@
     )
     local_sums = local_sums.reshape(-1, model_width)
     gm = reduce_sums(local_sums, frame_n, space_n)
-    gw = reduce_weight(share, frame_n).astype(jnp.float32)
-    grad_weight = gw.transpose(1, 0, 2).reshape(row_blk, 3 * model_width) * grad_scale_factor
+    gw = reduce_weight(share, nzh, ny)
+    grad_weight = gw.transpose(2, 1, 0, 3).reshape(row_blk, 3 * model_width) * grad_scale_factor
     grad_modulation = gm.reshape(clip_count, 2, model_width) * grad_scale_factor
     grad_normed = grad_hidden * (1.0 + scale)
     grad_input = (

time: 295 us -> 301 us (1.020)
  Pallas kernels: 81.2 us -> 88.1 us
    pallas_call x1, Pallas kernels: 46 us -> 52.9 us  [reduce_weight(): pl.pallas_call(functools.partial(weight_kernel, nzh, ny), out_shape=jax.S...]
where the time goes in v5:
time: 301 us
  waiting for transfers between devices  102 us (34%)
  Pallas kernels  88.1 us (29%)
  local copies, waits for them, and re-layouts  39.2 us (13%)
  matrix products  30.6 us (10%)
  starting transfers between devices  20 us (7%)
  between operations  14.4 us (5%)
  other arithmetic  6.83 us (2%)
    pallas_call x1, Pallas kernels, reduce_weight(): pl.pallas_call(functools.partial(weight_kernel, nzh, ny), out_shape=jax.S...  52.9 us
    unnamed x3, waiting for transfers between devices  44 us
    all_to_all x1, waiting for transfers between devices, per_device(): lax.all_to_all(both, 'frame', split_axis=2, concat_axis=1, tiled=True)  41.8 us
    pallas_call x1, Pallas kernels, reduce_sums(): pl.pallas_call(functools.partial(sums_kernel, nf, ns), out_shape=jax.Shap...  35.2 us
    all_gather x1, waiting for transfers between devices, per_device(): w_full = lax.all_gather(w_qkv, 'space', axis=0, tiled=True)  15.8 us
    all_to_all x1, starting transfers between devices, per_device(): lax.all_to_all(both, 'frame', split_axis=2, concat_axis=1, tiled=True)  11.2 us
    all_to_all x1, starting transfers between devices, per_device(): lax.all_to_all(grad_input, 'frame', split_axis=1, concat_axis=2, tiled=True)  8.67 us
    reshape x1, local copies, waits for them, and re-layouts, per_device(): pieces = projected.reshape(clip_count, frames, across, 3, HEADS, HEAD_DIM)  7.1 us
  transfers between devices with their start and end apart: 4, of which 3 were waited for; matrix products, arithmetic and copies ran while one was open for 6% of the time, Pallas kernels for 12%

profile of v5, /device:TPU:6, one launch (start us, length us, event | category | flops | bytes accessed | tf_op | source)
XLA Modules:
  0.0 300.6 jit_solution(3717851414330398555)
XLA Ops:
  9.6 1.7 copy.40
  11.3 2.7 pad_maximum_fusion.1
  13.9 11.2 %all-to-all-start = ((bf16[2,1,128,2,1152]{4,0,3,1,2:T(2,128)(2,1)}), bf16[2,1,128,2,1152]{4,0,3,1,2:T(2,128)(2,1)S(1)}, u32[]{:S(2)}, u32[]{:S(2)}) async-start(bf16[2,1,128,2,1152]{4,0,3,1,2:T(2,128)(2,1)} %pad_maximum_fusion.1), calls=%async_computation | async-start | bytes 2359296 | tf_op jit(solution)/shard_map/all_to_all | solution.py:190
  25.2 2.9 gather_fusion
  28.9 41.8 %all-to-all-done = bf16[2,1,128,2,1152]{4,0,3,1,2:T(2,128)(2,1)S(1)} async-done(((bf16[2,1,128,2,1152]{4,0,3,1,2:T(2,128)(2,1)}), bf16[2,1,128,2,1152]{4,0,3,1,2:T(2,128)(2,1)S(1)}, u32[]{:S(2)}, u32[]{:S(2)}) %all-to-all-start) | async-done | bytes 1179680 | tf_op jit(solution)/shard_map/all_to_all | solution.py:190
  71.5 3.1 %reshape.163 = f32[2,16,8,16,72]{4,3,2,1,0:T(8,128)} reshape(f32[2,16,8,1,1152]{4,2,1,0,3:T(8,128)S(1)} %slice_convert_fusion) | data formatting | bytes 2359296 | tf_op jit(solution)/shard_map/convert_element_type | solution.py:208
  75.0 15.8 %all-gather.2.cloned.1.call-done = bf16[1152,3456]{1,0:T(8,128)(2,1)} async-done(((bf16[72,3456]{1,0:T(8,128)(2,1)}), bf16[1152,3456]{1,0:T(8,128)(2,1)}) %all-gather.2.cloned.1.call-update) | async-done | bytes 7962640 | tf_op jit(solution)/shard_map/all_gather | solution.py:182
  90.8 7.0 %convolution_convert_fusion.1 = bf16[256,3456]{1,0:T(8,128)(2,1)} fusion(bf16[256,1152]{1,0:T(8,128)(2,1)S(1)} %fusion.8, bf16[1152,3456]{1,0:T(8,128)(2,1)} %all-gather.2.cloned.1.call-done), kind=kOutput, calls=%fused_computation.5 | convolution fusion | flops 2039316480 | bytes 10321920 | tf_op jit(solution)/shard_map/dot_general | solution.py:204
  97.8 7.1 %reshape.157 = bf16[2,16,8,3,16,72]{5,4,3,2,1,0:T(8,128)(2,1)S(1)} reshape(bf16[256,3456]{1,0:T(8,128)(2,1)} %convolution_convert_fusion.1) | data formatting | bytes 3538944 | tf_op jit(solution)/shard_map/reshape | solution.py:205
  105.9 1.7 fusion.4
  107.6 2.3 multiply_reduce_fusion
  109.9 2.4 fusion.6
  112.3 2.2 fusion.7
  114.5 2.8 fusion.5
  118.9 4.6 %dot_general.32 = bf16[2,16,8,3456]{3,2,1,0:T(8,128)(2,1)} reshape(bf16[2,16,8,3,16,72]{5,4,3,2,1,0:T(8,128)(2,1)S(1)} %copy.47) | data formatting | bytes 3538944 | tf_op jit(solution)/shard_map/dot_general | solution.py:222
  123.5 4.6 %reshape.159 = bf16[256,3456]{1,0:T(8,128)(2,1)} reshape(bf16[2,16,8,3,16,72]{5,4,3,2,1,0:T(8,128)(2,1)S(1)} %copy.47) | data formatting | bytes 3538944 | tf_op jit(solution)/shard_map/reshape | solution.py:212
  128.1 6.7 %multiply_reduce_fusion.1 = (f32[2,1152]{1,0:T(2,128)S(1)}, f32[2,16,8]{2,1,0:T(8,128)S(1)}, f32[2,16,8]{2,1,0:T(8,128)S(1)}, f32[2,1152]{1,0:T(2,128)S(1)}, bf1...) fusion(f32[2,16,8]{2,1,0:T(8,128)S(1)} %add_rsqrt_fusion, ...), kind=kOutput, calls=%fused_computation.28 | convolution fusion | flops 2042260480 | bytes 12132352 | tf_op jit(solution)/shard_map/dot_general | solution.py:222
  134.8 5.4 %convolution_convert_fusion = bf16[1152,3456]{1,0:T(8,128)(2,1)} fusion(bf16[256,1152]{1,0:T(8,128)(2,1)S(1)} %bitcast.105, bf16[256,3456]{1,0:T(8,128)(2,1)S(1)} %copy-done.3), kind=kOutput, calls=%fused_computation.2 | convolution fusion | flops 2042413056 | bytes 10321920 | tf_op jit(solution)/shard_map/dot_general | solution.py:214
  142.8 8.7 %all-to-all-start.1 = ((bf16[2,16,8,1152]{3,2,0,1:T(8,128)(2,1)}), bf16[2,16,8,1152]{3,2,0,1:T(8,128)(2,1)S(1)}, u32[]{:S(2)}, u32[]{:S(2)}) async-start(bf16[2,16,8,1152]{3,2,0,1:T(8,128)(2,1)} %copy.48), calls=%async_computation.1 | async-start | bytes 1179648 | tf_op jit(solution)/shard_map/all_to_all | solution.py:242
  152.2 35.2 %shard_map.95 = f32[4,1152]{1,0:T(4,128)} custom-call(f32[4,1152]{1,0:T(4,128)} %reshape.161.sums_ref), custom_call_target="tpu_custom_call" | custom-call | tf_op jit(solution)/shard_map/pallas_call | solution.py:159
  189.6 43.3 %reduce-scatter.5.cloned.1.call-done = bf16[72,3456]{1,0:T(8,128)(2,1)} async-done(((bf16[1152,3456]{1,0:T(8,128)(2,1)}), bf16[72,3456]{1,0:T(8,128)(2,1)}) %reduce-scatter.5.cloned.1.call-update) | async-done | bytes 497680
  232.9 2.8 reshape.160
  236.7 52.9 %shard_map.94 = f32[4,4,72,216]{3,2,1,0:T(8,128)} custom-call(bf16[4,4,72,216]{3,2,1,0:T(8,128)(2,1)} %bitcast.102), custom_call_target="tpu_custom_call" | custom-call | tf_op jit(solution)/shard_map/pallas_call | solution.py:140
  291.8 2.0 mul.144
  (55 shorter events, 15.3 us)
Async XLA Ops:
  7.2 21.0 %copy-start = (f32[1000]{0:T(1024)S(1)}, f32[1000]{0:T(1024)}, u32[]{:S(2)}) copy-start(f32[1000]{0:T(1024)} %param.11) | copy-start | bytes 12004
  7.2 83.6 %all-gather.2.cloned.1.call-start = ((), (), s32[]{:S(2)}) async-start(), calls=%async_computation.3 | async-start | bytes 8460288 | tf_op jit(solution)/shard_map/all_gather | solution.py:182
  11.3 13.9 %copy-start.5 = (s32[2]{0:T(128)S(1)}, s32[2]{0:T(128)}, u32[]{:S(2)}) copy-start(s32[2]{0:T(128)} %param.12) | copy-start | bytes 28
  11.3 16.9 %copy-start.6 = (s32[2]{0:T(128)S(1)}, s32[2]{0:T(128)}, u32[]{:S(2)}) copy-start(s32[2]{0:T(128)} %param.13) | copy-start | bytes 28
  13.9 56.7 %all-to-all-start = ((bf16[2,1,128,2,1152]{4,0,3,1,2:T(2,128)(2,1)}), bf16[2,1,128,2,1152]{4,0,3,1,2:T(2,128)(2,1)S(1)}, u32[]{:S(2)}, u32[]{:S(2)}) async-start(bf16[2,1,128,2,1152]{4,0,3,1,2:T(2,128)(2,1)} %pad_maximum_fusion.1), calls=%async_computation | async-start | bytes 2359296 | tf_op jit(solution)/shard_map/all_to_all | solution.py:190
  25.2 207.8 %reduce-scatter.5.cloned.1.call-start = ((), (), s32[]{:S(2)}) async-start(), calls=%async_computation.4 | async-start | bytes 8460288
  70.8 3.9 %copy-start.1 = (bf16[2,1,128,2,1152]{4,2,0,3,1:T(8,128)(2,1)}, bf16[2,1,128,2,1152]{4,2,0,3,1:T(8,128)(2,1)S(1)}, u32[]{:S(2)}) copy-start(bf16[2,1,128,2,1152]{4,2,0,3,1:T(8,128)(2,1)S(1)} %copy.86) | copy-start | bytes 3538948
  105.9 1.7 copy-start.4
  128.1 6.7 %copy-start.3 = (bf16[256,3456]{1,0:T(8,128)(2,1)S(1)}, bf16[256,3456]{1,0:T(8,128)(2,1)}, u32[]{:S(2)}) copy-start(bf16[256,3456]{1,0:T(8,128)(2,1)} %reshape.159) | copy-start | bytes 5308420
  140.3 1.3 copy-start.2
  142.8 45.9 %all-to-all-start.1 = ((bf16[2,16,8,1152]{3,2,0,1:T(8,128)(2,1)}), bf16[2,16,8,1152]{3,2,0,1:T(8,128)(2,1)S(1)}, u32[]{:S(2)}, u32[]{:S(2)}) async-start(bf16[2,16,8,1152]{3,2,0,1:T(8,128)(2,1)} %copy.48), calls=%async_computation.1 | async-start | bytes 1179648 | tf_op jit(solution)/shard_map/all_to_all | solution.py:242
Sparse Core Ops, SparseCore 0:
  9.9 80.8 all-gather.1
  140.4 92.4 reduce-scatter.4

commit v6 on v4

--- a/solution.py
+++ b/solution.py
@@ -15,19 +15,22 @@
 
 def attend_back(queries, keys, values, upstream):
     factor = queries.shape[-1] ** (-0.5)
-    queries = queries.astype(jnp.float32)
-    keys = keys.astype(jnp.float32)
-    values = values.astype(jnp.float32)
-    upstream = upstream.astype(jnp.float32)
-    highest = lax.Precision.HIGHEST
-    scores = jnp.einsum("bfxhe,bgxhe->bxhfg", queries, keys, precision=highest) * factor
+    f32 = jnp.float32
+    high = lax.Precision.HIGH
+    scores = jnp.einsum("bfxhe,bgxhe->bxhfg", queries, keys, preferred_element_type=f32) * factor
     expd = jnp.exp(scores)
     probs = expd / jnp.sum(expd, axis=-1, keepdims=True)
-    grad_probs = jnp.einsum("bfxhe,bgxhe->bxhfg", upstream, values, precision=highest)
-    grad_values = jnp.einsum("bxhfg,bfxhe->bgxhe", probs, upstream, precision=highest)
+    grad_probs = jnp.einsum("bfxhe,bgxhe->bxhfg", upstream, values, preferred_element_type=f32)
+    grad_values = jnp.einsum(
+        "bxhfg,bfxhe->bgxhe", probs, upstream.astype(f32), precision=high
+    )
     grad_scores = probs * (grad_probs - jnp.sum(probs * grad_probs, axis=-1, keepdims=True))
-    grad_queries = jnp.einsum("bxhfg,bgxhe->bfxhe", grad_scores, keys, precision=highest) * factor
-    grad_keys = jnp.einsum("bxhfg,bfxhe->bgxhe", grad_scores, queries, precision=highest) * factor
+    grad_queries = jnp.einsum(
+        "bxhfg,bgxhe->bfxhe", grad_scores, keys.astype(f32), precision=high
+    ) * factor
+    grad_keys = jnp.einsum(
+        "bxhfg,bfxhe->bgxhe", grad_scores, queries.astype(f32), precision=high
+    ) * factor
     return (
         grad_queries.astype(jnp.bfloat16),
         grad_keys.astype(jnp.bfloat16),

time: 295 us -> 294 us (level)
  no operation moved by 1% of the time
where the time goes in v6:
time: 294 us; the launch traced here: 291 us
  waiting for transfers between devices  102 us (35%)
  Pallas kernels  81.3 us (28%)
  local copies, waits for them, and re-layouts  38.6 us (13%)
  matrix products  28.9 us (10%)
  starting transfers between devices  20 us (7%)
  between operations  14.4 us (5%)
  other arithmetic  6.62 us (2%)
    pallas_call x1, Pallas kernels, reduce_weight(): pl.pallas_call(functools.partial(weight_kernel, nf), out_shape=jax.ShapeD...  46.1 us
    unnamed x3, waiting for transfers between devices  44 us
    all_to_all x1, waiting for transfers between devices, per_device(): lax.all_to_all(both, 'frame', split_axis=2, concat_axis=1, tiled=True)  41.8 us
    pallas_call x1, Pallas kernels, reduce_sums(): pl.pallas_call(functools.partial(sums_kernel, nf, ns), out_shape=jax.Shap...  35.2 us
    all_gather x1, waiting for transfers between devices, per_device(): w_full = lax.all_gather(w_qkv, 'space', axis=0, tiled=True)  15.8 us
    all_to_all x1, starting transfers between devices, per_device(): lax.all_to_all(both, 'frame', split_axis=2, concat_axis=1, tiled=True)  11.2 us
    all_to_all x1, starting transfers between devices, per_device(): lax.all_to_all(grad_input, 'frame', split_axis=1, concat_axis=2, tiled=True)  8.68 us
    reshape x1, local copies, waits for them, and re-layouts, per_device(): pieces = projected.reshape(clip_count, frames, across, 3, HEADS, HEAD_DIM)  7.1 us
  transfers between devices with their start and end apart: 4, of which 3 were waited for; matrix products, arithmetic and copies ran while one was open for 6% of the time, Pallas kernels for 12%

profile of v6, /device:TPU:6, one launch (start us, length us, event | category | flops | bytes accessed | tf_op | source)
XLA Modules:
  0.0 291.4 jit_solution(4855388960221929488)
XLA Ops:
  7.9 1.7 copy.39
  9.6 1.7 copy.40
  11.3 2.7 pad_maximum_fusion.1
  13.9 11.2 %all-to-all-start = ((bf16[2,1,128,2,1152]{4,0,3,1,2:T(2,128)(2,1)}), bf16[2,1,128,2,1152]{4,0,3,1,2:T(2,128)(2,1)S(1)}, u32[]{:S(2)}, u32[]{:S(2)}) async-start(bf16[2,1,128,2,1152]{4,0,3,1,2:T(2,128)(2,1)} %pad_maximum_fusion.1), calls=%async_computation | async-start | bytes 2359296 | tf_op jit(solution)/shard_map/all_to_all | solution.py:171
  25.2 2.9 gather_fusion
  28.9 41.8 %all-to-all-done = bf16[2,1,128,2,1152]{4,0,3,1,2:T(2,128)(2,1)S(1)} async-done(((bf16[2,1,128,2,1152]{4,0,3,1,2:T(2,128)(2,1)}), bf16[2,1,128,2,1152]{4,0,3,1,2:T(2,128)(2,1)S(1)}, u32[]{:S(2)}, u32[]{:S(2)}) %all-to-all-start) | async-done | bytes 1179680 | tf_op jit(solution)/shard_map/all_to_all | solution.py:171
  71.5 3.1 %reshape.163 = f32[2,16,8,16,72]{4,3,2,1,0:T(8,128)} reshape(f32[2,16,8,1,1152]{4,2,1,0,3:T(8,128)S(1)} %slice_convert_fusion) | data formatting | bytes 2359296 | tf_op jit(solution)/shard_map/convert_element_type | solution.py:189
  75.0 15.8 %all-gather.2.cloned.1.call-done = bf16[1152,3456]{1,0:T(8,128)(2,1)} async-done(((bf16[72,3456]{1,0:T(8,128)(2,1)}), bf16[1152,3456]{1,0:T(8,128)(2,1)}) %all-gather.2.cloned.1.call-update) | async-done | bytes 7962640 | tf_op jit(solution)/shard_map/all_gather | solution.py:163
  90.8 7.0 %convolution_convert_fusion.1 = bf16[256,3456]{1,0:T(8,128)(2,1)} fusion(bf16[256,1152]{1,0:T(8,128)(2,1)S(1)} %fusion.8, bf16[1152,3456]{1,0:T(8,128)(2,1)} %all-gather.2.cloned.1.call-done), kind=kOutput, calls=%fused_computation.5 | convolution fusion | flops 2039316480 | bytes 10321920 | tf_op jit(solution)/shard_map/dot_general | solution.py:185
  97.8 7.1 %reshape.157 = bf16[2,16,8,3,16,72]{5,4,3,2,1,0:T(8,128)(2,1)S(1)} reshape(bf16[256,3456]{1,0:T(8,128)(2,1)} %convolution_convert_fusion.1) | data formatting | bytes 3538944 | tf_op jit(solution)/shard_map/reshape | solution.py:186
  105.9 1.7 fusion.4
  107.6 2.3 multiply_reduce_fusion
  109.9 1.9 fusion.6
  111.8 1.7 fusion.7
  113.5 2.1 fusion.5
  117.5 4.6 %dot_general.32 = bf16[2,16,8,3456]{3,2,1,0:T(8,128)(2,1)} reshape(bf16[2,16,8,3,16,72]{5,4,3,2,1,0:T(8,128)(2,1)S(1)} %copy.47) | data formatting | bytes 3538944 | tf_op jit(solution)/shard_map/dot_general | solution.py:202
  122.1 4.6 %reshape.159 = bf16[256,3456]{1,0:T(8,128)(2,1)} reshape(bf16[2,16,8,3,16,72]{5,4,3,2,1,0:T(8,128)(2,1)S(1)} %copy.47) | data formatting | bytes 3538944 | tf_op jit(solution)/shard_map/reshape | solution.py:193
  126.6 6.7 %multiply_reduce_fusion.1 = (f32[2,1152]{1,0:T(2,128)S(1)}, f32[2,16,8]{2,1,0:T(8,128)S(1)}, f32[2,16,8]{2,1,0:T(8,128)S(1)}, f32[2,1152]{1,0:T(2,128)S(1)}, bf1...) fusion(f32[2,16,8]{2,1,0:T(8,128)S(1)} %add_rsqrt_fusion, ...), kind=kOutput, calls=%fused_computation.28 | convolution fusion | flops 2042260480 | bytes 12132352 | tf_op jit(solution)/shard_map/dot_general | solution.py:202
  133.4 5.4 %convolution_convert_fusion = bf16[1152,3456]{1,0:T(8,128)(2,1)} fusion(bf16[256,1152]{1,0:T(8,128)(2,1)S(1)} %bitcast.105, bf16[256,3456]{1,0:T(8,128)(2,1)S(1)} %copy-done.3), kind=kOutput, calls=%fused_computation.2 | convolution fusion | flops 2042413056 | bytes 10321920 | tf_op jit(solution)/shard_map/dot_general | solution.py:195
  141.4 8.7 %all-to-all-start.1 = ((bf16[2,16,8,1152]{3,2,0,1:T(8,128)(2,1)}), bf16[2,16,8,1152]{3,2,0,1:T(8,128)(2,1)S(1)}, u32[]{:S(2)}, u32[]{:S(2)}) async-start(bf16[2,16,8,1152]{3,2,0,1:T(8,128)(2,1)} %copy.48), calls=%async_computation.1 | async-start | bytes 1179648 | tf_op jit(solution)/shard_map/all_to_all | solution.py:222
  150.8 35.2 %shard_map.95 = f32[4,1152]{1,0:T(4,128)} custom-call(f32[4,1152]{1,0:T(4,128)} %reshape.161.sums_ref), custom_call_target="tpu_custom_call" | custom-call | tf_op jit(solution)/shard_map/pallas_call | solution.py:140
  188.2 43.3 %reduce-scatter.5.cloned.1.call-done = bf16[72,3456]{1,0:T(8,128)(2,1)} async-done(((bf16[1152,3456]{1,0:T(8,128)(2,1)}), bf16[72,3456]{1,0:T(8,128)(2,1)}) %reduce-scatter.5.cloned.1.call-update) | async-done | bytes 497680
  231.5 2.8 reshape.160
  235.3 46.1 %shard_map.94 = bf16[16,72,216]{2,1,0:T(8,128)(2,1)} custom-call(bf16[16,72,216]{2,1,0:T(8,128)(2,1)} %bitcast.102), custom_call_target="tpu_custom_call" | custom-call | tf_op jit(solution)/shard_map/pallas_call | solution.py:123
  (55 shorter events, 14.9 us)
Async XLA Ops:
  7.2 21.0 %copy-start = (f32[1000]{0:T(1024)S(1)}, f32[1000]{0:T(1024)}, u32[]{:S(2)}) copy-start(f32[1000]{0:T(1024)} %param.11) | copy-start | bytes 12004
  7.2 83.6 %all-gather.2.cloned.1.call-start = ((), (), s32[]{:S(2)}) async-start(), calls=%async_computation.3 | async-start | bytes 8460288 | tf_op jit(solution)/shard_map/all_gather | solution.py:163
  11.3 13.9 %copy-start.5 = (s32[2]{0:T(128)S(1)}, s32[2]{0:T(128)}, u32[]{:S(2)}) copy-start(s32[2]{0:T(128)} %param.12) | copy-start | bytes 28
  11.3 16.9 %copy-start.6 = (s32[2]{0:T(128)S(1)}, s32[2]{0:T(128)}, u32[]{:S(2)}) copy-start(s32[2]{0:T(128)} %param.13) | copy-start | bytes 28
  13.9 56.7 %all-to-all-start = ((bf16[2,1,128,2,1152]{4,0,3,1,2:T(2,128)(2,1)}), bf16[2,1,128,2,1152]{4,0,3,1,2:T(2,128)(2,1)S(1)}, u32[]{:S(2)}, u32[]{:S(2)}) async-start(bf16[2,1,128,2,1152]{4,0,3,1,2:T(2,128)(2,1)} %pad_maximum_fusion.1), calls=%async_computation | async-start | bytes 2359296 | tf_op jit(solution)/shard_map/all_to_all | solution.py:171
  25.2 206.3 %reduce-scatter.5.cloned.1.call-start = ((), (), s32[]{:S(2)}) async-start(), calls=%async_computation.4 | async-start | bytes 8460288
  70.8 3.9 %copy-start.1 = (bf16[2,1,128,2,1152]{4,2,0,3,1:T(8,128)(2,1)}, bf16[2,1,128,2,1152]{4,2,0,3,1:T(8,128)(2,1)S(1)}, u32[]{:S(2)}) copy-start(bf16[2,1,128,2,1152]{4,2,0,3,1:T(8,128)(2,1)S(1)} %copy.86) | copy-start | bytes 3538948
  105.9 1.7 copy-start.4
  126.6 6.7 %copy-start.3 = (bf16[256,3456]{1,0:T(8,128)(2,1)S(1)}, bf16[256,3456]{1,0:T(8,128)(2,1)}, u32[]{:S(2)}) copy-start(bf16[256,3456]{1,0:T(8,128)(2,1)} %reshape.159) | copy-start | bytes 5308420
  138.8 1.3 copy-start.2
  141.4 45.9 %all-to-all-start.1 = ((bf16[2,16,8,1152]{3,2,0,1:T(8,128)(2,1)}), bf16[2,16,8,1152]{3,2,0,1:T(8,128)(2,1)S(1)}, u32[]{:S(2)}, u32[]{:S(2)}) async-start(bf16[2,16,8,1152]{3,2,0,1:T(8,128)(2,1)} %copy.48), calls=%async_computation.1 | async-start | bytes 1179648 | tf_op jit(solution)/shard_map/all_to_all | solution.py:222
Sparse Core Ops, SparseCore 0:
  9.9 80.8 all-gather.1
  139.0 92.4 reduce-scatter.4

commit v7 on v6

--- a/solution.py
+++ b/solution.py
@@ -195,6 +195,7 @@
     term = lax.dot_general(
         mod_rows, grad_rows, (((0,), (0,)), ((), ())), preferred_element_type=jnp.float32
     ).astype(jnp.bfloat16)
+    term, grad_rows = lax.optimization_barrier((term, grad_rows))
     col_blk = 3 * model_width // frame_n
     share = lax.psum_scatter(term, "space", scatter_dimension=0, tiled=True)
     row_blk = share.shape[0]

time: 294 us -> 279 us (0.949)
  waiting for transfers between devices: 102 us -> 89.5 us
  other arithmetic: 6.62 us -> 11.6 us
    unnamed x3, waiting for transfers between devices: 44 us -> 35.9 us
    dot_general x1 -> x0, local copies, waits for them, and re-layouts: 4.61 us -> none  [per_device(): lax.dot_general(grad_rows, w_full, (((1,), (1,)), ((), ())), preferred_el...]
    all_gather x1, waiting for transfers between devices: 15.8 us -> 12 us  [per_device(): w_full = lax.all_gather(w_qkv, 'space', axis=0, tiled=True)]
  transfers between devices with their start and end apart: 4 -> 4, of which waited for: 3 -> 3; matrix products, arithmetic and copies ran while one was open for 6% -> 11% of each run, Pallas kernels for 12% -> 12%
where the time goes in v7:
time: 279 us; the launch traced here: 278 us
  waiting for transfers between devices  89.5 us (32%)
  Pallas kernels  78.9 us (28%)
  local copies, waits for them, and re-layouts  36.9 us (13%)
  matrix products  27.1 us (10%)
  starting transfers between devices  20 us (7%)
  between operations  14.5 us (5%)
  other arithmetic  11.6 us (4%)
    pallas_call x1, Pallas kernels, reduce_weight(): pl.pallas_call(functools.partial(weight_kernel, nf), out_shape=jax.ShapeD...  44.1 us
    all_to_all x1, waiting for transfers between devices, per_device(): lax.all_to_all(both, 'frame', split_axis=2, concat_axis=1, tiled=True)  41.7 us
    unnamed x3, waiting for transfers between devices  35.9 us
    pallas_call x1, Pallas kernels, reduce_sums(): pl.pallas_call(functools.partial(sums_kernel, nf, ns), out_shape=jax.Shap...  34.8 us
    all_gather x1, waiting for transfers between devices, per_device(): w_full = lax.all_gather(w_qkv, 'space', axis=0, tiled=True)  12 us
    all_to_all x1, starting transfers between devices, per_device(): lax.all_to_all(both, 'frame', split_axis=2, concat_axis=1, tiled=True)  11.2 us
    all_to_all x1, starting transfers between devices, per_device(): lax.all_to_all(grad_input, 'frame', split_axis=1, concat_axis=2, tiled=True)  8.68 us
    dot_general x1, matrix products, per_device(): lax.dot_general(grad_rows, w_full, (((1,), (1,)), ((), ())), preferred_el...  6.93 us
  transfers between devices with their start and end apart: 4, of which 3 were waited for; matrix products, arithmetic and copies ran while one was open for 11% of the time, Pallas kernels for 12%

profile of v7, /device:TPU:6, one launch (start us, length us, event | category | flops | bytes accessed | tf_op | source)
XLA Modules:
  0.0 278.4 jit_solution(14080278893786814094)
XLA Ops:
  9.6 1.7 copy.46
  11.3 2.6 pad_maximum_fusion.1
  13.9 11.2 %all-to-all-start = ((bf16[2,1,128,2,1152]{4,0,3,1,2:T(2,128)(2,1)}), bf16[2,1,128,2,1152]{4,0,3,1,2:T(2,128)(2,1)S(1)}, u32[]{:S(2)}, u32[]{:S(2)}) async-start(bf16[2,1,128,2,1152]{4,0,3,1,2:T(2,128)(2,1)} %pad_maximum_fusion.1), calls=%async_computation | async-start | bytes 2359296 | tf_op jit(solution)/shard_map/all_to_all | solution.py:171
  25.2 2.9 %gather_fusion = bf16[2,2,1152]{2,1,0:T(2,128)(2,1)S(1)} fusion(bf16[1000,2,1152]{2,1,0:T(2,128)(2,1)} %param.10, s32[1024]{0:T(1024)S(1)} %pad_clamp_fusion.1), kind=kCustom, calls=%fused_computation | custom fusion | bytes 18440 | tf_op jit(solution)/shard_map/gather | solution.py:180
  28.9 41.7 %all-to-all-done = bf16[2,1,128,2,1152]{4,0,3,1,2:T(2,128)(2,1)S(1)} async-done(((bf16[2,1,128,2,1152]{4,0,3,1,2:T(2,128)(2,1)}), bf16[2,1,128,2,1152]{4,0,3,1,2:T(2,128)(2,1)S(1)}, u32[]{:S(2)}, u32[]{:S(2)}) %all-to-all-start) | async-done | bytes 1179680 | tf_op jit(solution)/shard_map/all_to_all | solution.py:171
  73.1 2.9 %reshape.183 = f32[2,16,8,16,72]{4,3,2,1,0:T(8,128)S(1)} reshape(f32[2,16,8,1,1152]{4,2,1,0,3:T(8,128)} %slice_convert_fusion) | data formatting | bytes 2359296 | tf_op jit(solution)/shard_map/convert_element_type | solution.py:189
  78.8 12.0 %all-gather.2.cloned.1.call-done = bf16[1152,3456]{1,0:T(8,128)(2,1)} async-done(((bf16[72,3456]{1,0:T(8,128)(2,1)}), bf16[1152,3456]{1,0:T(8,128)(2,1)}) %all-gather.2.cloned.1.call-update) | async-done | bytes 7962640 | tf_op jit(solution)/shard_map/all_gather | solution.py:163
  90.7 6.0 %convolution_convert_fusion.1 = bf16[256,3456]{1,0:T(8,128)(2,1)S(1)} fusion(bf16[256,1152]{1,0:T(8,128)(2,1)} %fusion.6, bf16[1152,3456]{1,0:T(8,128)(2,1)} %all-gather.2.cloned.1.call-done), kind=kOutput, calls=%fused_computation.3 | convolution fusion | flops 2039316480 | bytes 10321920 | tf_op jit(solution)/shard_map/dot_general | solution.py:185
  96.7 6.5 %reshape.176 = bf16[2,16,8,3,16,72]{5,4,3,2,1,0:T(8,128)(2,1)} reshape(bf16[256,3456]{1,0:T(8,128)(2,1)S(1)} %convolution_convert_fusion.1) | data formatting | bytes 3538944 | tf_op jit(solution)/shard_map/reshape | solution.py:186
  103.2 2.5 fusion.18
  105.7 1.7 fusion.1
  109.0 1.8 multiply_reduce_fusion
  110.8 1.7 fusion.4
  112.5 1.9 fusion.3
  115.2 2.6 copy.54
  117.8 5.1 %reshape.177 = bf16[256,3456]{1,0:T(8,128)(2,1)S(1)} reshape(bf16[2,16,8,3,16,72]{5,4,3,2,1,0:T(8,128)(2,1)} %copy.54) | data formatting | bytes 3538944 | tf_op jit(solution)/shard_map/reshape | solution.py:193
  122.9 5.5 %convolution_convert_fusion = bf16[1152,3456]{1,0:T(8,128)(2,1)} fusion(bf16[256,1152]{1,0:T(8,128)(2,1)S(1)} %bitcast.106, bf16[256,3456]{1,0:T(8,128)(2,1)S(1)} %reshape.177), kind=kOutput, calls=%fused_computation.2 | convolution fusion | flops 2042413056 | bytes 10321920 | tf_op jit(solution)/shard_map/dot_general | solution.py:195
  129.1 6.9 %fusion.10 = (f32[256]{0:T(256)S(1)}, f32[256]{0:T(256)S(1)}, f32[256,1152]{1,0:T(8,128)}) fusion(f32[2,1152]{1,0:T(2,128)S(1)} %get-tuple-element.24, f32[256]{0:T(256)S(1)} %copy-done.13, f32[256]{0:T(256)S(1)} %copy-done.11, bf16[2,16,8,2,1152]{4,2,1,0,3:T(8,128)(2,1)S(1)} %bitcast.104, bf16[256,3456]{1,0:T(8,128)(2,1)S(1)} %reshape.177, ...), kind=kOutput, calls=%fused_computation.36 | convolution fusion | flops 2040495616 | bytes 11514880 | tf_op jit(solution)/shard_map/dot_general | solution.py:203
  136.3 1.9 bitcast_reduce_fusion
  139.0 8.7 %all-to-all-start.1 = ((bf16[2,16,8,1152]{3,2,0,1:T(8,128)(2,1)}), bf16[2,16,8,1152]{3,2,0,1:T(8,128)(2,1)S(1)}, u32[]{:S(2)}, u32[]{:S(2)}) async-start(bf16[2,16,8,1152]{3,2,0,1:T(8,128)(2,1)} %copy.55), calls=%async_computation.1 | async-start | bytes 1179648 | tf_op jit(solution)/shard_map/all_to_all | solution.py:223
  148.4 34.8 %shard_map.95 = f32[4,1152]{1,0:T(4,128)} custom-call(f32[4,1152]{1,0:T(4,128)} %reshape.181.sums_ref), custom_call_target="tpu_custom_call" | custom-call | tf_op jit(solution)/shard_map/pallas_call | solution.py:140
  185.4 35.2 %reduce-scatter.5.cloned.1.call-done = bf16[72,3456]{1,0:T(8,128)(2,1)} async-done(((bf16[1152,3456]{1,0:T(8,128)(2,1)}), bf16[72,3456]{1,0:T(8,128)(2,1)}) %reduce-scatter.5.cloned.1.call-update) | async-done | bytes 497680
  220.5 2.8 reshape.180
  224.3 44.1 %shard_map.94 = bf16[16,72,216]{2,1,0:T(8,128)(2,1)} custom-call(bf16[16,72,216]{2,1,0:T(8,128)(2,1)} %bitcast.107), custom_call_target="tpu_custom_call" | custom-call | tf_op jit(solution)/shard_map/pallas_call | solution.py:123
  (76 shorter events, 19.5 us)
Async XLA Ops:
  7.2 21.0 %copy-start = (f32[1000]{0:T(1024)S(1)}, f32[1000]{0:T(1024)}, u32[]{:S(2)}) copy-start(f32[1000]{0:T(1024)} %param.11) | copy-start | bytes 12004
  7.2 83.6 %all-gather.2.cloned.1.call-start = ((), (), s32[]{:S(2)}) async-start(), calls=%async_computation.3 | async-start | bytes 8460288 | tf_op jit(solution)/shard_map/all_gather | solution.py:163
  11.3 13.9 %copy-start.14 = (s32[2]{0:T(128)S(1)}, s32[2]{0:T(128)}, u32[]{:S(2)}) copy-start(s32[2]{0:T(128)} %param.12) | copy-start | bytes 28
  11.3 16.9 %copy-start.15 = (s32[2]{0:T(128)S(1)}, s32[2]{0:T(128)}, u32[]{:S(2)}) copy-start(s32[2]{0:T(128)} %param.13) | copy-start | bytes 28
  13.9 56.7 %all-to-all-start = ((bf16[2,1,128,2,1152]{4,0,3,1,2:T(2,128)(2,1)}), bf16[2,1,128,2,1152]{4,0,3,1,2:T(2,128)(2,1)S(1)}, u32[]{:S(2)}, u32[]{:S(2)}) async-start(bf16[2,1,128,2,1152]{4,0,3,1,2:T(2,128)(2,1)} %pad_maximum_fusion.1), calls=%async_computation | async-start | bytes 2359296 | tf_op jit(solution)/shard_map/all_to_all | solution.py:171
  25.1 195.4 %reduce-scatter.5.cloned.1.call-start = ((), (), s32[]{:S(2)}) async-start(), calls=%async_computation.4 | async-start | bytes 8460288
  28.8 47.1 %copy-start.8 = (f32[2,1152]{1,0:T(2,128)}, f32[2,1152]{1,0:T(2,128)S(1)}, u32[]{:S(2)}) copy-start(f32[2,1152]{1,0:T(2,128)S(1)} %get-tuple-element.23) | copy-start | bytes 27652
  70.9 0.6 copy-start.2
  71.0 5.0 %copy-start.10 = (f32[256]{0:T(256)}, f32[256]{0:T(256)S(1)}, u32[]{:S(2)}) copy-start(f32[256]{0:T(256)S(1)} %div.28) | copy-start | bytes 3076
  71.3 0.6 copy-start.5
  71.9 4.1 %copy-start.12 = (f32[256]{0:T(256)}, f32[256]{0:T(256)S(1)}, u32[]{:S(2)}) copy-start(f32[256]{0:T(256)S(1)} %rsqrt.13) | copy-start | bytes 3076
  76.0 2.5 copy-start.3
  76.0 2.4 copy-start.6
  77.1 1.3 copy-start.9
  105.7 1.7 copy-start.1
  128.4 0.7 copy-start.11
  128.4 0.7 copy-start.13
  129.1 7.1 %copy-start.4 = (f32[2,16,8]{2,1,0:T(8,128)S(1)}, f32[2,16,8]{2,1,0:T(8,128)}, u32[]{:S(2)}) copy-start(f32[2,16,8]{2,1,0:T(8,128)} %copy-done.2) | copy-start | bytes 3076
  129.1 7.1 %copy-start.7 = (f32[2,16,8]{2,1,0:T(8,128)S(1)}, f32[2,16,8]{2,1,0:T(8,128)}, u32[]{:S(2)}) copy-start(f32[2,16,8]{2,1,0:T(8,128)} %copy-done.5) | copy-start | bytes 3076
  139.0 45.5 %all-to-all-start.1 = ((bf16[2,16,8,1152]{3,2,0,1:T(8,128)(2,1)}), bf16[2,16,8,1152]{3,2,0,1:T(8,128)(2,1)S(1)}, u32[]{:S(2)}, u32[]{:S(2)}) async-start(bf16[2,16,8,1152]{3,2,0,1:T(8,128)(2,1)} %copy.55), calls=%async_computation.1 | async-start | bytes 1179648 | tf_op jit(solution)/shard_map/all_to_all | solution.py:223
Sparse Core Ops, SparseCore 0:
  9.9 80.8 all-gather.1
  128.6 91.9 reduce-scatter.4

commit v8 on v7

--- a/solution.py
+++ b/solution.py
@@ -69,14 +69,17 @@
         c.wait_send()
 
 
-def weight_kernel(nf, chunks_ref, gw_ref, recv1, redbuf, recv2, s1, r1, s2, r2):
+def weight_kernel(nf, scale, share_ref, gw_ref, chunks, recv1, redbuf, recv2, s1, r1, s2, r2):
+    cols = chunks.shape[2]
+    for j in range(nf):
+        chunks[j] = share_ref[:, j * cols:(j + 1) * cols]
     me_f = lax.axis_index("frame")
     me_s = lax.axis_index("space")
     peer = lambda t: (t, me_s)
     barrier_with([peer(lax.rem(me_f + k, nf)) for k in range(1, nf)])
-    first = lambda t: chunks_ref.at[t]
+    first = lambda t: chunks.at[t]
     sends = exchange(first, recv1, peer, me_f, nf, s1, r1)
-    recv1[me_f] = chunks_ref[me_f]
+    recv1[me_f] = chunks[me_f]
     wait_all(first, recv1, peer, me_f, nf, s1, r1, sends)
     acc = recv1[0].astype(jnp.float32)
     for j in range(1, nf):
@@ -87,7 +90,8 @@
     second = lambda t: redbuf
     sends = exchange(second, recv2, peer, me_f, nf, s2, r2)
     wait_all(second, recv2, peer, me_f, nf, s2, r2, sends)
-    gw_ref[...] = recv2[...]
+    for j in range(nf):
+        gw_ref[:, j * cols:(j + 1) * cols] = recv2[j].astype(jnp.float32) * scale
 
 
 def sums_kernel(nf, ns, sums_ref, gm_ref, msum1, mbuf, msum2, s1, r1, s2, r2):
@@ -117,22 +121,24 @@
     gm_ref[...] = total
 
 
-def reduce_weight(chunks, nf):
-    count, rows, cols = chunks.shape
+def reduce_weight(share, nf, scale):
+    rows, width = share.shape
+    cols = width // nf
     vmem = pl.BlockSpec(memory_space=pltpu.VMEM)
     return pl.pallas_call(
-        functools.partial(weight_kernel, nf),
-        out_shape=jax.ShapeDtypeStruct((count, rows, cols), chunks.dtype),
+        functools.partial(weight_kernel, nf, scale),
+        out_shape=jax.ShapeDtypeStruct((rows, width), jnp.float32),
         in_specs=[vmem],
         out_specs=vmem,
         scratch_shapes=[
-            pltpu.VMEM((nf, rows, cols), chunks.dtype),
-            pltpu.VMEM((rows, cols), chunks.dtype),
-            pltpu.VMEM((nf, rows, cols), chunks.dtype),
+            pltpu.VMEM((nf, rows, cols), share.dtype),
+            pltpu.VMEM((nf, rows, cols), share.dtype),
+            pltpu.VMEM((rows, cols), share.dtype),
+            pltpu.VMEM((nf, rows, cols), share.dtype),
         ]
         + [pltpu.SemaphoreType.DMA((nf,))] * 4,
         compiler_params=pltpu.CompilerParams(collective_id=0, has_side_effects=True),
-    )(chunks)
+    )(share)
 
 
 def reduce_sums(sums, nf, ns):
@@ -198,8 +204,6 @@
     term, grad_rows = lax.optimization_barrier((term, grad_rows))
     col_blk = 3 * model_width // frame_n
     share = lax.psum_scatter(term, "space", scatter_dimension=0, tiled=True)
-    row_blk = share.shape[0]
-    share = share.reshape(row_blk, frame_n, col_blk).transpose(1, 0, 2)
     grad_hidden = lax.dot_general(
         grad_rows, w_full, (((1,), (1,)), ((), ())), preferred_element_type=jnp.float32
     )
@@ -210,8 +214,7 @@
     )
     local_sums = local_sums.reshape(-1, model_width)
     gm = reduce_sums(local_sums, frame_n, space_n)
-    gw = reduce_weight(share, frame_n).astype(jnp.float32)
-    grad_weight = gw.transpose(1, 0, 2).reshape(row_blk, 3 * model_width) * grad_scale_factor
+    grad_weight = reduce_weight(share, frame_n, grad_scale_factor)
     grad_modulation = gm.reshape(clip_count, 2, model_width) * grad_scale_factor
     grad_normed = grad_hidden * (1.0 + scale)
     grad_input = (

time: 279 us -> 275 us (0.986)
  local copies, waits for them, and re-layouts: 36.9 us -> 33.4 us
    reshape x2 -> x0, local copies, waits for them, and re-layouts: 3.76 us -> none  [per_device(): share = share.reshape(row_blk, frame_n, col_blk).transpose(1, 0, 2)]
    unnamed x35 -> x36, local copies, waits for them, and re-layouts: 4.6 us -> 6.82 us
  transfers between devices with their start and end apart: 4 -> 4, of which waited for: 3 -> 3; matrix products, arithmetic and copies ran while one was open for 11% -> 11% of each run, Pallas kernels for 12% -> 13%
where the time goes in v8:
time: 275 us; the launch traced here: 274 us
  waiting for transfers between devices  89.5 us (33%)
  Pallas kernels  79.5 us (29%)
  local copies, waits for them, and re-layouts  33.4 us (12%)
  matrix products  27.1 us (10%)
  starting transfers between devices  20 us (7%)
  between operations  14.4 us (5%)
  other arithmetic  10.4 us (4%)
    pallas_call x1, Pallas kernels, reduce_weight(): pl.pallas_call(functools.partial(weight_kernel, nf, scale), out_shape=jax...  44.7 us
    all_to_all x1, waiting for transfers between devices, per_device(): lax.all_to_all(both, 'frame', split_axis=2, concat_axis=1, tiled=True)  41.7 us
    unnamed x3, waiting for transfers between devices  35.9 us
    pallas_call x1, Pallas kernels, reduce_sums(): pl.pallas_call(functools.partial(sums_kernel, nf, ns), out_shape=jax.Shap...  34.8 us
    all_gather x1, waiting for transfers between devices, per_device(): w_full = lax.all_gather(w_qkv, 'space', axis=0, tiled=True)  12 us
    all_to_all x1, starting transfers between devices, per_device(): lax.all_to_all(both, 'frame', split_axis=2, concat_axis=1, tiled=True)  11.2 us
    all_to_all x1, starting transfers between devices, per_device(): lax.all_to_all(grad_input, 'frame', split_axis=1, concat_axis=2, tiled=True)  8.68 us
    dot_general x1, matrix products, per_device(): lax.dot_general(grad_rows, w_full, (((1,), (1,)), ((), ())), preferred_el...  6.93 us
  transfers between devices with their start and end apart: 4, of which 3 were waited for; matrix products, arithmetic and copies ran while one was open for 11% of the time, Pallas kernels for 13%

profile of v8, /device:TPU:6, one launch (start us, length us, event | category | flops | bytes accessed | tf_op | source)
XLA Modules:
  0.0 274.3 jit_solution(860559595795664385)
XLA Ops:
  9.6 1.7 copy.42
  11.3 2.6 pad_maximum_fusion.1
  13.9 11.2 %all-to-all-start = ((bf16[2,1,128,2,1152]{4,0,3,1,2:T(2,128)(2,1)}), bf16[2,1,128,2,1152]{4,0,3,1,2:T(2,128)(2,1)S(1)}, u32[]{:S(2)}, u32[]{:S(2)}) async-start(bf16[2,1,128,2,1152]{4,0,3,1,2:T(2,128)(2,1)} %pad_maximum_fusion.1), calls=%async_computation | async-start | bytes 2359296 | tf_op jit(solution)/shard_map/all_to_all | solution.py:177
  25.2 2.9 %gather_fusion = bf16[2,2,1152]{2,1,0:T(2,128)(2,1)S(1)} fusion(bf16[1000,2,1152]{2,1,0:T(2,128)(2,1)} %param.10, s32[1024]{0:T(1024)S(1)} %pad_clamp_fusion.1), kind=kCustom, calls=%fused_computation | custom fusion | bytes 18440 | tf_op jit(solution)/shard_map/gather | solution.py:186
  28.9 41.7 %all-to-all-done = bf16[2,1,128,2,1152]{4,0,3,1,2:T(2,128)(2,1)S(1)} async-done(((bf16[2,1,128,2,1152]{4,0,3,1,2:T(2,128)(2,1)}), bf16[2,1,128,2,1152]{4,0,3,1,2:T(2,128)(2,1)S(1)}, u32[]{:S(2)}, u32[]{:S(2)}) %all-to-all-start) | async-done | bytes 1179680 | tf_op jit(solution)/shard_map/all_to_all | solution.py:177
  73.1 2.9 %reshape.176 = f32[2,16,8,16,72]{4,3,2,1,0:T(8,128)S(1)} reshape(f32[2,16,8,1,1152]{4,2,1,0,3:T(8,128)} %slice_convert_fusion) | data formatting | bytes 2359296 | tf_op jit(solution)/shard_map/convert_element_type | solution.py:195
  78.8 12.0 %all-gather.2.cloned.1.call-done = bf16[1152,3456]{1,0:T(8,128)(2,1)} async-done(((bf16[72,3456]{1,0:T(8,128)(2,1)}), bf16[1152,3456]{1,0:T(8,128)(2,1)}) %all-gather.2.cloned.1.call-update) | async-done | bytes 7962640 | tf_op jit(solution)/shard_map/all_gather | solution.py:169
  90.7 6.0 %convolution_convert_fusion.1 = bf16[256,3456]{1,0:T(8,128)(2,1)S(1)} fusion(bf16[256,1152]{1,0:T(8,128)(2,1)} %fusion.6, bf16[1152,3456]{1,0:T(8,128)(2,1)} %all-gather.2.cloned.1.call-done), kind=kOutput, calls=%fused_computation.3 | convolution fusion | flops 2039316480 | bytes 10321920 | tf_op jit(solution)/shard_map/dot_general | solution.py:191
  96.7 6.5 %reshape.170 = bf16[2,16,8,3,16,72]{5,4,3,2,1,0:T(8,128)(2,1)} reshape(bf16[256,3456]{1,0:T(8,128)(2,1)S(1)} %convolution_convert_fusion.1) | data formatting | bytes 3538944 | tf_op jit(solution)/shard_map/reshape | solution.py:192
  103.2 2.5 fusion.18
  105.7 1.7 fusion.1
  109.0 1.8 multiply_reduce_fusion
  110.8 1.7 fusion.4
  112.5 1.9 fusion.3
  115.2 2.6 copy.50
  117.8 5.1 %reshape.171 = bf16[256,3456]{1,0:T(8,128)(2,1)S(1)} reshape(bf16[2,16,8,3,16,72]{5,4,3,2,1,0:T(8,128)(2,1)} %copy.50) | data formatting | bytes 3538944 | tf_op jit(solution)/shard_map/reshape | solution.py:199
  122.9 5.5 %convolution_convert_fusion = bf16[1152,3456]{1,0:T(8,128)(2,1)} fusion(bf16[256,1152]{1,0:T(8,128)(2,1)S(1)} %bitcast.101, bf16[256,3456]{1,0:T(8,128)(2,1)S(1)} %reshape.171), kind=kOutput, calls=%fused_computation.2 | convolution fusion | flops 2042413056 | bytes 10321920 | tf_op jit(solution)/shard_map/dot_general | solution.py:201
  129.1 6.9 %fusion.10 = (f32[256]{0:T(256)S(1)}, f32[256]{0:T(256)S(1)}, f32[256,1152]{1,0:T(8,128)}) fusion(f32[2,1152]{1,0:T(2,128)S(1)} %get-tuple-element.24, f32[256]{0:T(256)S(1)} %copy-done.13, f32[256]{0:T(256)S(1)} %copy-done.11, bf16[2,16,8,2,1152]{4,2,1,0,3:T(8,128)(2,1)S(1)} %bitcast.99, bf16[256,3456]{1,0:T(8,128)(2,1)S(1)} %reshape.171, ...), kind=kOutput, calls=%fused_computation.35 | convolution fusion | flops 2040495616 | bytes 11514880 | tf_op jit(solution)/shard_map/dot_general | solution.py:207
  136.3 1.9 bitcast_reduce_fusion
  139.0 8.7 %all-to-all-start.1 = ((bf16[2,16,8,1152]{3,2,0,1:T(8,128)(2,1)}), bf16[2,16,8,1152]{3,2,0,1:T(8,128)(2,1)S(1)}, u32[]{:S(2)}, u32[]{:S(2)}) async-start(bf16[2,16,8,1152]{3,2,0,1:T(8,128)(2,1)} %copy.51), calls=%async_computation.1 | async-start | bytes 1179648 | tf_op jit(solution)/shard_map/all_to_all | solution.py:226
  148.4 34.8 %shard_map.95 = f32[4,1152]{1,0:T(4,128)} custom-call(f32[4,1152]{1,0:T(4,128)} %reshape.174.sums_ref), custom_call_target="tpu_custom_call" | custom-call | tf_op jit(solution)/shard_map/pallas_call | solution.py:146
  185.4 35.2 %reduce-scatter.5.cloned.1.call-done.share_ref = bf16[72,3456]{1,0:T(8,128)(2,1)} async-done(((bf16[1152,3456]{1,0:T(8,128)(2,1)}), bf16[72,3456]{1,0:T(8,128)(2,1)}) %reduce-scatter.5.cloned.1.call-update) | async-done | bytes 497680
  220.5 44.7 %shard_map.94 = f32[72,3456]{1,0:T(8,128)} custom-call(bf16[72,3456]{1,0:T(8,128)(2,1)} %reduce-scatter.5.cloned.1.call-done.share_ref), custom_call_target="tpu_custom_call" | custom-call | tf_op jit(solution)/shard_map/pallas_call | solution.py:128
  265.2 2.2 copy.85
  (72 shorter events, 15.3 us)
Async XLA Ops:
  7.2 21.0 %copy-start = (f32[1000]{0:T(1024)S(1)}, f32[1000]{0:T(1024)}, u32[]{:S(2)}) copy-start(f32[1000]{0:T(1024)} %param.11) | copy-start | bytes 12004
  7.2 83.6 %all-gather.2.cloned.1.call-start = ((), (), s32[]{:S(2)}) async-start(), calls=%async_computation.3 | async-start | bytes 8460288 | tf_op jit(solution)/shard_map/all_gather | solution.py:169
  11.3 13.9 %copy-start.14 = (s32[2]{0:T(128)S(1)}, s32[2]{0:T(128)}, u32[]{:S(2)}) copy-start(s32[2]{0:T(128)} %param.12) | copy-start | bytes 28
  11.3 16.9 %copy-start.15 = (s32[2]{0:T(128)S(1)}, s32[2]{0:T(128)}, u32[]{:S(2)}) copy-start(s32[2]{0:T(128)} %param.13) | copy-start | bytes 28
  13.9 56.7 %all-to-all-start = ((bf16[2,1,128,2,1152]{4,0,3,1,2:T(2,128)(2,1)}), bf16[2,1,128,2,1152]{4,0,3,1,2:T(2,128)(2,1)S(1)}, u32[]{:S(2)}, u32[]{:S(2)}) async-start(bf16[2,1,128,2,1152]{4,0,3,1,2:T(2,128)(2,1)} %pad_maximum_fusion.1), calls=%async_computation | async-start | bytes 2359296 | tf_op jit(solution)/shard_map/all_to_all | solution.py:177
  25.1 195.4 %reduce-scatter.5.cloned.1.call-start = ((), (), s32[]{:S(2)}) async-start(), calls=%async_computation.4 | async-start | bytes 8460288
  28.8 47.1 %copy-start.8 = (f32[2,1152]{1,0:T(2,128)}, f32[2,1152]{1,0:T(2,128)S(1)}, u32[]{:S(2)}) copy-start(f32[2,1152]{1,0:T(2,128)S(1)} %get-tuple-element.23) | copy-start | bytes 27652
  70.9 0.6 copy-start.2
  71.0 5.0 %copy-start.10 = (f32[256]{0:T(256)}, f32[256]{0:T(256)S(1)}, u32[]{:S(2)}) copy-start(f32[256]{0:T(256)S(1)} %div.28) | copy-start | bytes 3076
  71.3 0.6 copy-start.5
  71.9 4.1 %copy-start.12 = (f32[256]{0:T(256)}, f32[256]{0:T(256)S(1)}, u32[]{:S(2)}) copy-start(f32[256]{0:T(256)S(1)} %rsqrt.13) | copy-start | bytes 3076
  76.0 2.5 copy-start.3
  76.0 2.4 copy-start.6
  77.1 1.3 copy-start.9
  105.7 1.7 copy-start.1
  128.4 0.7 copy-start.11
  128.4 0.7 copy-start.13
  129.1 7.1 %copy-start.4 = (f32[2,16,8]{2,1,0:T(8,128)S(1)}, f32[2,16,8]{2,1,0:T(8,128)}, u32[]{:S(2)}) copy-start(f32[2,16,8]{2,1,0:T(8,128)} %copy-done.2) | copy-start | bytes 3076
  129.1 7.1 %copy-start.7 = (f32[2,16,8]{2,1,0:T(8,128)S(1)}, f32[2,16,8]{2,1,0:T(8,128)}, u32[]{:S(2)}) copy-start(f32[2,16,8]{2,1,0:T(8,128)} %copy-done.5) | copy-start | bytes 3076
  139.0 45.5 %all-to-all-start.1 = ((bf16[2,16,8,1152]{3,2,0,1:T(8,128)(2,1)}), bf16[2,16,8,1152]{3,2,0,1:T(8,128)(2,1)S(1)}, u32[]{:S(2)}, u32[]{:S(2)}) async-start(bf16[2,16,8,1152]{3,2,0,1:T(8,128)(2,1)} %copy.51), calls=%async_computation.1 | async-start | bytes 1179648 | tf_op jit(solution)/shard_map/all_to_all | solution.py:226
Sparse Core Ops, SparseCore 0:
  9.9 80.8 all-gather.1
  128.6 91.9 reduce-scatter.4

commit v9 on v8

--- a/solution.py
+++ b/solution.py
@@ -71,12 +71,17 @@
 
 def weight_kernel(nf, scale, share_ref, gw_ref, chunks, recv1, redbuf, recv2, s1, r1, s2, r2):
     cols = chunks.shape[2]
-    for j in range(nf):
-        chunks[j] = share_ref[:, j * cols:(j + 1) * cols]
     me_f = lax.axis_index("frame")
     me_s = lax.axis_index("space")
     peer = lambda t: (t, me_s)
-    barrier_with([peer(lax.rem(me_f + k, nf)) for k in range(1, nf)])
+    barrier = pltpu.get_barrier_semaphore()
+    for k in range(1, nf):
+        pl.semaphore_signal(
+            barrier, inc=1, device_id=peer(lax.rem(me_f + k, nf)), device_id_type=MESH
+        )
+    for j in range(nf):
+        chunks[j] = share_ref[:, j * cols:(j + 1) * cols]
+    pl.semaphore_wait(barrier, nf - 1)
     first = lambda t: chunks.at[t]
     sends = exchange(first, recv1, peer, me_f, nf, s1, r1)
     recv1[me_f] = chunks[me_f]

time: 275 us -> 275 us (level)
  no operation moved by 1% of the time
where the time goes in v9:
time: 275 us; the launch traced here: 274 us
  waiting for transfers between devices  89.5 us (33%)
  Pallas kernels  79.3 us (29%)
  local copies, waits for them, and re-layouts  33.4 us (12%)
  matrix products  27.1 us (10%)
  starting transfers between devices  20 us (7%)
  between operations  14.4 us (5%)
  other arithmetic  10.4 us (4%)
    pallas_call x1, Pallas kernels, reduce_weight(): pl.pallas_call(functools.partial(weight_kernel, nf, scale), out_shape=jax...  44.5 us
    all_to_all x1, waiting for transfers between devices, per_device(): lax.all_to_all(both, 'frame', split_axis=2, concat_axis=1, tiled=True)  41.7 us
    unnamed x3, waiting for transfers between devices  35.9 us
    pallas_call x1, Pallas kernels, reduce_sums(): pl.pallas_call(functools.partial(sums_kernel, nf, ns), out_shape=jax.Shap...  34.8 us
    all_gather x1, waiting for transfers between devices, per_device(): w_full = lax.all_gather(w_qkv, 'space', axis=0, tiled=True)  12 us
    all_to_all x1, starting transfers between devices, per_device(): lax.all_to_all(both, 'frame', split_axis=2, concat_axis=1, tiled=True)  11.2 us
    all_to_all x1, starting transfers between devices, per_device(): lax.all_to_all(grad_input, 'frame', split_axis=1, concat_axis=2, tiled=True)  8.68 us
    dot_general x1, matrix products, per_device(): lax.dot_general(grad_rows, w_full, (((1,), (1,)), ((), ())), preferred_el...  6.93 us
  transfers between devices with their start and end apart: 4, of which 3 were waited for; matrix products, arithmetic and copies ran while one was open for 11% of the time, Pallas kernels for 13%

profile of v9, /device:TPU:6, one launch (start us, length us, event | category | flops | bytes accessed | tf_op | source)
XLA Modules:
  0.0 274.1 jit_solution(11693492992371020150)
XLA Ops:
  9.6 1.7 copy.42
  11.3 2.6 pad_maximum_fusion.1
  13.9 11.2 %all-to-all-start = ((bf16[2,1,128,2,1152]{4,0,3,1,2:T(2,128)(2,1)}), bf16[2,1,128,2,1152]{4,0,3,1,2:T(2,128)(2,1)S(1)}, u32[]{:S(2)}, u32[]{:S(2)}) async-start(bf16[2,1,128,2,1152]{4,0,3,1,2:T(2,128)(2,1)} %pad_maximum_fusion.1), calls=%async_computation | async-start | bytes 2359296 | tf_op jit(solution)/shard_map/all_to_all | solution.py:182
  25.2 2.9 %gather_fusion = bf16[2,2,1152]{2,1,0:T(2,128)(2,1)S(1)} fusion(bf16[1000,2,1152]{2,1,0:T(2,128)(2,1)} %param.10, s32[1024]{0:T(1024)S(1)} %pad_clamp_fusion.1), kind=kCustom, calls=%fused_computation | custom fusion | bytes 18440 | tf_op jit(solution)/shard_map/gather | solution.py:191
  28.9 41.7 %all-to-all-done = bf16[2,1,128,2,1152]{4,0,3,1,2:T(2,128)(2,1)S(1)} async-done(((bf16[2,1,128,2,1152]{4,0,3,1,2:T(2,128)(2,1)}), bf16[2,1,128,2,1152]{4,0,3,1,2:T(2,128)(2,1)S(1)}, u32[]{:S(2)}, u32[]{:S(2)}) %all-to-all-start) | async-done | bytes 1179680 | tf_op jit(solution)/shard_map/all_to_all | solution.py:182
  73.1 2.9 %reshape.176 = f32[2,16,8,16,72]{4,3,2,1,0:T(8,128)S(1)} reshape(f32[2,16,8,1,1152]{4,2,1,0,3:T(8,128)} %slice_convert_fusion) | data formatting | bytes 2359296 | tf_op jit(solution)/shard_map/convert_element_type | solution.py:200
  78.8 12.0 %all-gather.2.cloned.1.call-done = bf16[1152,3456]{1,0:T(8,128)(2,1)} async-done(((bf16[72,3456]{1,0:T(8,128)(2,1)}), bf16[1152,3456]{1,0:T(8,128)(2,1)}) %all-gather.2.cloned.1.call-update) | async-done | bytes 7962640 | tf_op jit(solution)/shard_map/all_gather | solution.py:174
  90.7 6.0 %convolution_convert_fusion.1 = bf16[256,3456]{1,0:T(8,128)(2,1)S(1)} fusion(bf16[256,1152]{1,0:T(8,128)(2,1)} %fusion.6, bf16[1152,3456]{1,0:T(8,128)(2,1)} %all-gather.2.cloned.1.call-done), kind=kOutput, calls=%fused_computation.3 | convolution fusion | flops 2039316480 | bytes 10321920 | tf_op jit(solution)/shard_map/dot_general | solution.py:196
  96.7 6.5 %reshape.170 = bf16[2,16,8,3,16,72]{5,4,3,2,1,0:T(8,128)(2,1)} reshape(bf16[256,3456]{1,0:T(8,128)(2,1)S(1)} %convolution_convert_fusion.1) | data formatting | bytes 3538944 | tf_op jit(solution)/shard_map/reshape | solution.py:197
  103.2 2.5 fusion.18
  105.7 1.7 fusion.1
  109.0 1.8 multiply_reduce_fusion
  110.8 1.7 fusion.4
  112.5 1.9 fusion.3
  115.2 2.6 copy.50
  117.8 5.1 %reshape.171 = bf16[256,3456]{1,0:T(8,128)(2,1)S(1)} reshape(bf16[2,16,8,3,16,72]{5,4,3,2,1,0:T(8,128)(2,1)} %copy.50) | data formatting | bytes 3538944 | tf_op jit(solution)/shard_map/reshape | solution.py:204
  122.9 5.5 %convolution_convert_fusion = bf16[1152,3456]{1,0:T(8,128)(2,1)} fusion(bf16[256,1152]{1,0:T(8,128)(2,1)S(1)} %bitcast.101, bf16[256,3456]{1,0:T(8,128)(2,1)S(1)} %reshape.171), kind=kOutput, calls=%fused_computation.2 | convolution fusion | flops 2042413056 | bytes 10321920 | tf_op jit(solution)/shard_map/dot_general | solution.py:206
  129.1 6.9 %fusion.10 = (f32[256]{0:T(256)S(1)}, f32[256]{0:T(256)S(1)}, f32[256,1152]{1,0:T(8,128)}) fusion(f32[2,1152]{1,0:T(2,128)S(1)} %get-tuple-element.24, f32[256]{0:T(256)S(1)} %copy-done.13, f32[256]{0:T(256)S(1)} %copy-done.11, bf16[2,16,8,2,1152]{4,2,1,0,3:T(8,128)(2,1)S(1)} %bitcast.99, bf16[256,3456]{1,0:T(8,128)(2,1)S(1)} %reshape.171, ...), kind=kOutput, calls=%fused_computation.35 | convolution fusion | flops 2040495616 | bytes 11514880 | tf_op jit(solution)/shard_map/dot_general | solution.py:212
  136.3 1.9 bitcast_reduce_fusion
  139.0 8.7 %all-to-all-start.1 = ((bf16[2,16,8,1152]{3,2,0,1:T(8,128)(2,1)}), bf16[2,16,8,1152]{3,2,0,1:T(8,128)(2,1)S(1)}, u32[]{:S(2)}, u32[]{:S(2)}) async-start(bf16[2,16,8,1152]{3,2,0,1:T(8,128)(2,1)} %copy.51), calls=%async_computation.1 | async-start | bytes 1179648 | tf_op jit(solution)/shard_map/all_to_all | solution.py:231
  148.4 34.8 %shard_map.95 = f32[4,1152]{1,0:T(4,128)} custom-call(f32[4,1152]{1,0:T(4,128)} %reshape.174.sums_ref), custom_call_target="tpu_custom_call" | custom-call | tf_op jit(solution)/shard_map/pallas_call | solution.py:151
  185.4 35.2 %reduce-scatter.5.cloned.1.call-done.share_ref = bf16[72,3456]{1,0:T(8,128)(2,1)} async-done(((bf16[1152,3456]{1,0:T(8,128)(2,1)}), bf16[72,3456]{1,0:T(8,128)(2,1)}) %reduce-scatter.5.cloned.1.call-update) | async-done | bytes 497680
  220.5 44.5 %shard_map.94 = f32[72,3456]{1,0:T(8,128)} custom-call(bf16[72,3456]{1,0:T(8,128)(2,1)} %reduce-scatter.5.cloned.1.call-done.share_ref), custom_call_target="tpu_custom_call" | custom-call | tf_op jit(solution)/shard_map/pallas_call | solution.py:133
  265.1 2.2 copy.85
  (72 shorter events, 15.3 us)
Async XLA Ops:
  7.2 21.0 %copy-start = (f32[1000]{0:T(1024)S(1)}, f32[1000]{0:T(1024)}, u32[]{:S(2)}) copy-start(f32[1000]{0:T(1024)} %param.11) | copy-start | bytes 12004
  7.2 83.6 %all-gather.2.cloned.1.call-start = ((), (), s32[]{:S(2)}) async-start(), calls=%async_computation.3 | async-start | bytes 8460288 | tf_op jit(solution)/shard_map/all_gather | solution.py:174
  11.3 13.9 %copy-start.14 = (s32[2]{0:T(128)S(1)}, s32[2]{0:T(128)}, u32[]{:S(2)}) copy-start(s32[2]{0:T(128)} %param.12) | copy-start | bytes 28
  11.3 16.9 %copy-start.15 = (s32[2]{0:T(128)S(1)}, s32[2]{0:T(128)}, u32[]{:S(2)}) copy-start(s32[2]{0:T(128)} %param.13) | copy-start | bytes 28
  13.9 56.7 %all-to-all-start = ((bf16[2,1,128,2,1152]{4,0,3,1,2:T(2,128)(2,1)}), bf16[2,1,128,2,1152]{4,0,3,1,2:T(2,128)(2,1)S(1)}, u32[]{:S(2)}, u32[]{:S(2)}) async-start(bf16[2,1,128,2,1152]{4,0,3,1,2:T(2,128)(2,1)} %pad_maximum_fusion.1), calls=%async_computation | async-start | bytes 2359296 | tf_op jit(solution)/shard_map/all_to_all | solution.py:182
  25.1 195.4 %reduce-scatter.5.cloned.1.call-start = ((), (), s32[]{:S(2)}) async-start(), calls=%async_computation.4 | async-start | bytes 8460288
  28.8 47.1 %copy-start.8 = (f32[2,1152]{1,0:T(2,128)}, f32[2,1152]{1,0:T(2,128)S(1)}, u32[]{:S(2)}) copy-start(f32[2,1152]{1,0:T(2,128)S(1)} %get-tuple-element.23) | copy-start | bytes 27652
  70.9 0.6 copy-start.2
  71.0 5.0 %copy-start.10 = (f32[256]{0:T(256)}, f32[256]{0:T(256)S(1)}, u32[]{:S(2)}) copy-start(f32[256]{0:T(256)S(1)} %div.28) | copy-start | bytes 3076
  71.3 0.6 copy-start.5
  71.9 4.1 %copy-start.12 = (f32[256]{0:T(256)}, f32[256]{0:T(256)S(1)}, u32[]{:S(2)}) copy-start(f32[256]{0:T(256)S(1)} %rsqrt.13) | copy-start | bytes 3076
  76.0 2.5 copy-start.3
  76.0 2.4 copy-start.6
  77.1 1.3 copy-start.9
  105.7 1.7 copy-start.1
  128.4 0.7 copy-start.11
  128.4 0.7 copy-start.13
  129.1 7.1 %copy-start.4 = (f32[2,16,8]{2,1,0:T(8,128)S(1)}, f32[2,16,8]{2,1,0:T(8,128)}, u32[]{:S(2)}) copy-start(f32[2,16,8]{2,1,0:T(8,128)} %copy-done.2) | copy-start | bytes 3076
  129.1 7.1 %copy-start.7 = (f32[2,16,8]{2,1,0:T(8,128)S(1)}, f32[2,16,8]{2,1,0:T(8,128)}, u32[]{:S(2)}) copy-start(f32[2,16,8]{2,1,0:T(8,128)} %copy-done.5) | copy-start | bytes 3076
  139.0 45.5 %all-to-all-start.1 = ((bf16[2,16,8,1152]{3,2,0,1:T(8,128)(2,1)}), bf16[2,16,8,1152]{3,2,0,1:T(8,128)(2,1)S(1)}, u32[]{:S(2)}, u32[]{:S(2)}) async-start(bf16[2,16,8,1152]{3,2,0,1:T(8,128)(2,1)} %copy.51), calls=%async_computation.1 | async-start | bytes 1179648 | tf_op jit(solution)/shard_map/all_to_all | solution.py:231
Sparse Core Ops, SparseCore 0:
  9.9 80.8 all-gather.1
  128.6 91.9 reduce-scatter.4

commit v10 on v9

--- a/solution.py
+++ b/solution.py
@@ -16,21 +16,21 @@
 def attend_back(queries, keys, values, upstream):
     factor = queries.shape[-1] ** (-0.5)
     f32 = jnp.float32
-    high = lax.Precision.HIGH
     scores = jnp.einsum("bfxhe,bgxhe->bxhfg", queries, keys, preferred_element_type=f32) * factor
     expd = jnp.exp(scores)
     probs = expd / jnp.sum(expd, axis=-1, keepdims=True)
     grad_probs = jnp.einsum("bfxhe,bgxhe->bxhfg", upstream, values, preferred_element_type=f32)
-    grad_values = jnp.einsum(
-        "bxhfg,bfxhe->bgxhe", probs, upstream.astype(f32), precision=high
-    )
+    def two_pass(spec, factor, operand):
+        hi = factor.astype(jnp.bfloat16)
+        lo = (factor - hi.astype(f32)).astype(jnp.bfloat16)
+        return jnp.einsum(spec, hi, operand, preferred_element_type=f32) + jnp.einsum(
+            spec, lo, operand, preferred_element_type=f32
+        )
+
+    grad_values = two_pass("bxhfg,bfxhe->bgxhe", probs, upstream)
     grad_scores = probs * (grad_probs - jnp.sum(probs * grad_probs, axis=-1, keepdims=True))
-    grad_queries = jnp.einsum(
-        "bxhfg,bgxhe->bfxhe", grad_scores, keys.astype(f32), precision=high
-    ) * factor
-    grad_keys = jnp.einsum(
-        "bxhfg,bfxhe->bgxhe", grad_scores, queries.astype(f32), precision=high
-    ) * factor
+    grad_queries = two_pass("bxhfg,bgxhe->bfxhe", grad_scores, keys) * factor
+    grad_keys = two_pass("bxhfg,bfxhe->bgxhe", grad_scores, queries) * factor
     return (
         grad_queries.astype(jnp.bfloat16),
         grad_keys.astype(jnp.bfloat16),

time: 275 us -> 281 us (1.022); the launches traced: 274 us -> 275 us
    unnamed x36 -> x34, local copies, waits for them, and re-layouts: 6.82 us -> 6.81 us
where the time goes in v10:
time: 281 us; the launch traced here: 275 us
  waiting for transfers between devices  89.6 us (32%)
  Pallas kernels  79 us (28%)
  local copies, waits for them, and re-layouts  33.6 us (12%)
  matrix products  27.4 us (10%)
  starting transfers between devices  19.9 us (7%)
  between operations  14.4 us (5%)
  other arithmetic  11.3 us (4%)
    pallas_call x1, Pallas kernels, reduce_weight(): pl.pallas_call(functools.partial(weight_kernel, nf, scale), out_shape=jax...  44.2 us
    all_to_all x1, waiting for transfers between devices, per_device(): lax.all_to_all(both, 'frame', split_axis=2, concat_axis=1, tiled=True)  41.7 us
    unnamed x3, waiting for transfers between devices  35.9 us
    pallas_call x1, Pallas kernels, reduce_sums(): pl.pallas_call(functools.partial(sums_kernel, nf, ns), out_shape=jax.Shap...  34.8 us
    all_gather x1, waiting for transfers between devices, per_device(): w_full = lax.all_gather(w_qkv, 'space', axis=0, tiled=True)  12 us
    all_to_all x1, starting transfers between devices, per_device(): lax.all_to_all(both, 'frame', split_axis=2, concat_axis=1, tiled=True)  11.2 us
    all_to_all x1, starting transfers between devices, per_device(): lax.all_to_all(grad_input, 'frame', split_axis=1, concat_axis=2, tiled=True)  8.66 us
    dot_general x1, matrix products, per_device(): lax.dot_general(grad_rows, w_full, (((1,), (1,)), ((), ())), preferred_el...  6.93 us
  transfers between devices with their start and end apart: 4, of which 3 were waited for; matrix products, arithmetic and copies ran while one was open for 11% of the time, Pallas kernels for 13%

profile of v10, /device:TPU:6, one launch (start us, length us, event | category | flops | bytes accessed | tf_op | source)
XLA Modules:
  0.0 275.3 jit_solution(1786677231844449174)
XLA Ops:
  7.9 1.7 copy.46
  9.6 1.7 copy.47
  11.3 2.6 pad_maximum_fusion.1
  13.9 11.2 %all-to-all-start = ((bf16[2,1,128,2,1152]{4,0,3,1,2:T(2,128)(2,1)}), bf16[2,1,128,2,1152]{4,0,3,1,2:T(2,128)(2,1)S(1)}, u32[]{:S(2)}, u32[]{:S(2)}) async-start(bf16[2,1,128,2,1152]{4,0,3,1,2:T(2,128)(2,1)} %pad_maximum_fusion.1), calls=%async_computation | async-start | bytes 2359296 | tf_op jit(solution)/shard_map/all_to_all | solution.py:182
  25.2 2.9 %gather_fusion = bf16[2,2,1152]{2,1,0:T(2,128)(2,1)S(1)} fusion(bf16[1000,2,1152]{2,1,0:T(2,128)(2,1)} %param.10, s32[1024]{0:T(1024)S(1)} %pad_clamp_fusion.1), kind=kCustom, calls=%fused_computation | custom fusion | bytes 18440 | tf_op jit(solution)/shard_map/gather | solution.py:191
  28.9 41.7 %all-to-all-done = bf16[2,1,128,2,1152]{4,0,3,1,2:T(2,128)(2,1)S(1)} async-done(((bf16[2,1,128,2,1152]{4,0,3,1,2:T(2,128)(2,1)}), bf16[2,1,128,2,1152]{4,0,3,1,2:T(2,128)(2,1)S(1)}, u32[]{:S(2)}, u32[]{:S(2)}) %all-to-all-start) | async-done | bytes 1179680 | tf_op jit(solution)/shard_map/all_to_all | solution.py:182
  73.1 2.9 %reshape.176 = f32[2,16,8,16,72]{4,3,2,1,0:T(8,128)S(1)} reshape(f32[2,16,8,1,1152]{4,2,1,0,3:T(8,128)} %slice_convert_fusion) | data formatting | bytes 2359296 | tf_op jit(solution)/shard_map/convert_element_type | solution.py:200
  77.1 1.3 multiply_convert_fusion.2
  78.8 12.0 %all-gather.2.cloned.1.call-done = bf16[1152,3456]{1,0:T(8,128)(2,1)} async-done(((bf16[72,3456]{1,0:T(8,128)(2,1)}), bf16[1152,3456]{1,0:T(8,128)(2,1)}) %all-gather.2.cloned.1.call-update) | async-done | bytes 7962640 | tf_op jit(solution)/shard_map/all_gather | solution.py:174
  90.7 6.0 %convolution_convert_fusion.1 = bf16[256,3456]{1,0:T(8,128)(2,1)S(1)} fusion(bf16[256,1152]{1,0:T(8,128)(2,1)} %fusion.6, bf16[1152,3456]{1,0:T(8,128)(2,1)} %all-gather.2.cloned.1.call-done), kind=kOutput, calls=%fused_computation.3 | convolution fusion | flops 2039316480 | bytes 10321920 | tf_op jit(solution)/shard_map/dot_general | solution.py:196
  96.7 6.5 %reshape.170 = bf16[2,16,8,3,16,72]{5,4,3,2,1,0:T(8,128)(2,1)} reshape(bf16[256,3456]{1,0:T(8,128)(2,1)S(1)} %convolution_convert_fusion.1) | data formatting | bytes 3538944 | tf_op jit(solution)/shard_map/reshape | solution.py:197
  103.2 2.5 fusion.25
  105.7 1.7 fusion.1
  107.4 1.8 multiply_reduce_fusion
  116.3 2.8 %copy.57 = bf16[2,16,8,3,16,72]{5,4,3,2,1,0:T(8,128)(2,1)} copy(bf16[2,16,8,3,16,72]{5,1,4,2,0,3:T(8,128)(2,1)S(1)} %pad_maximum_fusion) | data formatting | bytes 3538944 | tf_op jit(solution)/shard_map/stack | solution.py:204
  119.1 5.1 %reshape.171 = bf16[256,3456]{1,0:T(8,128)(2,1)S(1)} reshape(bf16[2,16,8,3,16,72]{5,4,3,2,1,0:T(8,128)(2,1)} %copy.57) | data formatting | bytes 3538944 | tf_op jit(solution)/shard_map/reshape | solution.py:204
  124.3 5.5 %convolution_convert_fusion = bf16[1152,3456]{1,0:T(8,128)(2,1)} fusion(bf16[256,1152]{1,0:T(8,128)(2,1)S(1)} %bitcast.107, bf16[256,3456]{1,0:T(8,128)(2,1)S(1)} %reshape.171), kind=kOutput, calls=%fused_computation.2 | convolution fusion | flops 2042413056 | bytes 10321920 | tf_op jit(solution)/shard_map/dot_general | solution.py:206
  130.5 6.9 %fusion.10 = (f32[256]{0:T(256)S(1)}, f32[256]{0:T(256)S(1)}, f32[256,1152]{1,0:T(8,128)}) fusion(f32[2,1152]{1,0:T(2,128)S(1)} %get-tuple-element.26, f32[256]{0:T(256)S(1)} %copy-done.12, f32[256]{0:T(256)S(1)} %div.28, bf16[2,16,8,2,1152]{4,2,1,0,3:T(8,128)(2,1)S(1)} %bitcast.105, bf16[256,3456]{1,0:T(8,128)(2,1)S(1)} %reshape.171, ...), kind=kOutput, calls=%fused_computation.37 | convolution fusion | flops 2040495616 | bytes 11514880 | tf_op jit(solution)/shard_map/dot_general | solution.py:212
  137.6 1.9 bitcast_reduce_fusion
  140.4 8.7 %all-to-all-start.1 = ((bf16[2,16,8,1152]{3,2,0,1:T(8,128)(2,1)}), bf16[2,16,8,1152]{3,2,0,1:T(8,128)(2,1)S(1)}, u32[]{:S(2)}, u32[]{:S(2)}) async-start(bf16[2,16,8,1152]{3,2,0,1:T(8,128)(2,1)} %copy.58), calls=%async_computation.1 | async-start | bytes 1179648 | tf_op jit(solution)/shard_map/all_to_all | solution.py:231
  149.7 34.8 %shard_map.95 = f32[4,1152]{1,0:T(4,128)} custom-call(f32[4,1152]{1,0:T(4,128)} %reshape.174.sums_ref), custom_call_target="tpu_custom_call" | custom-call | tf_op jit(solution)/shard_map/pallas_call | solution.py:151
  186.8 35.2 %reduce-scatter.5.cloned.1.call-done.share_ref = bf16[72,3456]{1,0:T(8,128)(2,1)} async-done(((bf16[1152,3456]{1,0:T(8,128)(2,1)}), bf16[72,3456]{1,0:T(8,128)(2,1)}) %reduce-scatter.5.cloned.1.call-update) | async-done | bytes 497680
  222.0 44.2 %shard_map.94 = f32[72,3456]{1,0:T(8,128)} custom-call(bf16[72,3456]{1,0:T(8,128)(2,1)} %reduce-scatter.5.cloned.1.call-done.share_ref), custom_call_target="tpu_custom_call" | custom-call | tf_op jit(solution)/shard_map/pallas_call | solution.py:133
  266.2 2.2 copy.97
  (74 shorter events, 17.1 us)
Async XLA Ops:
  7.2 21.0 %copy-start = (f32[1000]{0:T(1024)S(1)}, f32[1000]{0:T(1024)}, u32[]{:S(2)}) copy-start(f32[1000]{0:T(1024)} %param.11) | copy-start | bytes 12004
  7.2 83.6 %all-gather.2.cloned.1.call-start = ((), (), s32[]{:S(2)}) async-start(), calls=%async_computation.3 | async-start | bytes 8460288 | tf_op jit(solution)/shard_map/all_gather | solution.py:174
  11.3 13.9 %copy-start.13 = (s32[2]{0:T(128)S(1)}, s32[2]{0:T(128)}, u32[]{:S(2)}) copy-start(s32[2]{0:T(128)} %param.12) | copy-start | bytes 28
  11.3 16.9 %copy-start.14 = (s32[2]{0:T(128)S(1)}, s32[2]{0:T(128)}, u32[]{:S(2)}) copy-start(s32[2]{0:T(128)} %param.13) | copy-start | bytes 28
  13.9 56.7 %all-to-all-start = ((bf16[2,1,128,2,1152]{4,0,3,1,2:T(2,128)(2,1)}), bf16[2,1,128,2,1152]{4,0,3,1,2:T(2,128)(2,1)S(1)}, u32[]{:S(2)}, u32[]{:S(2)}) async-start(bf16[2,1,128,2,1152]{4,0,3,1,2:T(2,128)(2,1)} %pad_maximum_fusion.1), calls=%async_computation | async-start | bytes 2359296 | tf_op jit(solution)/shard_map/all_to_all | solution.py:182
  25.1 196.9 %reduce-scatter.5.cloned.1.call-start = ((), (), s32[]{:S(2)}) async-start(), calls=%async_computation.4 | async-start | bytes 8460288
  28.8 47.1 %copy-start.9 = (f32[2,1152]{1,0:T(2,128)}, f32[2,1152]{1,0:T(2,128)S(1)}, u32[]{:S(2)}) copy-start(f32[2,1152]{1,0:T(2,128)S(1)} %get-tuple-element.25) | copy-start | bytes 27652
  70.9 0.6 copy-start.3
  71.3 0.6 copy-start.6
  71.9 4.1 %copy-start.11 = (f32[256]{0:T(256)}, f32[256]{0:T(256)S(1)}, u32[]{:S(2)}) copy-start(f32[256]{0:T(256)S(1)} %rsqrt.13) | copy-start | bytes 3076
  76.0 2.5 copy-start.4
  76.0 2.4 copy-start.7
  77.1 1.3 copy-start.10
  105.7 1.7 copy-start.2
  129.8 0.7 copy-start.12
  130.5 7.1 %copy-start.5 = (f32[2,16,8]{2,1,0:T(8,128)S(1)}, f32[2,16,8]{2,1,0:T(8,128)}, u32[]{:S(2)}) copy-start(f32[2,16,8]{2,1,0:T(8,128)} %copy-done.3) | copy-start | bytes 3076
  130.5 7.1 %copy-start.8 = (f32[2,16,8]{2,1,0:T(8,128)S(1)}, f32[2,16,8]{2,1,0:T(8,128)}, u32[]{:S(2)}) copy-start(f32[2,16,8]{2,1,0:T(8,128)} %copy-done.6) | copy-start | bytes 3076
  140.4 45.6 %all-to-all-start.1 = ((bf16[2,16,8,1152]{3,2,0,1:T(8,128)(2,1)}), bf16[2,16,8,1152]{3,2,0,1:T(8,128)(2,1)S(1)}, u32[]{:S(2)}, u32[]{:S(2)}) async-start(bf16[2,16,8,1152]{3,2,0,1:T(8,128)(2,1)} %copy.58), calls=%async_computation.1 | async-start | bytes 1179648 | tf_op jit(solution)/shard_map/all_to_all | solution.py:231
  185.3 83.2 %copy-start.1 = (f32[1000]{0:T(1024)S(1)}, f32[1000]{0:T(1024)}, u32[]{:S(2)}) copy-start(f32[1000]{0:T(1024)} %param.11) | copy-start | bytes 12004
Sparse Core Ops, SparseCore 0:
  9.9 80.8 all-gather.1
  129.9 92.0 reduce-scatter.4

commit v11 on v9

--- a/solution.py
+++ b/solution.py
@@ -91,9 +91,9 @@
         acc = acc + recv1[j].astype(jnp.float32)
     acc = acc.astype(redbuf.dtype)
     redbuf[...] = acc
-    recv2[me_f] = acc
     second = lambda t: redbuf
     sends = exchange(second, recv2, peer, me_f, nf, s2, r2)
+    recv2[me_f] = acc
     wait_all(second, recv2, peer, me_f, nf, s2, r2, sends)
     for j in range(nf):
         gw_ref[:, j * cols:(j + 1) * cols] = recv2[j].astype(jnp.float32) * scale

time: 275 us -> 275 us (level)
  no operation moved by 1% of the time
where the time goes in v11:
time: 275 us; the launch traced here: 274 us
  waiting for transfers between devices  89.5 us (33%)
  Pallas kernels  79.3 us (29%)
  local copies, waits for them, and re-layouts  33.4 us (12%)
  matrix products  27.1 us (10%)
  starting transfers between devices  20 us (7%)
  between operations  14.4 us (5%)
  other arithmetic  10.4 us (4%)
    pallas_call x1, Pallas kernels, reduce_weight(): pl.pallas_call(functools.partial(weight_kernel, nf, scale), out_shape=jax...  44.5 us
    all_to_all x1, waiting for transfers between devices, per_device(): lax.all_to_all(both, 'frame', split_axis=2, concat_axis=1, tiled=True)  41.7 us
    unnamed x3, waiting for transfers between devices  35.9 us
    pallas_call x1, Pallas kernels, reduce_sums(): pl.pallas_call(functools.partial(sums_kernel, nf, ns), out_shape=jax.Shap...  34.8 us
    all_gather x1, waiting for transfers between devices, per_device(): w_full = lax.all_gather(w_qkv, 'space', axis=0, tiled=True)  12 us
    all_to_all x1, starting transfers between devices, per_device(): lax.all_to_all(both, 'frame', split_axis=2, concat_axis=1, tiled=True)  11.2 us
    all_to_all x1, starting transfers between devices, per_device(): lax.all_to_all(grad_input, 'frame', split_axis=1, concat_axis=2, tiled=True)  8.68 us
    dot_general x1, matrix products, per_device(): lax.dot_general(grad_rows, w_full, (((1,), (1,)), ((), ())), preferred_el...  6.93 us
  transfers between devices with their start and end apart: 4, of which 3 were waited for; matrix products, arithmetic and copies ran while one was open for 11% of the time, Pallas kernels for 13%

profile of v11, /device:TPU:6, one launch (start us, length us, event | category | flops | bytes accessed | tf_op | source)
XLA Modules:
  0.0 274.1 jit_solution(6586834791894129754)
XLA Ops:
  9.6 1.7 copy.42
  11.3 2.6 pad_maximum_fusion.1
  13.9 11.2 %all-to-all-start = ((bf16[2,1,128,2,1152]{4,0,3,1,2:T(2,128)(2,1)}), bf16[2,1,128,2,1152]{4,0,3,1,2:T(2,128)(2,1)S(1)}, u32[]{:S(2)}, u32[]{:S(2)}) async-start(bf16[2,1,128,2,1152]{4,0,3,1,2:T(2,128)(2,1)} %pad_maximum_fusion.1), calls=%async_computation | async-start | bytes 2359296 | tf_op jit(solution)/shard_map/all_to_all | solution.py:182
  25.2 2.9 %gather_fusion = bf16[2,2,1152]{2,1,0:T(2,128)(2,1)S(1)} fusion(bf16[1000,2,1152]{2,1,0:T(2,128)(2,1)} %param.10, s32[1024]{0:T(1024)S(1)} %pad_clamp_fusion.1), kind=kCustom, calls=%fused_computation | custom fusion | bytes 18440 | tf_op jit(solution)/shard_map/gather | solution.py:191
  28.9 41.7 %all-to-all-done = bf16[2,1,128,2,1152]{4,0,3,1,2:T(2,128)(2,1)S(1)} async-done(((bf16[2,1,128,2,1152]{4,0,3,1,2:T(2,128)(2,1)}), bf16[2,1,128,2,1152]{4,0,3,1,2:T(2,128)(2,1)S(1)}, u32[]{:S(2)}, u32[]{:S(2)}) %all-to-all-start) | async-done | bytes 1179680 | tf_op jit(solution)/shard_map/all_to_all | solution.py:182
  73.1 2.9 %reshape.176 = f32[2,16,8,16,72]{4,3,2,1,0:T(8,128)S(1)} reshape(f32[2,16,8,1,1152]{4,2,1,0,3:T(8,128)} %slice_convert_fusion) | data formatting | bytes 2359296 | tf_op jit(solution)/shard_map/convert_element_type | solution.py:200
  78.8 12.0 %all-gather.2.cloned.1.call-done = bf16[1152,3456]{1,0:T(8,128)(2,1)} async-done(((bf16[72,3456]{1,0:T(8,128)(2,1)}), bf16[1152,3456]{1,0:T(8,128)(2,1)}) %all-gather.2.cloned.1.call-update) | async-done | bytes 7962640 | tf_op jit(solution)/shard_map/all_gather | solution.py:174
  90.7 6.0 %convolution_convert_fusion.1 = bf16[256,3456]{1,0:T(8,128)(2,1)S(1)} fusion(bf16[256,1152]{1,0:T(8,128)(2,1)} %fusion.6, bf16[1152,3456]{1,0:T(8,128)(2,1)} %all-gather.2.cloned.1.call-done), kind=kOutput, calls=%fused_computation.3 | convolution fusion | flops 2039316480 | bytes 10321920 | tf_op jit(solution)/shard_map/dot_general | solution.py:196
  96.7 6.5 %reshape.170 = bf16[2,16,8,3,16,72]{5,4,3,2,1,0:T(8,128)(2,1)} reshape(bf16[256,3456]{1,0:T(8,128)(2,1)S(1)} %convolution_convert_fusion.1) | data formatting | bytes 3538944 | tf_op jit(solution)/shard_map/reshape | solution.py:197
  103.2 2.5 fusion.18
  105.7 1.7 fusion.1
  109.0 1.8 multiply_reduce_fusion
  110.8 1.7 fusion.4
  112.5 1.9 fusion.3
  115.2 2.6 copy.50
  117.8 5.1 %reshape.171 = bf16[256,3456]{1,0:T(8,128)(2,1)S(1)} reshape(bf16[2,16,8,3,16,72]{5,4,3,2,1,0:T(8,128)(2,1)} %copy.50) | data formatting | bytes 3538944 | tf_op jit(solution)/shard_map/reshape | solution.py:204
  122.9 5.5 %convolution_convert_fusion = bf16[1152,3456]{1,0:T(8,128)(2,1)} fusion(bf16[256,1152]{1,0:T(8,128)(2,1)S(1)} %bitcast.101, bf16[256,3456]{1,0:T(8,128)(2,1)S(1)} %reshape.171), kind=kOutput, calls=%fused_computation.2 | convolution fusion | flops 2042413056 | bytes 10321920 | tf_op jit(solution)/shard_map/dot_general | solution.py:206
  129.1 6.9 %fusion.10 = (f32[256]{0:T(256)S(1)}, f32[256]{0:T(256)S(1)}, f32[256,1152]{1,0:T(8,128)}) fusion(f32[2,1152]{1,0:T(2,128)S(1)} %get-tuple-element.24, f32[256]{0:T(256)S(1)} %copy-done.13, f32[256]{0:T(256)S(1)} %copy-done.11, bf16[2,16,8,2,1152]{4,2,1,0,3:T(8,128)(2,1)S(1)} %bitcast.99, bf16[256,3456]{1,0:T(8,128)(2,1)S(1)} %reshape.171, ...), kind=kOutput, calls=%fused_computation.35 | convolution fusion | flops 2040495616 | bytes 11514880 | tf_op jit(solution)/shard_map/dot_general | solution.py:212
  136.3 1.9 bitcast_reduce_fusion
  139.0 8.7 %all-to-all-start.1 = ((bf16[2,16,8,1152]{3,2,0,1:T(8,128)(2,1)}), bf16[2,16,8,1152]{3,2,0,1:T(8,128)(2,1)S(1)}, u32[]{:S(2)}, u32[]{:S(2)}) async-start(bf16[2,16,8,1152]{3,2,0,1:T(8,128)(2,1)} %copy.51), calls=%async_computation.1 | async-start | bytes 1179648 | tf_op jit(solution)/shard_map/all_to_all | solution.py:231
  148.4 34.8 %shard_map.95 = f32[4,1152]{1,0:T(4,128)} custom-call(f32[4,1152]{1,0:T(4,128)} %reshape.174.sums_ref), custom_call_target="tpu_custom_call" | custom-call | tf_op jit(solution)/shard_map/pallas_call | solution.py:151
  185.4 35.2 %reduce-scatter.5.cloned.1.call-done.share_ref = bf16[72,3456]{1,0:T(8,128)(2,1)} async-done(((bf16[1152,3456]{1,0:T(8,128)(2,1)}), bf16[72,3456]{1,0:T(8,128)(2,1)}) %reduce-scatter.5.cloned.1.call-update) | async-done | bytes 497680
  220.5 44.5 %shard_map.94 = f32[72,3456]{1,0:T(8,128)} custom-call(bf16[72,3456]{1,0:T(8,128)(2,1)} %reduce-scatter.5.cloned.1.call-done.share_ref), custom_call_target="tpu_custom_call" | custom-call | tf_op jit(solution)/shard_map/pallas_call | solution.py:133
  265.1 2.2 copy.85
  (72 shorter events, 15.3 us)
Async XLA Ops:
  7.2 21.0 %copy-start = (f32[1000]{0:T(1024)S(1)}, f32[1000]{0:T(1024)}, u32[]{:S(2)}) copy-start(f32[1000]{0:T(1024)} %param.11) | copy-start | bytes 12004
  7.2 83.6 %all-gather.2.cloned.1.call-start = ((), (), s32[]{:S(2)}) async-start(), calls=%async_computation.3 | async-start | bytes 8460288 | tf_op jit(solution)/shard_map/all_gather | solution.py:174
  11.3 13.9 %copy-start.14 = (s32[2]{0:T(128)S(1)}, s32[2]{0:T(128)}, u32[]{:S(2)}) copy-start(s32[2]{0:T(128)} %param.12) | copy-start | bytes 28
  11.3 16.9 %copy-start.15 = (s32[2]{0:T(128)S(1)}, s32[2]{0:T(128)}, u32[]{:S(2)}) copy-start(s32[2]{0:T(128)} %param.13) | copy-start | bytes 28
  13.9 56.7 %all-to-all-start = ((bf16[2,1,128,2,1152]{4,0,3,1,2:T(2,128)(2,1)}), bf16[2,1,128,2,1152]{4,0,3,1,2:T(2,128)(2,1)S(1)}, u32[]{:S(2)}, u32[]{:S(2)}) async-start(bf16[2,1,128,2,1152]{4,0,3,1,2:T(2,128)(2,1)} %pad_maximum_fusion.1), calls=%async_computation | async-start | bytes 2359296 | tf_op jit(solution)/shard_map/all_to_all | solution.py:182
  25.1 195.4 %reduce-scatter.5.cloned.1.call-start = ((), (), s32[]{:S(2)}) async-start(), calls=%async_computation.4 | async-start | bytes 8460288
  28.8 47.1 %copy-start.8 = (f32[2,1152]{1,0:T(2,128)}, f32[2,1152]{1,0:T(2,128)S(1)}, u32[]{:S(2)}) copy-start(f32[2,1152]{1,0:T(2,128)S(1)} %get-tuple-element.23) | copy-start | bytes 27652
  70.9 0.6 copy-start.2
  71.0 5.0 %copy-start.10 = (f32[256]{0:T(256)}, f32[256]{0:T(256)S(1)}, u32[]{:S(2)}) copy-start(f32[256]{0:T(256)S(1)} %div.28) | copy-start | bytes 3076
  71.3 0.6 copy-start.5
  71.9 4.1 %copy-start.12 = (f32[256]{0:T(256)}, f32[256]{0:T(256)S(1)}, u32[]{:S(2)}) copy-start(f32[256]{0:T(256)S(1)} %rsqrt.13) | copy-start | bytes 3076
  76.0 2.5 copy-start.3
  76.0 2.4 copy-start.6
  77.1 1.3 copy-start.9
  105.7 1.7 copy-start.1
  128.4 0.7 copy-start.11
  128.4 0.7 copy-start.13
  129.1 7.1 %copy-start.4 = (f32[2,16,8]{2,1,0:T(8,128)S(1)}, f32[2,16,8]{2,1,0:T(8,128)}, u32[]{:S(2)}) copy-start(f32[2,16,8]{2,1,0:T(8,128)} %copy-done.2) | copy-start | bytes 3076
  129.1 7.1 %copy-start.7 = (f32[2,16,8]{2,1,0:T(8,128)S(1)}, f32[2,16,8]{2,1,0:T(8,128)}, u32[]{:S(2)}) copy-start(f32[2,16,8]{2,1,0:T(8,128)} %copy-done.5) | copy-start | bytes 3076
  139.0 45.5 %all-to-all-start.1 = ((bf16[2,16,8,1152]{3,2,0,1:T(8,128)(2,1)}), bf16[2,16,8,1152]{3,2,0,1:T(8,128)(2,1)S(1)}, u32[]{:S(2)}, u32[]{:S(2)}) async-start(bf16[2,16,8,1152]{3,2,0,1:T(8,128)(2,1)} %copy.51), calls=%async_computation.1 | async-start | bytes 1179648 | tf_op jit(solution)/shard_map/all_to_all | solution.py:231
Sparse Core Ops, SparseCore 0:
  9.9 80.8 all-gather.1
  128.6 91.9 reduce-scatter.4
